TPU v7x, 32 devices: a whole 2x2x4 slice. The times are simulated.
32 devices in a mesh: fsdp: 8 (over y, x, core), tp: 4 (over z).
Axes of the slice: x: 2, y: 2, z: 4, core: 2. Of those that a mesh axis runs over, the one named last changes fastest.
Arguments:
- tokens: bfloat16 [16384, 1024], P(('fsdp', 'tp')), may hold values from -6 to 6
- lengths: int32 [8, 4], P('fsdp'), may hold values from 1 to 1024, 2048 in all within a row
- rates: float32 [8], P('tp'), may hold values from 0.00012207031 to 0.03
- w_query: bfloat16 [1024, 1024], P('fsdp', 'tp'), may hold values from -0.1875 to 0.1875
- w_key: bfloat16 [1024, 1024], P('fsdp', 'tp'), may hold values from -0.1875 to 0.1875
- w_value: bfloat16 [1024, 1024], P('fsdp', 'tp'), may hold values from -0.1875 to 0.1875
- w_update: bfloat16 [1024, 1024], P('fsdp', 'tp'), may hold values from -0.1875 to 0.1875
- w_output: bfloat16 [1024, 1024], P('tp', 'fsdp'), may hold values from -0.25 to 0.25
- w_gate: bfloat16 [1024, 2816], P('fsdp', 'tp'), may hold values from -0.1875 to 0.1875
- w_up: bfloat16 [1024, 2816], P('fsdp', 'tp'), may hold values from -0.1875 to 0.1875
- w_down: bfloat16 [2816, 1024], P('tp', 'fsdp'), may hold values from -0.109375 to 0.109375
- out_grad: bfloat16 [16384, 1024], P(('fsdp', 'tp')), may hold values from -6 to 6
Outputs:
- result: bfloat16 [16384, 1024], P(('fsdp', 'tp'))
- d_tokens: float32 [16384, 1024], P(('fsdp', 'tp'))
- g_query: float32 [1024, 1024], P('fsdp', 'tp')
- g_key: float32 [1024, 1024], P('fsdp', 'tp')
- g_value: float32 [1024, 1024], P('fsdp', 'tp')
- g_update: float32 [1024, 1024], P('fsdp', 'tp')
- g_output: float32 [1024, 1024], P('tp', 'fsdp')
- g_gate: float32 [1024, 2816], P('fsdp', 'tp')
- g_up: float32 [1024, 2816], P('fsdp', 'tp')
- g_down: float32 [2816, 1024], P('tp', 'fsdp')
Inputs may be any that keep to these rules, and one draw needn't show every extreme that they name: Each row of lengths sums to 2048; its largest entry is 1024 exactly; the last entry counts padded slots.
All inputs are finite; a program needn't handle non-finite values.
Results may differ from a plain program's by a relative error of at most 0.015.
Values may be sent and summed in bfloat16 or wider, within the bound.
A program may use at most 192 MiB of HBM per device.

v0:
```python
import jax
import jax.numpy as jnp
from jax import lax
from jax.sharding import PartitionSpec as P

HEAD_DIM = 128
SLOTS = 4


epsilon = 1e-06
head_floor = 1.0


def swish(values):
    return values * jax.nn.sigmoid(values)


def swish_slope(values):
    sigma = jax.nn.sigmoid(values)
    return sigma * (1.0 + values * (1.0 - sigma))


def rms_scale(values, offset=epsilon):
    return lax.rsqrt(jnp.mean(values * values, axis=-1, keepdims=True) + offset)


def norm_back(values, scale, grads):
    normed = values * scale
    return scale * (grads - normed * jnp.mean(grads * normed, axis=-1, keepdims=True))


def layout(lengths_row, group_rows):
    ends = jnp.cumsum(lengths_row, dtype=jnp.int32)
    places = jnp.arange(group_rows, dtype=jnp.int32)
    segment_ids = jnp.sum(
        (places[:, None] >= ends[None, :]).astype(jnp.int32), axis=1, dtype=jnp.int32
    )
    starts = ends - lengths_row
    slot_ids = jnp.arange(SLOTS, dtype=jnp.int32)
    zero_int = jnp.zeros((), jnp.int32)
    first_place = jnp.sum(
        jnp.where(segment_ids[:, None] == slot_ids[None, :], starts[None, :], zero_int),
        axis=1,
        dtype=jnp.int32,
    )
    positions = (places - first_place).astype(jnp.float32)
    live_rows = (segment_ids < SLOTS - 1).astype(jnp.float32)
    return (segment_ids, places, positions, live_rows)


def angles(positions, head_width):
    half_width = head_width // 2
    frequency = 10000.0 ** (-2.0 * jnp.arange(half_width, dtype=jnp.float32) / head_width)
    turned = positions[:, None] * frequency[None, :]
    return (jnp.cos(turned)[:, None, :], jnp.sin(turned)[:, None, :])


def rotate(values, cos_table, sin_table):
    half_width = values.shape[-1] // 2
    front_half = values[..., :half_width]
    back_half = values[..., half_width:]
    return jnp.concatenate(
        [
            front_half * cos_table - back_half * sin_table,
            front_half * sin_table + back_half * cos_table,
        ],
        axis=-1,
    )


def rotate_back(grads, cos_table, sin_table):
    half_width = grads.shape[-1] // 2
    front_half = grads[..., :half_width]
    back_half = grads[..., half_width:]
    return jnp.concatenate(
        [
            front_half * cos_table + back_half * sin_table,
            back_half * cos_table - front_half * sin_table,
        ],
        axis=-1,
    )


def decay_table(rates, seg_block, segment_ids, place_block, places):
    gaps = place_block[:, None] - places[None, :]
    allowed = (seg_block[:, None] == segment_ids[None, :]) & (gaps >= 0)
    spans = jnp.maximum(gaps, 0).astype(jnp.float32)
    factors = jnp.exp(-rates[:, None, None] * spans[None, :, :])
    return jnp.where(allowed[None, :, :], factors, jnp.zeros_like(factors))


def dot_trans(left, right):
    return lax.dot_general(
        left, right, (((1,), (1,)), ((), ())), preferred_element_type=jnp.float32
    )


def dot_inner(left, right):
    return lax.dot_general(
        left, right, (((0,), (0,)), ((), ())), preferred_element_type=jnp.float32
    )


def rows_times(left, right):
    return jnp.dot(left, right, preferred_element_type=jnp.float32)


def rows_times_trans(left, right):
    return dot_trans(left, right)


def body(
    tokens,
    lengths,
    rates,
    w_query,
    w_key,
    w_value,
    w_update,
    w_output,
    w_gate,
    w_up,
    w_down,
    out_grad,
):
    tp_count = lax.axis_size("tp")
    tp_index = lax.axis_index("tp")
    local_rows = tokens.shape[0]
    group_rows = local_rows * tp_count
    head_count = rates.shape[0]
    head_width = HEAD_DIM
    local_width = head_count * head_width
    unit_count = w_gate.shape[1]
    segment_ids, places, positions, live_rows = layout(lengths[0], group_rows)
    my_live = lax.dynamic_slice_in_dim(live_rows, tp_index * local_rows, local_rows, 0)
    cos_table, sin_table = angles(positions, head_width)
    shape_heads = (group_rows, head_count, head_width)
    block_rows = min(512, group_rows)
    block_count = group_rows // block_rows
    block_ids = jnp.arange(block_count, dtype=jnp.int32)
    tokens_f = tokens.astype(jnp.float32)
    scale1 = rms_scale(tokens_f)
    normed1 = lax.all_gather((tokens_f * scale1).astype(jnp.bfloat16), "tp", axis=0, tiled=True)
    query_full, key_full, value_full, update_full, output_full = (
        lax.all_gather(w_query, "fsdp", axis=0, tiled=True),
        lax.all_gather(w_key, "fsdp", axis=0, tiled=True),
        lax.all_gather(w_value, "fsdp", axis=0, tiled=True),
        lax.all_gather(w_update, "fsdp", axis=0, tiled=True),
        lax.all_gather(w_output, "fsdp", axis=1, tiled=True),
    )
    stacked = jnp.concatenate([query_full, key_full, value_full, update_full], axis=1)
    projected = jnp.dot(normed1, stacked, preferred_element_type=jnp.float32)
    query_pre = projected[:, :local_width]
    key_pre = projected[:, local_width : 2 * local_width]
    value_pre = projected[:, 2 * local_width : 3 * local_width]
    update_pre = projected[:, 3 * local_width :]
    query = rotate(swish(query_pre).reshape(shape_heads), cos_table, sin_table).astype(jnp.bfloat16)
    key_rows = rotate(swish(key_pre).reshape(shape_heads), cos_table, sin_table).astype(
        jnp.bfloat16
    )
    value_rows = value_pre.astype(jnp.bfloat16).reshape(shape_heads)
    update = swish(update_pre)

    def block_scores(first_row):
        query_block = lax.dynamic_slice_in_dim(query, first_row, block_rows, 0)
        seg_block = lax.dynamic_slice_in_dim(segment_ids, first_row, block_rows, 0)
        place_block = lax.dynamic_slice_in_dim(places, first_row, block_rows, 0)
        raw_scores = jnp.einsum(
            "thd,shd->hts", query_block, key_rows, preferred_element_type=jnp.float32
        )
        decay = decay_table(rates, seg_block, segment_ids, place_block, places)
        return (query_block, raw_scores, decay)

    def forward_block(block_index):
        query_block, raw_scores, decay = block_scores(block_index * block_rows)
        weights = (raw_scores * decay).astype(jnp.bfloat16)
        return jnp.einsum("hts,shd->thd", weights, value_rows, preferred_element_type=jnp.float32)

    attn = lax.map(forward_block, block_ids).reshape(shape_heads)
    scale_attn = rms_scale(attn, head_floor)
    normed_attn = (attn * scale_attn).reshape(group_rows, local_width)
    mixed = (normed_attn * update).astype(jnp.bfloat16)
    branch = lax.psum_scatter(rows_times(mixed, output_full), "tp", scatter_dimension=0, tiled=True)
    middle = tokens_f + branch
    scale2 = rms_scale(middle)
    normed2 = lax.all_gather((middle * scale2).astype(jnp.bfloat16), "tp", axis=0, tiled=True)
    gate_full, up_full, down_full = (
        lax.all_gather(w_gate, "fsdp", axis=0, tiled=True),
        lax.all_gather(w_up, "fsdp", axis=0, tiled=True),
        lax.all_gather(w_down, "fsdp", axis=1, tiled=True),
    )
    paired = jnp.concatenate([gate_full, up_full], axis=1)
    gate_up = jnp.dot(normed2, paired, preferred_element_type=jnp.float32)
    gate_rows = gate_up[:, :unit_count]
    up_rows = gate_up[:, unit_count:]
    hidden = (gate_rows * up_rows).astype(jnp.bfloat16)
    second = lax.psum_scatter(
        rows_times(hidden, down_full).astype(jnp.bfloat16), "tp", scatter_dimension=0, tiled=True
    ).astype(jnp.float32)
    result = (middle + second).astype(jnp.bfloat16)
    cotangent = out_grad.astype(jnp.float32) * my_live[:, None]
    cot_rows = lax.all_gather(cotangent.astype(jnp.bfloat16), "tp", axis=0, tiled=True)
    query_full, key_full, value_full, update_full, output_full, gate_full, up_full, down_full = (
        lax.all_gather(w_query, "fsdp", axis=0, tiled=True),
        lax.all_gather(w_key, "fsdp", axis=0, tiled=True),
        lax.all_gather(w_value, "fsdp", axis=0, tiled=True),
        lax.all_gather(w_update, "fsdp", axis=0, tiled=True),
        lax.all_gather(w_output, "fsdp", axis=1, tiled=True),
        lax.all_gather(w_gate, "fsdp", axis=0, tiled=True),
        lax.all_gather(w_up, "fsdp", axis=0, tiled=True),
        lax.all_gather(w_down, "fsdp", axis=1, tiled=True),
    )
    stacked = jnp.concatenate([query_full, key_full, value_full, update_full], axis=1)
    paired = jnp.concatenate([gate_full, up_full], axis=1)
    d_hidden = dot_trans(cot_rows, down_full)
    grad_down = dot_inner(hidden, cot_rows)
    d_paired = jnp.concatenate([d_hidden * up_rows, d_hidden * gate_rows], axis=1).astype(
        jnp.bfloat16
    )
    grad_paired = dot_inner(normed2, d_paired)
    grad_gate = grad_paired[:, :unit_count]
    grad_up = grad_paired[:, unit_count:]
    d_normed2 = lax.psum_scatter(
        rows_times_trans(d_paired, paired), "tp", scatter_dimension=0, tiled=True
    )
    d_middle = cotangent + norm_back(middle, scale2, d_normed2)
    mid_rows = lax.all_gather(d_middle.astype(jnp.bfloat16), "tp", axis=0, tiled=True)
    d_mixed = dot_trans(mid_rows, output_full)
    grad_output = dot_inner(mixed, mid_rows)
    d_normed_attn = (d_mixed * update).reshape(shape_heads)
    d_update = d_mixed * normed_attn
    d_update_pre = (d_update * swish_slope(update_pre)).astype(jnp.bfloat16)
    d_attn = norm_back(attn, scale_attn, d_normed_attn).astype(jnp.bfloat16)

    def backward_block(carry, block_index):
        d_key_sum, d_value_sum = carry
        first_row = block_index * block_rows
        query_block, raw_scores, decay = block_scores(first_row)
        grad_block = lax.dynamic_slice_in_dim(d_attn, first_row, block_rows, 0)
        weights = (raw_scores * decay).astype(jnp.bfloat16)
        d_weights = jnp.einsum(
            "thd,shd->hts", grad_block, value_rows, preferred_element_type=jnp.float32
        )
        d_value_sum = d_value_sum + jnp.einsum(
            "hts,thd->shd", weights, grad_block, preferred_element_type=jnp.float32
        )
        d_raw = (d_weights * decay).astype(jnp.bfloat16)
        d_query_block = jnp.einsum(
            "hts,shd->thd", d_raw, key_rows, preferred_element_type=jnp.float32
        )
        d_key_sum = d_key_sum + jnp.einsum(
            "hts,thd->shd", d_raw, query_block, preferred_element_type=jnp.float32
        )
        return ((d_key_sum, d_value_sum), d_query_block)

    zero_heads = jnp.zeros(shape_heads, jnp.float32)
    (d_key, d_value), d_query = lax.scan(backward_block, (zero_heads, zero_heads), block_ids)
    d_query = d_query.reshape(shape_heads)
    d_query_pre = (
        swish_slope(query_pre)
        * rotate_back(d_query, cos_table, sin_table).reshape(group_rows, local_width)
    ).astype(jnp.bfloat16)
    d_key_pre = (
        swish_slope(key_pre)
        * rotate_back(d_key, cos_table, sin_table).reshape(group_rows, local_width)
    ).astype(jnp.bfloat16)
    d_value_pre = d_value.reshape(group_rows, local_width).astype(jnp.bfloat16)
    d_projected = jnp.concatenate([d_query_pre, d_key_pre, d_value_pre, d_update_pre], axis=1)
    grad_stacked = dot_inner(normed1, d_projected)
    grad_query = grad_stacked[:, :local_width]
    grad_key = grad_stacked[:, local_width : 2 * local_width]
    grad_value = grad_stacked[:, 2 * local_width : 3 * local_width]
    grad_update = grad_stacked[:, 3 * local_width :]
    d_normed1 = lax.psum_scatter(
        rows_times_trans(d_projected, stacked).astype(jnp.bfloat16),
        "tp",
        scatter_dimension=0,
        tiled=True,
    ).astype(jnp.float32)
    d_tokens = d_middle + norm_back(tokens_f, scale1, d_normed1)
    grad_query, grad_key, grad_value, grad_update, grad_output, grad_gate, grad_up, grad_down = (
        lax.psum_scatter(grad_query, "fsdp", scatter_dimension=0, tiled=True),
        lax.psum_scatter(grad_key, "fsdp", scatter_dimension=0, tiled=True),
        lax.psum_scatter(grad_value, "fsdp", scatter_dimension=0, tiled=True),
        lax.psum_scatter(grad_update, "fsdp", scatter_dimension=0, tiled=True),
        lax.psum_scatter(grad_output, "fsdp", scatter_dimension=1, tiled=True),
        lax.psum_scatter(grad_gate, "fsdp", scatter_dimension=0, tiled=True),
        lax.psum_scatter(grad_up, "fsdp", scatter_dimension=0, tiled=True),
        lax.psum_scatter(grad_down, "fsdp", scatter_dimension=1, tiled=True),
    )
    return (
        result,
        d_tokens,
        grad_query,
        grad_key,
        grad_value,
        grad_update,
        grad_output,
        grad_gate,
        grad_up,
        grad_down,
    )


def solution(mesh):
    placed = (
        P(("fsdp", "tp"), None),
        P("fsdp", None),
        P("tp"),
        P("fsdp", "tp"),
        P("fsdp", "tp"),
        P("fsdp", "tp"),
        P("fsdp", "tp"),
        P("tp", "fsdp"),
        P("fsdp", "tp"),
        P("fsdp", "tp"),
        P("tp", "fsdp"),
        P(("fsdp", "tp"), None),
    )
    return jax.shard_map(
        body,
        mesh=mesh,
        in_specs=placed,
        out_specs=(
            P(("fsdp", "tp"), None),
            P(("fsdp", "tp"), None),
            P("fsdp", "tp"),
            P("fsdp", "tp"),
            P("fsdp", "tp"),
            P("fsdp", "tp"),
            P("tp", "fsdp"),
            P("fsdp", "tp"),
            P("fsdp", "tp"),
            P("tp", "fsdp"),
        ),
        check_vma=False,
    )
```

profile of v0, /device:TPU:0, one launch (start us, length us, event | category | flops | bytes accessed | tf_op | source)
XLA Modules:
  0.0 1331.6 jit_solution(12378258071507762168)
XLA Ops:
  12.6 11.3 all_gather.45
  23.9 9.8 all_gather.46
  33.8 8.9 all_gather.47
  42.6 9.8 all_gather.48
  52.4 10.1 all_gather.49
  68.2 27.6 %all-gather.8.cloned.1.call-done = bf16[2048,1024]{1,0:T(8,128)(2,1)} async-done(((bf16[512,1024]{1,0:T(8,128)(2,1)}), bf16[2048,1024]{1,0:T(8,128)(2,1)}) %all-gather.8.cloned.1.call-update) | async-done | bytes 4194320 | tf_op jit(solution)/shard_map/all_gather | solution.py:143
  131.4 45.3 %while.31 = (s32[]{:T(128)}, f32[4,512,2,128]{3,1,2,0:T(8,128)}, s32[4]{0:T(128)S(1)}, bf16[2048,2,128]{2,0,1:T(8,128)(2,1)S(1)}, bf16[2048,2,128]{2,0,1:T(8,128...) while((s32[]{:T(128)}, f32[4,512,2,128]{3,1,2,0:T(8,128)}, ...), condition=%wide.region_5.6_spmd.clone, body=%wide.region_4.5_spmd.clone.sunk | while | flops 1089470464 | bytes 13409475 | solution.py:179
  193.4 142.1 %reduce-scatter.13.cloned.1.call-done = f32[512,1024]{1,0:T(8,128)} async-done(((f32[2048,1024]{1,0:T(8,128)}), f32[512,1024]{1,0:T(8,128)}) %reduce-scatter.13.cloned.1.call-update) | async-done | bytes 2097168 | tf_op jit(solution)/shard_map/reduce_scatter | solution.py:183
  346.3 74.0 %all-gather.10.cloned.1.call-done = bf16[2048,1024]{1,0:T(8,128)(2,1)} async-done(((bf16[512,1024]{1,0:T(8,128)(2,1)}), bf16[2048,1024]{1,0:T(8,128)(2,1)}) %all-gather.10.cloned.1.call-update) | async-done | bytes 4194320 | tf_op jit(solution)/shard_map/all_gather | solution.py:186
  420.3 11.9 fusion.55
  432.2 13.6 %all-gather.16.cloned.1.call-done = bf16[704,1024]{1,0:T(8,128)(2,1)} async-done(((bf16[704,128]{1,0:T(8,128)(2,1)}), bf16[704,1024]{1,0:T(8,128)(2,1)}) %all-gather.16.cloned.1.call-update) | async-done | bytes 1441808 | tf_op jit(solution)/shard_map/all_gather | solution.py:190
  445.8 82.2 %all-gather.18.cloned.1.call-done = bf16[2048,1024]{1,0:T(8,128)(2,1)} async-done(((bf16[512,1024]{1,0:T(8,128)(2,1)}), bf16[2048,1024]{1,0:T(8,128)(2,1)}) %all-gather.18.cloned.1.call-update) | async-done | bytes 4194320 | tf_op jit(solution)/shard_map/all_gather | solution.py:202
  528.1 11.1 multiply_convert_fusion.4
  541.6 9.2 fusion.26
  550.8 7.7 convolution_convert_fusion
  558.8 135.2 %reduce-scatter.17.cloned.1.call-done = f32[512,1024]{1,0:T(8,128)} async-done(((f32[2048,1024]{1,0:T(8,128)}), f32[512,1024]{1,0:T(8,128)}) %reduce-scatter.17.cloned.1.call-update) | async-done | bytes 2097168 | tf_op jit(solution)/shard_map/reduce_scatter | solution.py:223
  696.7 76.8 %reduce-scatter.15.cloned.1.call-done = bf16[512,1024]{1,0:T(8,128)(2,1)} async-done(((bf16[2048,1024]{1,0:T(8,128)(2,1)}), bf16[512,1024]{1,0:T(8,128)(2,1)}) %reduce-scatter.15.cloned.1.call-update) | async-done | bytes 1048592 | tf_op jit(solution)/shard_map/reduce_scatter | solution.py:197
  778.9 10.8 fusion.25
  796.6 63.6 %all-gather.20.cloned.1.call-done = bf16[2048,1024]{1,0:T(8,128)(2,1)} async-done(((bf16[512,1024]{1,0:T(8,128)(2,1)}), bf16[2048,1024]{1,0:T(8,128)(2,1)}) %all-gather.20.cloned.1.call-update) | async-done | bytes 4194320 | tf_op jit(solution)/shard_map/all_gather | solution.py:227
  876.5 91.8 %while.32 = (s32[]{:T(128)}, f32[2048,2,128]{0,2,1:T(8,128)S(1)}, f32[2048,2,128]{0,2,1:T(8,128)}, f32[4,512,2,128]{3,1,0,2:T(8,128)}, s32[4]{0:T(128)S(1)}, /*i...) while((s32[]{:T(128)}, f32[2048,2,128]{0,2,1:T(8,128)S(1)}, ...), condition=%wide.region_14.15_spmd.clone.clone, body=%wide.region_13.14_spmd.clone.clone.sunk | while | flops 2710568960 | bytes 83403112 | solution.py:257
  914.4 7.7 fusion.123
  937.5 7.7 fusion.123
  960.6 7.7 fusion.123
  1001.1 7.8 fusion.57
  1015.0 7.4 fusion.40
  1030.5 45.9 %reduce-scatter.19.cloned.1.call-done = bf16[512,1024]{1,0:T(8,128)(2,1)} async-done(((bf16[2048,1024]{1,0:T(8,128)(2,1)}), bf16[512,1024]{1,0:T(8,128)(2,1)}) %reduce-scatter.19.cloned.1.call-update) | async-done | bytes 1048592 | tf_op jit(solution)/shard_map/reduce_scatter | solution.py:274
  1080.2 45.2 %reduce-scatter.35.cloned.1.call-done = f32[704,128]{1,0:T(8,128)} async-done(((f32[704,1024]{1,0:T(8,128)}), f32[704,128]{1,0:T(8,128)}) %reduce-scatter.35.cloned.1.call-update) | async-done | bytes 360464 | tf_op jit(solution)/shard_map/reduce_scatter | solution.py:289
  1125.4 39.7 %reduce-scatter.29.cloned.1.call-done = f32[256,128]{1,0:T(8,128)} async-done(((f32[256,1024]{1,0:T(8,128)}), f32[256,128]{1,0:T(8,128)}) %reduce-scatter.29.cloned.1.call-update) | async-done | bytes 131088 | tf_op jit(solution)/shard_map/reduce_scatter | solution.py:286
  1165.1 39.6 %reduce-scatter.21.cloned.1.call-done = f32[128,256]{1,0:T(8,128)} async-done(((f32[1024,256]{1,0:T(8,128)}), f32[128,256]{1,0:T(8,128)}) %reduce-scatter.21.cloned.1.call-update) | async-done | bytes 131088 | tf_op jit(solution)/shard_map/reduce_scatter | solution.py:282
  1204.6 39.7 %reduce-scatter.23.cloned.1.call-done = f32[128,256]{1,0:T(8,128)} async-done(((f32[1024,256]{1,0:T(8,128)}), f32[128,256]{1,0:T(8,128)}) %reduce-scatter.23.cloned.1.call-update) | async-done | bytes 131088 | tf_op jit(solution)/shard_map/reduce_scatter | solution.py:283
  1244.3 39.7 %reduce-scatter.25.cloned.1.call-done = f32[128,256]{1,0:T(8,128)} async-done(((f32[1024,256]{1,0:T(8,128)}), f32[128,256]{1,0:T(8,128)}) %reduce-scatter.25.cloned.1.call-update) | async-done | bytes 131088 | tf_op jit(solution)/shard_map/reduce_scatter | solution.py:284
  1284.0 39.7 %reduce-scatter.27.cloned.1.call-done = f32[128,256]{1,0:T(8,128)} async-done(((f32[1024,256]{1,0:T(8,128)}), f32[128,256]{1,0:T(8,128)}) %reduce-scatter.27.cloned.1.call-update) | async-done | bytes 131088 | tf_op jit(solution)/shard_map/reduce_scatter | solution.py:285
  (285 shorter events, 265.8 us)
Async XLA Ops:
  8.0 87.7 %all-gather.8.cloned.1.call-start = ((), (), s32[]{:S(2)}) async-start(), calls=%async_computation.12 | async-start | bytes 5242880 | tf_op jit(solution)/shard_map/all_gather | solution.py:143
  9.6 14.4 %copy-start.34 = (bf16[128,256]{1,0:T(8,128)(2,1)S(1)}, bf16[128,256]{1,0:T(8,128)(2,1)}, u32[]{:S(2)}) copy-start(bf16[128,256]{1,0:T(8,128)(2,1)} %param.20) | copy-start | bytes 196612
  9.6 24.2 %copy-start.38 = (f32[512]{0:T(512)}, f32[512]{0:T(512)S(1)}, u32[]{:S(2)}) copy-start(f32[512]{0:T(512)S(1)} %add_rsqrt_fusion.2) | copy-start | bytes 6148
  9.6 24.1 %copy-start.35 = (bf16[128,256]{1,0:T(8,128)(2,1)S(1)}, bf16[128,256]{1,0:T(8,128)(2,1)}, u32[]{:S(2)}) copy-start(bf16[128,256]{1,0:T(8,128)(2,1)} %param.21) | copy-start | bytes 196612
  9.6 33.0 %copy-start.36 = (bf16[128,256]{1,0:T(8,128)(2,1)S(1)}, bf16[128,256]{1,0:T(8,128)(2,1)}, u32[]{:S(2)}) copy-start(bf16[128,256]{1,0:T(8,128)(2,1)} %param.22) | copy-start | bytes 196612
  12.1 40.3 %copy-start.37 = (bf16[256,128]{1,0:T(8,128)(2,1)S(1)}, bf16[256,128]{1,0:T(8,128)(2,1)}, u32[]{:S(2)}) copy-start(bf16[256,128]{1,0:T(8,128)(2,1)} %param.23) | copy-start | bytes 196612
  12.1 323.4 %reduce-scatter.13.cloned.1.call-start = ((), (), s32[]{:S(2)}) async-start(), calls=%async_computation.13 | async-start | bytes 10485760 | tf_op jit(solution)/shard_map/reduce_scatter | solution.py:183
  68.2 57.5 %copy-start.11 = (f32[2048,64]{1,0:T(8,128)}, f32[2048,64]{1,0:T(8,128)S(1)}, u32[]{:S(2)}) copy-start(f32[2048,64]{1,0:T(8,128)S(1)} %get-tuple-element.554) | copy-start | bytes 1572868
  68.2 57.5 %copy-start.13 = (f32[2048,64]{1,0:T(8,128)}, f32[2048,64]{1,0:T(8,128)S(1)}, u32[]{:S(2)}) copy-start(f32[2048,64]{1,0:T(8,128)S(1)} %get-tuple-element.555) | copy-start | bytes 1572868
  192.2 143.3 %copy-start.2 = (bf16[512,1024]{1,0:T(8,128)(2,1)S(1)}, bf16[512,1024]{1,0:T(8,128)(2,1)}, u32[]{:S(2)}) copy-start(bf16[512,1024]{1,0:T(8,128)(2,1)} %param.16) | copy-start | bytes 3145732
  192.2 149.0 %all-gather.12.cloned.1.call-start = ((), (), s32[]{:S(2)}) async-start(), calls=%async_computation.15 | async-start | bytes 1622016 | tf_op jit(solution)/shard_map/all_gather | solution.py:188
  192.8 151.0 %all-gather.14.cloned.1.call-start = ((), (), s32[]{:S(2)}) async-start(), calls=%async_computation.16 | async-start | bytes 1622016 | tf_op jit(solution)/shard_map/all_gather | solution.py:189
  193.4 227.0 %all-gather.10.cloned.1.call-start = ((), (), s32[]{:S(2)}) async-start(), calls=%async_computation.14 | async-start | bytes 5242880 | tf_op jit(solution)/shard_map/all_gather | solution.py:186
  339.0 106.8 %all-gather.16.cloned.1.call-start = ((), (), s32[]{:S(2)}) async-start(), calls=%async_computation.17 | async-start | bytes 1622016 | tf_op jit(solution)/shard_map/all_gather | solution.py:190
  339.7 188.3 %all-gather.18.cloned.1.call-start = ((), (), s32[]{:S(2)}) async-start(), calls=%async_computation.19 | async-start | bytes 5242880 | tf_op jit(solution)/shard_map/all_gather | solution.py:202
  341.1 352.9 %reduce-scatter.17.cloned.1.call-start = ((), (), s32[]{:S(2)}) async-start(), calls=%async_computation.20 | async-start | bytes 10485760 | tf_op jit(solution)/shard_map/reduce_scatter | solution.py:223
  528.0 13.5 %copy-start.30 = (bf16[1024,1408]{0,1:T(8,128)(2,1)S(1)}, bf16[1024,1408]{0,1:T(8,128)(2,1)}, u32[]{:S(2)}) copy-start(bf16[1024,1408]{0,1:T(8,128)(2,1)} %constant_dynamic-update-slice_fusion.4) | copy-start | bytes 8650756
  550.8 222.7 %reduce-scatter.15.cloned.1.call-start = ((), (), s32[]{:S(2)}) async-start(), calls=%async_computation.18 | async-start | bytes 5242880 | tf_op jit(solution)/shard_map/reduce_scatter | solution.py:197
  558.6 301.6 %all-gather.20.cloned.1.call-start = ((), (), s32[]{:S(2)}) async-start(), calls=%async_computation.21 | async-start | bytes 5242880 | tf_op jit(solution)/shard_map/all_gather | solution.py:227
  778.8 247.9 %reduce-scatter.31.cloned.1.call-start = ((), (), s32[]{:S(2)}) async-start(), calls=%async_computation.28 | async-start | bytes 3538944 | tf_op jit(solution)/shard_map/reduce_scatter | solution.py:287
  793.3 235.3 %reduce-scatter.33.cloned.1.call-start = ((), (), s32[]{:S(2)}) async-start(), calls=%async_computation.29 | async-start | bytes 3538944 | tf_op jit(solution)/shard_map/reduce_scatter | solution.py:288
  796.5 279.9 %reduce-scatter.19.cloned.1.call-start = ((), (), s32[]{:S(2)}) async-start(), calls=%async_computation.22 | async-start | bytes 5242880 | tf_op jit(solution)/shard_map/reduce_scatter | solution.py:274
  1001.0 124.3 %reduce-scatter.35.cloned.1.call-start = ((), (), s32[]{:S(2)}) async-start(), calls=%async_computation.30 | async-start | bytes 3244032 | tf_op jit(solution)/shard_map/reduce_scatter | solution.py:289
  1008.9 6.0 copy-start.24
  1008.9 156.1 %reduce-scatter.29.cloned.1.call-start = ((), (), s32[]{:S(2)}) async-start(), calls=%async_computation.27 | async-start | bytes 1179648 | tf_op jit(solution)/shard_map/reduce_scatter | solution.py:286
  1014.6 190.0 %reduce-scatter.21.cloned.1.call-start = ((), (), s32[]{:S(2)}) async-start(), calls=%async_computation.23 | async-start | bytes 1179648 | tf_op jit(solution)/shard_map/reduce_scatter | solution.py:282
  1024.4 219.9 %reduce-scatter.23.cloned.1.call-start = ((), (), s32[]{:S(2)}) async-start(), calls=%async_computation.24 | async-start | bytes 1179648 | tf_op jit(solution)/shard_map/reduce_scatter | solution.py:283
  1024.5 51.9 %copy-start.3 = (bf16[512,1024]{1,0:T(8,128)(2,1)S(1)}, bf16[512,1024]{1,0:T(8,128)(2,1)}, u32[]{:S(2)}) copy-start(bf16[512,1024]{1,0:T(8,128)(2,1)} %param.16) | copy-start | bytes 3145732
  1024.5 51.9 %copy-start.39 = (f32[512]{0:T(512)S(1)}, f32[512]{0:T(512)}, u32[]{:S(2)}) copy-start(f32[512]{0:T(512)} %copy-done.38) | copy-start | bytes 6148
  1025.2 258.9 %reduce-scatter.25.cloned.1.call-start = ((), (), s32[]{:S(2)}) async-start(), calls=%async_computation.25 | async-start | bytes 1179648 | tf_op jit(solution)/shard_map/reduce_scatter | solution.py:284
  1025.9 297.8 %reduce-scatter.27.cloned.1.call-start = ((), (), s32[]{:S(2)}) async-start(), calls=%async_computation.26 | async-start | bytes 1179648 | tf_op jit(solution)/shard_map/reduce_scatter | solution.py:285
  1026.0 52.3 %copy-start.16 = (f32[512,1024]{1,0:T(8,128)S(1)}, f32[512,1024]{1,0:T(8,128)}, u32[]{:S(2)}) copy-start(f32[512,1024]{1,0:T(8,128)} %get-tuple-element.521) | copy-start | bytes 6291460
  (43 other events, 111.6 us)
Sparse Core Ops, SparseCore 0:
  12.2 83.4 all-gather.7
  192.3 143.1 reduce-scatter.12
  778.9 81.2 all-gather.19
Sparse Core Ops, SparseCore 1:
  194.6 23.6 all-gather.11
  219.9 25.0 all-gather.13
  339.1 81.2 all-gather.9
  422.2 23.5 all-gather.15
  447.4 80.6 all-gather.17
  550.9 143.1 reduce-scatter.16
  696.1 77.2 reduce-scatter.14
  793.4 46.4 reduce-scatter.30
  843.1 45.9 reduce-scatter.32
  1001.1 75.2 reduce-scatter.18
  1080.2 45.0 reduce-scatter.34
  1129.1 35.9 reduce-scatter.28
  1168.7 35.9 reduce-scatter.20
  1208.4 35.9 reduce-scatter.22
  1248.1 35.9 reduce-scatter.24
  1287.8 35.9 reduce-scatter.26
where the time goes:
time: 1340 us; the launch traced here: 1330 us
  waiting for transfers between devices  909 us (68%)
  matrix products  192 us (14%)
  other arithmetic  81.2 us (6%)
  local copies, waits for them, and re-layouts  76.3 us (6%)
  blocking collectives  49.9 us (4%)
  between operations  16.7 us (1%)
    reduce_scatter x1, waiting for transfers between devices, body(): lax.psum_scatter(rows_times(mixed, output_full), 'tp', scatter_dimension=...  142 us
    reduce_scatter x1, waiting for transfers between devices, body(): lax.psum_scatter(rows_times_trans(d_paired, paired), 'tp', scatter_dimens...  135 us
    all_gather x1, waiting for transfers between devices, body(): lax.all_gather(cotangent.astype(jnp.bfloat16), 'tp', axis=0, tiled=True)  82.2 us
    reduce_scatter x1, waiting for transfers between devices, body(): lax.psum_scatter(rows_times(hidden, down_full).astype(jnp.bfloat16), 'tp'...  76.8 us
    all_gather x1, waiting for transfers between devices, body(): lax.all_gather((middle * scale2).astype(jnp.bfloat16), 'tp', axis=0, tile...  74 us
    all_gather x1, waiting for transfers between devices, body(): lax.all_gather(d_middle.astype(jnp.bfloat16), 'tp', axis=0, tiled=True)  63.6 us
    reduce_scatter x1, waiting for transfers between devices, body(): lax.psum_scatter(rows_times_trans(d_projected, stacked).astype(jnp.bfloat...  45.9 us
    reduce_scatter x1, waiting for transfers between devices, body(): lax.psum_scatter(grad_down, 'fsdp', scatter_dimension=1, tiled=True)  45.2 us
  transfers between devices with their start and end apart: 19, of which 15 were waited for; matrix products, arithmetic and copies ran while one was open for 16% of the time, Pallas kernels for 0%

commit v1 on v0

v1 whole, which is shorter than its diff:
```python
import jax
import jax.numpy as jnp
from jax import lax
from jax.sharding import PartitionSpec as P

HEAD_DIM = 128
SLOTS = 4

epsilon = 1e-06
head_floor = 1.0
AXES = ("fsdp", "tp")


def swish(values):
    return values * jax.nn.sigmoid(values)


def swish_slope(values):
    sigma = jax.nn.sigmoid(values)
    return sigma * (1.0 + values * (1.0 - sigma))


def rms_scale(values, offset=epsilon):
    return lax.rsqrt(jnp.mean(values * values, axis=-1, keepdims=True) + offset)


def norm_back(values, scale, grads):
    normed = values * scale
    return scale * (grads - normed * jnp.mean(grads * normed, axis=-1, keepdims=True))


def segment_of(places, ends):
    return jnp.sum((places[..., None] >= ends).astype(jnp.int32), axis=-1, dtype=jnp.int32)


def rotate(values, cos_table, sin_table):
    half = values.shape[-1] // 2
    front, back = values[..., :half], values[..., half:]
    return jnp.concatenate(
        [front * cos_table - back * sin_table, front * sin_table + back * cos_table], axis=-1
    )


def rotate_back(values, cos_table, sin_table):
    return rotate(values, cos_table, -sin_table)


def mm(left, right):
    return jnp.dot(left, right, preferred_element_type=jnp.float32)


def mm_trans(left, right):
    return lax.dot_general(
        left, right, (((1,), (1,)), ((), ())), preferred_element_type=jnp.float32
    )


def mm_inner(left, right):
    return lax.dot_general(
        left, right, (((0,), (0,)), ((), ())), preferred_element_type=jnp.float32
    )


def heads_dot(spec, left, right):
    return jnp.einsum(spec, left, right, preferred_element_type=jnp.float32)


def gather_full(shard, row_axis, column_axis):
    part = lax.all_gather(shard, "tp", axis=0 if row_axis == "tp" else 1, tiled=True)
    return lax.all_gather(part, "fsdp", axis=0 if row_axis == "fsdp" else 1, tiled=True)


def scatter_grad(grad, row_axis, column_axis):
    part = grad.astype(jnp.bfloat16)
    part = lax.psum_scatter(
        part, "fsdp", scatter_dimension=0 if row_axis == "fsdp" else 1, tiled=True
    )
    part = lax.psum_scatter(part, "tp", scatter_dimension=0 if row_axis == "tp" else 1, tiled=True)
    return part.astype(jnp.float32)


def body(
    tokens,
    lengths,
    rates,
    w_query,
    w_key,
    w_value,
    w_update,
    w_output,
    w_gate,
    w_up,
    w_down,
    out_grad,
):
    tp_count = lax.axis_size("tp")
    tp_index = lax.axis_index("tp")
    rows, width = tokens.shape
    head_width = HEAD_DIM
    all_rates = lax.all_gather(rates, "tp", axis=0, tiled=True)
    heads = all_rates.shape[0]
    ends = jnp.cumsum(lengths[0], dtype=jnp.int32)
    first = tp_index * rows
    places = first + jnp.arange(rows, dtype=jnp.int32)
    segments = segment_of(places, ends)
    starts = ends - lengths[0]
    slots = jnp.arange(SLOTS, dtype=jnp.int32)
    positions = (
        places - jnp.sum(jnp.where(segments[:, None] == slots, starts, 0), axis=1)
    ).astype(jnp.float32)
    live = (segments < SLOTS - 1).astype(jnp.float32)
    frequency = 10000.0 ** (-2.0 * jnp.arange(head_width // 2, dtype=jnp.float32) / head_width)
    turned = positions[:, None] * frequency[None, :]
    cos_table, sin_table = jnp.cos(turned)[:, None, :], jnp.sin(turned)[:, None, :]

    gaps = places[:, None] - places[None, :]
    allowed = (segments[:, None] == segments[None, :]) & (gaps >= 0)
    spans = jnp.maximum(gaps, 0).astype(jnp.float32)
    decay = jnp.where(
        allowed[None], jnp.exp(-all_rates[:, None, None] * spans[None]), 0.0
    )
    blocks = jnp.arange(tp_count, dtype=jnp.int32)
    seg_before = segment_of(first - 1, ends)
    seg_after = segment_of(first + rows, ends)
    seg_last = segment_of(blocks * rows + rows - 1, ends)
    seg_first = segment_of(blocks * rows, ends)
    offsets = jnp.arange(rows, dtype=jnp.float32)

    def row_decay(distance, mask):
        return jnp.where(mask[:, None], jnp.exp(-distance[:, None] * all_rates[None]), 0.0)[
            :, :, None
        ]

    to_end = row_decay(rows - 1 - offsets, segments == segments[rows - 1])
    from_start = row_decay(offsets, segments == segments[0])
    into = row_decay(offsets + 1.0, segments == seg_before)
    out_of = row_decay(rows - offsets, segments == seg_after)

    def block_weights(mask, distance):
        distance = jnp.maximum(distance, 0).astype(jnp.float32)
        return jnp.where(mask[:, None], jnp.exp(-distance[:, None] * all_rates[None]), 0.0)

    before_weights = block_weights(
        (blocks < tp_index) & (seg_last == seg_before), (tp_index - blocks - 1) * rows
    )
    after_weights = block_weights(
        (blocks > tp_index) & (seg_first == seg_after), (blocks - tp_index - 1) * rows
    )

    tokens_f = tokens.astype(jnp.float32)
    scale1 = rms_scale(tokens_f)
    normed1 = (tokens_f * scale1).astype(jnp.bfloat16)
    query_full, key_full, value_full, update_full = (
        gather_full(w, "fsdp", "tp") for w in (w_query, w_key, w_value, w_update)
    )
    output_full = gather_full(w_output, "tp", "fsdp")
    gate_full, up_full = (gather_full(w, "fsdp", "tp") for w in (w_gate, w_up))
    down_full = gather_full(w_down, "tp", "fsdp")
    shape_heads = (rows, heads, head_width)
    query_pre = mm(normed1, query_full)
    key_pre = mm(normed1, key_full)
    value_rows = mm(normed1, value_full).astype(jnp.bfloat16).reshape(shape_heads)
    update_pre = mm(normed1, update_full)
    query = rotate(swish(query_pre).reshape(shape_heads), cos_table, sin_table).astype(jnp.bfloat16)
    key_rows = rotate(swish(key_pre).reshape(shape_heads), cos_table, sin_table).astype(
        jnp.bfloat16
    )
    update = swish(update_pre)
    key_state = heads_dot(
        "shc,shd->hcd", (key_rows * to_end).astype(jnp.bfloat16), value_rows
    ).astype(jnp.bfloat16)
    key_states = lax.all_gather(key_state, "tp", axis=0, tiled=False)
    state_in = jnp.sum(
        key_states.astype(jnp.float32) * before_weights[:, :, None, None], axis=0
    ).astype(jnp.bfloat16)
    weights = (heads_dot("thc,shc->hts", query, key_rows) * decay).astype(jnp.bfloat16)
    attn = heads_dot("hts,shd->thd", weights, value_rows) + into * heads_dot(
        "thc,hcd->thd", query, state_in
    )
    scale_attn = rms_scale(attn, head_floor)
    normed_attn = (attn * scale_attn).reshape(rows, width)
    mixed = (normed_attn * update).astype(jnp.bfloat16)
    middle = tokens_f + mm(mixed, output_full)
    scale2 = rms_scale(middle)
    normed2 = (middle * scale2).astype(jnp.bfloat16)
    gate_rows = mm(normed2, gate_full)
    up_rows = mm(normed2, up_full)
    hidden = (gate_rows * up_rows).astype(jnp.bfloat16)
    result = (middle + mm(hidden, down_full)).astype(jnp.bfloat16)

    cotangent = out_grad.astype(jnp.float32) * live[:, None]
    cot_rows = cotangent.astype(jnp.bfloat16)
    grad_down = mm_inner(hidden, cot_rows)
    d_hidden = mm_trans(cot_rows, down_full)
    d_gate = (d_hidden * up_rows).astype(jnp.bfloat16)
    d_up = (d_hidden * gate_rows).astype(jnp.bfloat16)
    grad_gate = mm_inner(normed2, d_gate)
    grad_up = mm_inner(normed2, d_up)
    d_normed2 = mm_trans(d_gate, gate_full) + mm_trans(d_up, up_full)
    d_middle = cotangent + norm_back(middle, scale2, d_normed2)
    mid_rows = d_middle.astype(jnp.bfloat16)
    d_mixed = mm_trans(mid_rows, output_full)
    grad_output = mm_inner(mixed, mid_rows)
    d_update_pre = (d_mixed * normed_attn * swish_slope(update_pre)).astype(jnp.bfloat16)
    d_attn = norm_back(attn, scale_attn, (d_mixed * update).reshape(shape_heads)).astype(
        jnp.bfloat16
    )
    query_state = heads_dot(
        "thc,thd->hcd", (query * from_start).astype(jnp.bfloat16), d_attn
    ).astype(jnp.bfloat16)
    query_states = lax.all_gather(query_state, "tp", axis=0, tiled=False)
    state_back = jnp.sum(
        query_states.astype(jnp.float32) * after_weights[:, :, None, None], axis=0
    ).astype(jnp.bfloat16)
    d_raw = (heads_dot("thd,shd->hts", d_attn, value_rows) * decay).astype(jnp.bfloat16)
    d_value = heads_dot("hts,thd->shd", weights, d_attn) + out_of * heads_dot(
        "shc,hcd->shd", key_rows, state_back
    )
    d_query = heads_dot("hts,shc->thc", d_raw, key_rows) + into * heads_dot(
        "thd,hcd->thc", d_attn, state_in
    )
    d_key = heads_dot("hts,thc->shc", d_raw, query) + out_of * heads_dot(
        "shd,hcd->shc", value_rows, state_back
    )
    d_query_pre = (
        swish_slope(query_pre) * rotate_back(d_query, cos_table, sin_table).reshape(rows, width)
    ).astype(jnp.bfloat16)
    d_key_pre = (
        swish_slope(key_pre) * rotate_back(d_key, cos_table, sin_table).reshape(rows, width)
    ).astype(jnp.bfloat16)
    d_value_pre = d_value.reshape(rows, width).astype(jnp.bfloat16)
    grads = [mm_inner(normed1, d) for d in (d_query_pre, d_key_pre, d_value_pre, d_update_pre)]
    d_normed1 = (
        mm_trans(d_query_pre, query_full)
        + mm_trans(d_key_pre, key_full)
        + mm_trans(d_value_pre, value_full)
        + mm_trans(d_update_pre, update_full)
    )
    d_tokens = d_middle + norm_back(tokens_f, scale1, d_normed1)
    return (
        result,
        d_tokens,
        *(scatter_grad(g, "fsdp", "tp") for g in grads),
        scatter_grad(grad_output, "tp", "fsdp"),
        scatter_grad(grad_gate, "fsdp", "tp"),
        scatter_grad(grad_up, "fsdp", "tp"),
        scatter_grad(grad_down, "tp", "fsdp"),
    )


def solution(mesh):
    rows = P(AXES, None)
    inner, outer = P("fsdp", "tp"), P("tp", "fsdp")
    return jax.shard_map(
        body,
        mesh=mesh,
        in_specs=(
            rows,
            P("fsdp", None),
            P("tp"),
            inner,
            inner,
            inner,
            inner,
            outer,
            inner,
            inner,
            outer,
            rows,
        ),
        out_specs=(rows, rows, inner, inner, inner, inner, outer, inner, inner, outer),
        check_vma=False,
    )
```

time: 1340 us -> 1020 us (0.76)
  waiting for transfers between devices: 909 us -> 608 us
  blocking collectives: 49.9 us -> 146 us
  matrix products: 192 us -> 148 us
  other arithmetic: 81.2 us -> 43.5 us
  local copies, waits for them, and re-layouts: 76.3 us -> 44.8 us
    reduce_scatter x12, waiting for transfers between devices: 644 us -> 389 us  [the longest x6 277 us: scatter_grad(): lax.psum_scatter(part, 'fsdp', scatter_dimension=0 if row_axis == 'fsdp'...]
    all_gather x7 -> x10, waiting for transfers between devices: 261 us -> 128 us  [the longest x8 122 us: gather_full(): lax.all_gather(part, 'fsdp', axis=0 if row_axis == 'fsdp' else 1, tiled=T...]
    unnamed x19 -> x30, waiting for transfers between devices: 3.97 us -> 90.9 us
    all_gather x5 -> x8, blocking collectives: 49.9 us -> 135 us  [gather_full(): lax.all_gather(shard, 'tp', axis=0 if row_axis == 'tp' else 1, tiled=True)]
    dot_general x32 -> x36, matrix products: 192 us -> 148 us  [the longest x8 43 us: mm(): return jnp.dot(left, right, preferred_element_type=jnp.float32)]
    convert_element_type x17 -> x11, other arithmetic: 30.4 us -> 13.7 us  [the longest x6 9.2 us: scatter_grad(): return part.astype(jnp.float32)]
    while x35 -> x0, local copies, waits for them, and re-layouts: 16.2 us -> none
    unnamed x92 -> x107, local copies, waits for them, and re-layouts: 33 us -> 41.3 us
  transfers between devices with their start and end apart: 19 -> 26, of which waited for: 15 -> 21; matrix products, arithmetic and copies ran while one was open for 16% -> 18% of each run, Pallas kernels for 0% -> 0%
where the time goes in v1:
time: 1020 us; the launch traced here: 1010 us
  waiting for transfers between devices  608 us (60%)
  matrix products  148 us (15%)
  blocking collectives  146 us (14%)
  local copies, waits for them, and re-layouts  44.8 us (4%)
  other arithmetic  43.5 us (4%)
  between operations  15.7 us (2%)
    reduce_scatter x6, waiting for transfers between devices, scatter_grad(): lax.psum_scatter(part, 'fsdp', scatter_dimension=0 if row_axis == 'fsdp'...  277 us
    all_gather x8, blocking collectives, gather_full(): lax.all_gather(shard, 'tp', axis=0 if row_axis == 'tp' else 1, tiled=True)  135 us
    all_gather x8, waiting for transfers between devices, gather_full(): lax.all_gather(part, 'fsdp', axis=0 if row_axis == 'fsdp' else 1, tiled=T...  122 us
    reduce_scatter x6, waiting for transfers between devices, scatter_grad(): lax.psum_scatter(part, 'tp', scatter_dimension=0 if row_axis == 'tp' else...  112 us
    unnamed x30, waiting for transfers between devices  90.9 us
    dot_general x8, matrix products, mm(): return jnp.dot(left, right, preferred_element_type=jnp.float32)  43 us
    unnamed x107, local copies, waits for them, and re-layouts  41.3 us
    dot_general x8, matrix products, mm_trans(): lax.dot_general(left, right, (((1,), (1,)), ((), ())), preferred_element_...  36.8 us
  transfers between devices with their start and end apart: 26, of which 21 were waited for; matrix products, arithmetic and copies ran while one was open for 18% of the time, Pallas kernels for 0%

profile of v1, /device:TPU:0, one launch (start us, length us, event | category | flops | bytes accessed | tf_op | source)
XLA Modules:
  0.0 1007.5 jit_solution(16899703952253602569)
XLA Ops:
  7.2 17.6 %all_gather.65 = bf16[128,1024]{1,0:T(8,128)(2,1)} all-gather(bf16[128,256]{1,0:T(8,128)(2,1)} %param.15), channel_id=1, replica_groups=mesh['fsdp'=8,'tp'=4] {'tp'}, dimensions={1}, use_global_device_ids=true | all-gather | bytes 327680 | tf_op jit(solution)/shard_map/all_gather | solution.py:69
  24.9 15.0 %all_gather.67 = bf16[128,1024]{1,0:T(8,128)(2,1)} all-gather(bf16[128,256]{1,0:T(8,128)(2,1)} %param.16), channel_id=1, replica_groups=mesh['fsdp'=8,'tp'=4] {'tp'}, dimensions={1}, use_global_device_ids=true | all-gather | bytes 327680 | tf_op jit(solution)/shard_map/all_gather | solution.py:69
  40.0 15.3 %all_gather.63 = bf16[128,1024]{1,0:T(8,128)(2,1)} all-gather(bf16[128,256]{1,0:T(8,128)(2,1)} %param.17), channel_id=1, replica_groups=mesh['fsdp'=8,'tp'=4] {'tp'}, dimensions={1}, use_global_device_ids=true | all-gather | bytes 327680 | tf_op jit(solution)/shard_map/all_gather | solution.py:69
  58.3 10.7 %all-reduce = f32[8]{0:T(128)S(1)} all-reduce(f32[8]{0:T(128)S(1)} %dynamic-update-slice), channel_id=1, replica_groups=mesh['fsdp'=8,'tp'=4] {'tp'}, use_global_device_ids=true, to_apply=%add | all-reduce | flops 8 | bytes 64
  92.3 19.9 %all-gather.13.cloned.1.call-done = bf16[1024,1024]{1,0:T(8,128)(2,1)} async-done(((bf16[128,1024]{1,0:T(8,128)(2,1)}), bf16[1024,1024]{1,0:T(8,128)(2,1)}) %all-gather.13.cloned.1.call-update) | async-done | bytes 2097168 | tf_op jit(solution)/shard_map/all_gather | solution.py:70
  117.6 15.9 %all_gather.72 = bf16[128,1024]{1,0:T(8,128)(2,1)} all-gather(bf16[128,256]{1,0:T(8,128)(2,1)S(1)} %copy-done.40), channel_id=1, replica_groups=mesh['fsdp'=8,'tp'=4] {'tp'}, dimensions={1}, use_global_device_ids=true | all-gather | bytes 327680 | tf_op jit(solution)/shard_map/all_gather | solution.py:69
  133.6 17.5 %all_gather.74 = bf16[1024,128]{1,0:T(8,128)(2,1)} all-gather(bf16[256,128]{1,0:T(8,128)(2,1)S(1)} %copy-done.41), channel_id=1, replica_groups=mesh['fsdp'=8,'tp'=4] {'tp'}, dimensions={0}, use_global_device_ids=true | all-gather | bytes 327680 | tf_op jit(solution)/shard_map/all_gather | solution.py:69
  151.2 17.9 %all_gather.78 = bf16[128,2816]{0,1:T(8,128)(2,1)} all-gather(bf16[128,704]{0,1:T(8,128)(2,1)S(1)} %copy-done.39), channel_id=1, replica_groups=mesh['fsdp'=8,'tp'=4] {'tp'}, dimensions={1}, use_global_device_ids=true | all-gather | bytes 901120 | tf_op jit(solution)/shard_map/all_gather | solution.py:69
  169.2 19.2 %all_gather.76 = bf16[128,2816]{0,1:T(8,128)(2,1)} all-gather(bf16[128,704]{0,1:T(8,128)(2,1)} %param.20), channel_id=1, replica_groups=mesh['fsdp'=8,'tp'=4] {'tp'}, dimensions={1}, use_global_device_ids=true | all-gather | bytes 901120 | tf_op jit(solution)/shard_map/all_gather | solution.py:69
  188.4 16.7 %all_gather.80 = bf16[2816,128]{1,0:T(8,128)(2,1)} all-gather(bf16[704,128]{1,0:T(8,128)(2,1)} %param.22), channel_id=1, replica_groups=mesh['fsdp'=8,'tp'=4] {'tp'}, dimensions={0}, use_global_device_ids=true | all-gather | bytes 901120 | tf_op jit(solution)/shard_map/all_gather | solution.py:69
  230.3 26.0 %all-gather.25.cloned.1.call-done = bf16[1024,2816]{0,1:T(8,128)(2,1)} async-done(((bf16[128,2816]{0,1:T(8,128)(2,1)}), bf16[1024,2816]{0,1:T(8,128)(2,1)}) %all-gather.25.cloned.1.call-update) | async-done | bytes 5767184 | tf_op jit(solution)/shard_map/all_gather | solution.py:70
  256.3 8.7 fusion.70
  265.0 37.5 %all-gather.23.cloned.1.call-done = bf16[1024,2816]{0,1:T(8,128)(2,1)} async-done(((bf16[128,2816]{0,1:T(8,128)(2,1)}), bf16[1024,2816]{0,1:T(8,128)(2,1)}) %all-gather.23.cloned.1.call-update) | async-done | bytes 5767184 | tf_op jit(solution)/shard_map/all_gather | solution.py:70
  302.5 8.6 fusion.69
  311.1 37.6 %all-gather.27.cloned.1.call-done = bf16[2816,1024]{1,0:T(8,128)(2,1)} async-done(((bf16[2816,128]{1,0:T(8,128)(2,1)}), bf16[2816,1024]{1,0:T(8,128)(2,1)}) %all-gather.27.cloned.1.call-update) | async-done | bytes 5767184 | tf_op jit(solution)/shard_map/all_gather | solution.py:70
  348.7 11.2 %multiply_convert_fusion.2 = (bf16[512,2816]{1,0:T(8,128)(2,1)S(1)}, bf16[512,2816]{1,0:T(8,128)(2,1)}, bf16[512,2816]{1,0:T(8,128)(2,1)S(1)}) fusion(f32[512,2816]{1,0:T(8,128)} %fusion.69, f32[512,2816]{1,0:T(8,128)} %fusion.70, bf16[2816,1024]{1,0:T(8,128)(2,1)} %all-gather.27.cloned.1.call-done, bf16[512,1024]{1,0:T(8,128)(2,1)} %param.23, ...), kind=kOutput, calls=%fused_computation.3 | convolution fusion | flops 2963013632 | bytes 27002880 | tf_op jit(solution)/shard_map/dot_general | solution.py:53
  470.1 8.4 copy.166
  480.5 21.4 %reduce-scatter.37.cloned.1.call-done = bf16[128,1024]{1,0:T(8,128)(2,1)} async-done(((bf16[1024,1024]{1,0:T(8,128)(2,1)}), bf16[128,1024]{1,0:T(8,128)(2,1)}) %reduce-scatter.37.cloned.1.call-update) | async-done | bytes 262160 | tf_op jit(solution)/shard_map/reduce_scatter | solution.py:75
  502.0 44.3 %reduce-scatter.33.cloned.1.call-done = bf16[128,1024]{1,0:T(8,128)(2,1)} async-done(((bf16[1024,1024]{1,0:T(8,128)(2,1)}), bf16[128,1024]{1,0:T(8,128)(2,1)}) %reduce-scatter.33.cloned.1.call-update) | async-done | bytes 262160 | tf_op jit(solution)/shard_map/reduce_scatter | solution.py:75
  546.4 44.2 %reduce-scatter.29.cloned.1.call-done = bf16[128,1024]{1,0:T(8,128)(2,1)} async-done(((bf16[1024,1024]{1,0:T(8,128)(2,1)}), bf16[128,1024]{1,0:T(8,128)(2,1)}) %reduce-scatter.29.cloned.1.call-update) | async-done | bytes 262160 | tf_op jit(solution)/shard_map/reduce_scatter | solution.py:75
  590.7 44.8 %reduce-scatter.25.cloned.1.call-done = bf16[128,1024]{1,0:T(8,128)(2,1)} async-done(((bf16[1024,1024]{1,0:T(8,128)(2,1)}), bf16[128,1024]{1,0:T(8,128)(2,1)}) %reduce-scatter.25.cloned.1.call-update) | async-done | bytes 262160 | tf_op jit(solution)/shard_map/reduce_scatter | solution.py:75
  635.5 62.3 %reduce-scatter.45.cloned.1.call-done = bf16[128,2816]{1,0:T(8,128)(2,1)} async-done(((bf16[1024,2816]{1,0:T(8,128)(2,1)}), bf16[128,2816]{1,0:T(8,128)(2,1)}) %reduce-scatter.45.cloned.1.call-update) | async-done | bytes 720912 | tf_op jit(solution)/shard_map/reduce_scatter | solution.py:75
  700.1 60.0 %reduce-scatter.43.cloned.1.call-done = bf16[128,2816]{1,0:T(8,128)(2,1)} async-done(((bf16[1024,2816]{1,0:T(8,128)(2,1)}), bf16[128,2816]{1,0:T(8,128)(2,1)}) %reduce-scatter.43.cloned.1.call-update) | async-done | bytes 720912 | tf_op jit(solution)/shard_map/reduce_scatter | solution.py:75
  776.3 46.2 %reduce-scatter.55.cloned.1.call-done = bf16[128,2816]{1,0:T(8,128)(2,1)} async-done(((bf16[1024,2816]{1,0:T(8,128)(2,1)}), bf16[128,2816]{1,0:T(8,128)(2,1)}) %reduce-scatter.55.cloned.1.call-update) | async-done | bytes 720912
  831.8 13.5 %reduce-scatter.41.cloned.1.call-done = bf16[256,128]{1,0:T(8,128)(2,1)} async-done(((bf16[1024,128]{1,0:T(8,128)(2,1)}), bf16[256,128]{1,0:T(8,128)(2,1)}) %reduce-scatter.41.cloned.1.call-update) | async-done | bytes 65552 | tf_op jit(solution)/shard_map/reduce_scatter | solution.py:78
  846.8 18.9 %reduce-scatter.39.cloned.1.call-done = bf16[128,256]{1,0:T(8,128)(2,1)} async-done(((bf16[128,1024]{1,0:T(8,128)(2,1)}), bf16[128,256]{1,0:T(8,128)(2,1)}) %reduce-scatter.39.cloned.1.call-update) | async-done | bytes 65552 | tf_op jit(solution)/shard_map/reduce_scatter | solution.py:78
  867.2 19.0 %reduce-scatter.35.cloned.1.call-done = bf16[128,256]{1,0:T(8,128)(2,1)} async-done(((bf16[128,1024]{1,0:T(8,128)(2,1)}), bf16[128,256]{1,0:T(8,128)(2,1)}) %reduce-scatter.35.cloned.1.call-update) | async-done | bytes 65552 | tf_op jit(solution)/shard_map/reduce_scatter | solution.py:78
  887.7 19.0 %reduce-scatter.31.cloned.1.call-done = bf16[128,256]{1,0:T(8,128)(2,1)} async-done(((bf16[128,1024]{1,0:T(8,128)(2,1)}), bf16[128,256]{1,0:T(8,128)(2,1)}) %reduce-scatter.31.cloned.1.call-update) | async-done | bytes 65552 | tf_op jit(solution)/shard_map/reduce_scatter | solution.py:78
  908.2 19.0 %reduce-scatter.27.cloned.1.call-done = bf16[128,256]{1,0:T(8,128)(2,1)} async-done(((bf16[128,1024]{1,0:T(8,128)(2,1)}), bf16[128,256]{1,0:T(8,128)(2,1)}) %reduce-scatter.27.cloned.1.call-update) | async-done | bytes 65552 | tf_op jit(solution)/shard_map/reduce_scatter | solution.py:78
  928.7 21.9 %reduce-scatter.53.cloned.1.call-done = bf16[704,128]{1,0:T(8,128)(2,1)} async-done(((bf16[2816,128]{1,0:T(8,128)(2,1)}), bf16[704,128]{1,0:T(8,128)(2,1)}) %reduce-scatter.53.cloned.1.call-update) | async-done | bytes 180240
  952.5 22.4 %reduce-scatter.51.cloned.1.call-done = bf16[704,128]{1,0:T(8,128)(2,1)} async-done(((bf16[2816,128]{1,0:T(8,128)(2,1)}), bf16[704,128]{1,0:T(8,128)(2,1)}) %reduce-scatter.51.cloned.1.call-update) | async-done | bytes 180240
  976.9 22.3 %reduce-scatter.47.cloned.1.call-done = bf16[704,128]{1,0:T(8,128)(2,1)} async-done(((bf16[2816,128]{1,0:T(8,128)(2,1)}), bf16[704,128]{1,0:T(8,128)(2,1)}) %reduce-scatter.47.cloned.1.call-update) | async-done | bytes 180240 | tf_op jit(solution)/shard_map/reduce_scatter | solution.py:78
  (250 shorter events, 209.1 us)
Async XLA Ops:
  7.2 64.6 %copy-start.1 = (bf16[512,1024]{1,0:T(8,128)(2,1)S(1)}, bf16[512,1024]{1,0:T(8,128)(2,1)}, u32[]{:S(2)}) copy-start(bf16[512,1024]{1,0:T(8,128)(2,1)} %param.12) | copy-start | bytes 3145732
  7.2 69.5 %all-gather.15.cloned.1.call-start = ((), (), s32[]{:S(2)}) async-start(), calls=%async_computation.17 | async-start | bytes 2359296 | tf_op jit(solution)/shard_map/all_gather | solution.py:70
  24.9 57.7 %all-gather.17.cloned.1.call-start = ((), (), s32[]{:S(2)}) async-start(), calls=%async_computation.18 | async-start | bytes 2359296 | tf_op jit(solution)/shard_map/all_gather | solution.py:70
  40.0 72.3 %all-gather.13.cloned.1.call-start = ((), (), s32[]{:S(2)}) async-start(), calls=%async_computation.16 | async-start | bytes 2359296 | tf_op jit(solution)/shard_map/all_gather | solution.py:70
  55.4 158.4 %all-gather.29.cloned.1.call-start = ((), (), s32[]{:S(2)}) async-start(), calls=%async_computation.36 | async-start | bytes 1310720 | tf_op jit(solution)/shard_map/all_gather | solution.py:172
  115.2 35.9 %copy-start.16 = (bf16[64,8,8,128]{3,2,1,0:T(8,128)(2,1)}, bf16[64,8,8,128]{3,2,1,0:T(8,128)(2,1)S(1)}, u32[]{:S(2)}) copy-start(bf16[64,8,8,128]{3,2,1,0:T(8,128)(2,1)S(1)} %fusion.25) | copy-start | bytes 3145732
  115.2 18.4 %copy-start.41 = (bf16[256,128]{1,0:T(8,128)(2,1)S(1)}, bf16[256,128]{1,0:T(8,128)(2,1)}, u32[]{:S(2)}) copy-start(bf16[256,128]{1,0:T(8,128)(2,1)} %param.19) | copy-start | bytes 196612
  115.2 35.9 %copy-start.39 = (bf16[128,704]{0,1:T(8,128)(2,1)S(1)}, bf16[128,704]{0,1:T(8,128)(2,1)}, u32[]{:S(2)}) copy-start(bf16[128,704]{0,1:T(8,128)(2,1)} %param.21) | copy-start | bytes 540676
  117.5 101.5 %all-gather.19.cloned.1.call-start = ((), (), s32[]{:S(2)}) async-start(), calls=%async_computation.19 | async-start | bytes 2359296 | tf_op jit(solution)/shard_map/all_gather | solution.py:70
  133.5 90.8 %all-gather.21.cloned.1.call-start = ((), (), s32[]{:S(2)}) async-start(), calls=%async_computation.20 | async-start | bytes 2359296 | tf_op jit(solution)/shard_map/all_gather | solution.py:70
  151.1 105.2 %all-gather.25.cloned.1.call-start = ((), (), s32[]{:S(2)}) async-start(), calls=%async_computation.22 | async-start | bytes 6488064 | tf_op jit(solution)/shard_map/all_gather | solution.py:70
  169.1 38.3 %copy-start.15 = (bf16[512,8,64]{2,0,1:T(8,128)(2,1)S(1)}, bf16[512,8,64]{2,0,1:T(8,128)(2,1)}, u32[]{:S(2)}) copy-start(bf16[512,8,64]{2,0,1:T(8,128)(2,1)} %get-tuple-element.73) | copy-start | bytes 1572868
  169.1 133.4 %all-gather.23.cloned.1.call-start = ((), (), s32[]{:S(2)}) async-start(), calls=%async_computation.21 | async-start | bytes 6488064 | tf_op jit(solution)/shard_map/all_gather | solution.py:70
  188.4 160.3 %all-gather.27.cloned.1.call-start = ((), (), s32[]{:S(2)}) async-start(), calls=%async_computation.23 | async-start | bytes 6488064 | tf_op jit(solution)/shard_map/all_gather | solution.py:70
  205.1 208.6 %all-gather.31.cloned.1.call-start = ((), (), s32[]{:S(2)}) async-start(), calls=%async_computation.37 | async-start | bytes 1310720 | tf_op jit(solution)/shard_map/all_gather | solution.py:211
  385.6 93.0 %reduce-scatter.49.cloned.1.call-start = ((), (), s32[]{:S(2)}) async-start(), calls=%async_computation.38 | async-start | bytes 2359296
  393.5 108.4 %reduce-scatter.37.cloned.1.call-start = ((), (), s32[]{:S(2)}) async-start(), calls=%async_computation.30 | async-start | bytes 2359296 | tf_op jit(solution)/shard_map/reduce_scatter | solution.py:75
  397.8 148.5 %reduce-scatter.33.cloned.1.call-start = ((), (), s32[]{:S(2)}) async-start(), calls=%async_computation.28 | async-start | bytes 2359296 | tf_op jit(solution)/shard_map/reduce_scatter | solution.py:75
  423.6 167.0 %reduce-scatter.29.cloned.1.call-start = ((), (), s32[]{:S(2)}) async-start(), calls=%async_computation.26 | async-start | bytes 2359296 | tf_op jit(solution)/shard_map/reduce_scatter | solution.py:75
  439.0 196.4 %reduce-scatter.25.cloned.1.call-start = ((), (), s32[]{:S(2)}) async-start(), calls=%async_computation.24 | async-start | bytes 2359296 | tf_op jit(solution)/shard_map/reduce_scatter | solution.py:75
  447.0 250.8 %reduce-scatter.45.cloned.1.call-start = ((), (), s32[]{:S(2)}) async-start(), calls=%async_computation.34 | async-start | bytes 6488064 | tf_op jit(solution)/shard_map/reduce_scatter | solution.py:75
  455.0 305.1 %reduce-scatter.43.cloned.1.call-start = ((), (), s32[]{:S(2)}) async-start(), calls=%async_computation.33 | async-start | bytes 6488064 | tf_op jit(solution)/shard_map/reduce_scatter | solution.py:75
  462.0 360.5 %reduce-scatter.55.cloned.1.call-start = ((), (), s32[]{:S(2)}) async-start(), calls=%async_computation.41 | async-start | bytes 6488064
  478.6 366.7 %reduce-scatter.41.cloned.1.call-start = ((), (), s32[]{:S(2)}) async-start(), calls=%async_computation.32 | async-start | bytes 327680 | tf_op jit(solution)/shard_map/reduce_scatter | solution.py:78
  480.5 385.2 %reduce-scatter.39.cloned.1.call-start = ((), (), s32[]{:S(2)}) async-start(), calls=%async_computation.31 | async-start | bytes 327680 | tf_op jit(solution)/shard_map/reduce_scatter | solution.py:78
  501.9 384.3 %reduce-scatter.35.cloned.1.call-start = ((), (), s32[]{:S(2)}) async-start(), calls=%async_computation.29 | async-start | bytes 327680 | tf_op jit(solution)/shard_map/reduce_scatter | solution.py:78
  546.3 360.4 %reduce-scatter.31.cloned.1.call-start = ((), (), s32[]{:S(2)}) async-start(), calls=%async_computation.27 | async-start | bytes 327680 | tf_op jit(solution)/shard_map/reduce_scatter | solution.py:78
  590.6 336.6 %reduce-scatter.27.cloned.1.call-start = ((), (), s32[]{:S(2)}) async-start(), calls=%async_computation.25 | async-start | bytes 327680 | tf_op jit(solution)/shard_map/reduce_scatter | solution.py:78
  635.5 315.1 %reduce-scatter.53.cloned.1.call-start = ((), (), s32[]{:S(2)}) async-start(), calls=%async_computation.40 | async-start | bytes 901120
  700.1 274.8 %reduce-scatter.51.cloned.1.call-start = ((), (), s32[]{:S(2)}) async-start(), calls=%async_computation.39 | async-start | bytes 901120
  762.4 8.6 copy-start.34
  762.4 236.7 %reduce-scatter.47.cloned.1.call-start = ((), (), s32[]{:S(2)}) async-start(), calls=%async_computation.35 | async-start | bytes 901120 | tf_op jit(solution)/shard_map/reduce_scatter | solution.py:78
  (40 other events, 114.8 us)
Sparse Core Ops, SparseCore 0:
  25.0 27.8 all-gather.14
  54.8 27.7 all-gather.16
  84.5 27.7 all-gather.12
  117.7 34.6 all-gather.28
  154.1 26.1 all-gather.18
  182.0 28.0 all-gather.20
  212.0 44.2 all-gather.24
  258.2 44.2 all-gather.22
  304.4 44.2 all-gather.26
  385.7 27.9 all-gather.30
  417.0 40.4 reduce-scatter.48
  460.7 41.1 reduce-scatter.36
  505.2 41.0 reduce-scatter.32
  549.4 41.1 reduce-scatter.28
  594.3 41.1 reduce-scatter.24
  638.8 58.9 reduce-scatter.44
  701.1 58.9 reduce-scatter.42
  763.4 58.9 reduce-scatter.54
  825.3 19.9 reduce-scatter.40
  847.4 18.2 reduce-scatter.38
  867.9 18.2 reduce-scatter.34
  888.4 18.2 reduce-scatter.30
  909.0 18.2 reduce-scatter.26
  929.4 21.1 reduce-scatter.52
  952.9 21.9 reduce-scatter.50
  977.1 21.9 reduce-scatter.46

commit v2 on v1

--- a/solution.py
+++ b/solution.py
@@ -1,6 +1,10 @@
+import functools
+
 import jax
 import jax.numpy as jnp
 from jax import lax
+from jax.experimental import pallas as pl
+from jax.experimental.pallas import tpu as pltpu
 from jax.sharding import PartitionSpec as P
 
 HEAD_DIM = 128
@@ -79,7 +83,359 @@
     return part.astype(jnp.float32)
 
 
+MESH = pl.DeviceIdType.MESH
+VMEM_BYTES = 66_000_000
+
+
+def place():
+    f, t = lax.axis_index("fsdp"), lax.axis_index("tp")
+    return f // 4, (f // 2) % 2, f % 2, f, t
+
+
+def meet(peers):
+    barrier = pltpu.get_barrier_semaphore()
+    for peer in peers:
+        pl.semaphore_signal(barrier, inc=1, device_id=peer, device_id_type=MESH)
+    pl.semaphore_wait(barrier, len(peers))
+
+
+def peers_of(f, t):
+    core = (f // 2 * 2 + (1 - f % 2), t)
+    along_x = (f // 4 * 4 + (f + 2) % 4, t)
+    along_y = ((f + 4) % 8, t)
+    along_z = [(f, (t + d) % 4) for d in (1, 2, 3)]
+    return core, along_x, along_y, along_z
+
+
+def gather_kernel(count, *refs):
+    ins, outs = refs[:count], refs[count : 2 * count]
+    own_sem, z_send, z_recv, n_send, n_recv, c_send, c_recv = refs[2 * count :]
+    y, x, c, f, t = place()
+    core, along_x, along_y, along_z = peers_of(f, t)
+    meet([core, along_x, along_y, *along_z])
+    pieces = [(w, h) for w in range(count) for h in range(2)]
+
+    def rows_of(piece):
+        w, h = piece
+        half = ins[w].shape[0] // 2
+        return pl.ds(h * half, half)
+
+    def slot(piece, *index):
+        return outs[piece[0]].at[(*index, rows_of(piece))]
+
+    def remote(src, dst, send, recv, peer):
+        return pltpu.make_async_remote_copy(
+            src_ref=src, dst_ref=dst, send_sem=send, recv_sem=recv, device_id=peer, device_id_type=MESH
+        )
+
+    def own_copy(p):
+        piece = pieces[p]
+        return pltpu.make_async_copy(
+            ins[piece[0]].at[rows_of(piece)], slot(piece, y, x, c, t), own_sem.at[p]
+        )
+
+    def z_copy(p, d, source):
+        piece = pieces[p]
+        return remote(
+            ins[piece[0]].at[rows_of(piece)],
+            slot(piece, y, x, c, source),
+            z_send.at[p, d],
+            z_recv.at[p, d],
+            along_z[d],
+        )
+
+    def near_copy(p, stage, arriving):
+        piece = pieces[p]
+        over_x = (piece[1] == 0) == (stage == 0)
+        if stage == 0:
+            index = (y, x, c)
+            if arriving:
+                index = (y, 1 - x, c) if over_x else (1 - y, x, c)
+        else:
+            all_ = slice(None)
+            if over_x:
+                index = (all_, (1 - x) if arriving else x, c)
+            else:
+                index = ((1 - y) if arriving else y, all_, c)
+        ref = slot(piece, *index, slice(None))
+        return remote(
+            ref, ref, n_send.at[p, stage], n_recv.at[p, stage], along_x if over_x else along_y
+        )
+
+    def core_copy(p, part, arriving):
+        piece = pieces[p]
+        side = (1 - c) if arriving else c
+        first_x = piece[1] == 0
+        all_ = slice(None)
+        index = (
+            (y, x, side),
+            (y, 1 - x, side) if first_x else (1 - y, x, side),
+            (1 - y, all_, side) if first_x else (all_, 1 - x, side),
+        )[part]
+        ref = slot(piece, *index, slice(None))
+        return remote(ref, ref, c_send.at[p, part], c_recv.at[p, part], core)
+
+    total = len(pieces)
+
+    def start_z(p):
+        own_copy(p).start()
+        for d in range(3):
+            z_copy(p, d, t).start()
+
+    lead = 4
+    for p in range(min(lead, total)):
+        start_z(p)
+    lag = 2
+    for step in range(total + 2 * lag):
+        if lead <= step + lead < total:
+            start_z(step + lead)
+        p = step
+        if p < total:
+            own_copy(p).wait()
+            for d in range(3):
+                z_copy(p, d, (t + 3 - d) % 4).wait_recv()
+            near_copy(p, 0, False).start()
+            core_copy(p, 0, False).start()
+        p = step - lag
+        if 0 <= p < total:
+            near_copy(p, 0, True).wait_recv()
+            near_copy(p, 1, False).start()
+            core_copy(p, 1, False).start()
+        p = step - 2 * lag
+        if 0 <= p < total:
+            near_copy(p, 1, True).wait_recv()
+            core_copy(p, 2, False).start()
+    for p in range(total):
+        for part in range(3):
+            core_copy(p, part, True).wait_recv()
+    for p in range(total):
+        for d in range(3):
+            z_copy(p, d, t).wait_send()
+        for stage in range(2):
+            near_copy(p, stage, False).wait_send()
+        for part in range(3):
+            core_copy(p, part, False).wait_send()
+
+
+def gather_weights(shards):
+    count = len(shards)
+    pieces = 2 * count
+    dma = pltpu.SemaphoreType.DMA
+    return pl.pallas_call(
+        functools.partial(gather_kernel, count),
+        name="gather_weights",
+        out_shape=[jax.ShapeDtypeStruct((2, 2, 2, 4, *s.shape), s.dtype) for s in shards],
+        in_specs=[pl.BlockSpec(memory_space=pltpu.VMEM)] * count,
+        out_specs=[pl.BlockSpec(memory_space=pl.ANY)] * count,
+        scratch_shapes=[
+            dma((pieces,)),
+            dma((pieces, 3)),
+            dma((pieces, 3)),
+            dma((pieces, 2)),
+            dma((pieces, 2)),
+            dma((pieces, 3)),
+            dma((pieces, 3)),
+        ],
+        compiler_params=pltpu.CompilerParams(collective_id=0, has_side_effects=True),
+    )(*shards)
+
+
+def scatter_kernel(count, *refs):
+    ins, outs = refs[:count], refs[count : 2 * count]
+    rest = refs[2 * count :]
+    mine, from_core, from_near, from_far, from_z = (
+        rest[i * count : (i + 1) * count] for i in range(5)
+    )
+    own_sem, c_send, c_recv, n_send, n_recv, z_send, z_recv = rest[5 * count :]
+    y, x, c, f, t = place()
+    core, along_x, along_y, along_z = peers_of(f, t)
+    meet([core, along_x, along_y, *along_z])
+    pieces = [(w, h) for w in range(count) for h in range(2)]
+    total = len(pieces)
+    all_ = slice(None)
+
+    def rows_of(p):
+        w, h = pieces[p]
+        half = outs[w].shape[0] // 2
+        return pl.ds(h * half, half)
+
+    def remote(src, dst, send, recv, peer):
+        return pltpu.make_async_remote_copy(
+            src_ref=src, dst_ref=dst, send_sem=send, recv_sem=recv, device_id=peer, device_id_type=MESH
+        )
+
+    def own_copy(p):
+        w, rows = pieces[p][0], rows_of(p)
+        return pltpu.make_async_copy(
+            ins[w].at[:, :, c, :, rows], mine[w].at[:, :, :, rows], own_sem.at[p]
+        )
+
+    def core_copy(p):
+        w, rows = pieces[p][0], rows_of(p)
+        return remote(
+            ins[w].at[:, :, 1 - c, :, rows],
+            from_core[w].at[:, :, :, rows],
+            c_send.at[p],
+            c_recv.at[p],
+            core,
+        )
+
+    def near_copy(p):
+        (w, h), rows = pieces[p], rows_of(p)
+        src = mine[w].at[1 - y, :, :, rows] if h == 0 else mine[w].at[:, 1 - x, :, rows]
+        return remote(
+            src,
+            from_near[w].at[:, :, rows],
+            n_send.at[p, 0],
+            n_recv.at[p, 0],
+            along_y if h == 0 else along_x,
+        )
+
+    def far_copy(p):
+        (w, h), rows = pieces[p], rows_of(p)
+        src = mine[w].at[y, 1 - x, :, rows] if h == 0 else mine[w].at[1 - y, x, :, rows]
+        return remote(
+            src,
+            from_far[w].at[:, rows],
+            n_send.at[p, 1],
+            n_recv.at[p, 1],
+            along_x if h == 0 else along_y,
+        )
+
+    def z_copy(p, d):
+        w, rows = pieces[p][0], rows_of(p)
+        return remote(
+            mine[w].at[y, x, (t + d + 1) % 4, rows],
+            from_z[w].at[d, rows],
+            z_send.at[p, d],
+            z_recv.at[p, d],
+            along_z[d],
+        )
+
+    def add(steps, target, other):
+        def step(i, carry):
+            into, term = target(i), other(i)
+            into[...] = (into[...].astype(jnp.float32) + term[...].astype(jnp.float32)).astype(
+                jnp.bfloat16
+            )
+            return carry
+
+        lax.fori_loop(0, steps, step, 0)
+
+    def start(p):
+        core_copy(p).start()
+        own_copy(p).start()
+
+    lead, lag = 4, 2
+    for p in range(min(lead, total)):
+        start(p)
+    for step in range(total + 3 * lag):
+        if lead <= step + lead < total:
+            start(step + lead)
+        p = step
+        if p < total:
+            (w, h), rows = pieces[p], rows_of(p)
+            own_copy(p).wait()
+            core_copy(p).wait_recv()
+            add(
+                16,
+                lambda i: mine[w].at[i // 8, i // 4 % 2, i % 4, rows],
+                lambda i: from_core[w].at[i // 8, i // 4 % 2, i % 4, rows],
+            )
+            near_copy(p).start()
+        p = step - lag
+        if 0 <= p < total:
+            (w, h), rows = pieces[p], rows_of(p)
+            near_copy(p).wait_recv()
+            if h == 0:
+                into = lambda i: mine[w].at[y, i // 4, i % 4, rows]
+            else:
+                into = lambda i: mine[w].at[i // 4, x, i % 4, rows]
+            add(8, into, lambda i: from_near[w].at[i // 4, i % 4, rows])
+            far_copy(p).start()
+        p = step - 2 * lag
+        if 0 <= p < total:
+            (w, h), rows = pieces[p], rows_of(p)
+            far_copy(p).wait_recv()
+            add(4, lambda i: mine[w].at[y, x, i, rows], lambda i: from_far[w].at[i, rows])
+            for d in range(3):
+                z_copy(p, d).start()
+        p = step - 3 * lag
+        if 0 <= p < total:
+            (w, h), rows = pieces[p], rows_of(p)
+            for d in range(3):
+                z_copy(p, d).wait_recv()
+            result = mine[w][y, x, t, rows].astype(jnp.float32)
+            for d in range(3):
+                result = result + from_z[w][d, rows].astype(jnp.float32)
+            outs[w][rows] = result
+    for p in range(total):
+        core_copy(p).wait_send()
+        near_copy(p).wait_send()
+        far_copy(p).wait_send()
+        for d in range(3):
+            z_copy(p, d).wait_send()
+
+
+def scatter_grads(grads):
+    count = len(grads)
+    pieces = 2 * count
+    dma = pltpu.SemaphoreType.DMA
+    shards = [g.shape[4:] for g in grads]
+
+    def buffers(*lead):
+        return [pltpu.VMEM((*lead, *s), jnp.bfloat16) for s in shards]
+
+    return pl.pallas_call(
+        functools.partial(scatter_kernel, count),
+        name="scatter_grads",
+        out_shape=[jax.ShapeDtypeStruct(s, jnp.float32) for s in shards],
+        in_specs=[pl.BlockSpec(memory_space=pl.ANY)] * count,
+        out_specs=[pl.BlockSpec(memory_space=pltpu.VMEM)] * count,
+        scratch_shapes=[
+            *buffers(2, 2, 4),
+            *buffers(2, 2, 4),
+            *buffers(2, 4),
+            *buffers(4),
+            *buffers(3),
+            dma((pieces,)),
+            dma((pieces,)),
+            dma((pieces,)),
+            dma((pieces, 2)),
+            dma((pieces, 2)),
+            dma((pieces, 3)),
+            dma((pieces, 3)),
+        ],
+        compiler_params=pltpu.CompilerParams(
+            collective_id=1, has_side_effects=True, vmem_limit_bytes=VMEM_BYTES
+        ),
+    )(*grads)
+
+
+def whole_in(blocks):
+    depth, width = blocks.shape[4:]
+    return blocks.reshape(8, 4, depth, width).transpose(0, 2, 1, 3).reshape(8 * depth, 4 * width)
+
+
+def whole_out(blocks):
+    depth, width = blocks.shape[4:]
+    return blocks.reshape(8, 4, depth, width).transpose(1, 2, 0, 3).reshape(4 * depth, 8 * width)
+
+
+def blocks_in(grad):
+    depth, width = grad.shape[0] // 8, grad.shape[1] // 4
+    part = grad.astype(jnp.bfloat16).reshape(8, depth, 4, width).transpose(0, 2, 1, 3)
+    return part.reshape(2, 2, 2, 4, depth, width)
+
+
+def blocks_out(grad):
+    depth, width = grad.shape[0] // 4, grad.shape[1] // 8
+    part = grad.astype(jnp.bfloat16).reshape(4, depth, 8, width).transpose(2, 0, 1, 3)
+    return part.reshape(2, 2, 2, 4, depth, width)
+
+
 def body(
+    by_kernels,
     tokens,
     lengths,
     rates,
@@ -150,12 +506,28 @@
     tokens_f = tokens.astype(jnp.float32)
     scale1 = rms_scale(tokens_f)
     normed1 = (tokens_f * scale1).astype(jnp.bfloat16)
-    query_full, key_full, value_full, update_full = (
-        gather_full(w, "fsdp", "tp") for w in (w_query, w_key, w_value, w_update)
-    )
-    output_full = gather_full(w_output, "tp", "fsdp")
-    gate_full, up_full = (gather_full(w, "fsdp", "tp") for w in (w_gate, w_up))
-    down_full = gather_full(w_down, "tp", "fsdp")
+    shards = (w_query, w_key, w_value, w_update, w_output, w_gate, w_up, w_down)
+    inner = (True, True, True, True, False, True, True, False)
+    if by_kernels:
+        full = [
+            whole_in(w) if rows_first else whole_out(w)
+            for w, rows_first in zip(gather_weights(shards), inner)
+        ]
+    else:
+        full = [
+            gather_full(w, "fsdp", "tp") if rows_first else gather_full(w, "tp", "fsdp")
+            for w, rows_first in zip(shards, inner)
+        ]
+    (
+        query_full,
+        key_full,
+        value_full,
+        update_full,
+        output_full,
+        gate_full,
+        up_full,
+        down_full,
+    ) = full
     shape_heads = (rows, heads, head_width)
     query_pre = mm(normed1, query_full)
     key_pre = mm(normed1, key_full)
@@ -237,22 +609,25 @@
         + mm_trans(d_update_pre, update_full)
     )
     d_tokens = d_middle + norm_back(tokens_f, scale1, d_normed1)
-    return (
-        result,
-        d_tokens,
-        *(scatter_grad(g, "fsdp", "tp") for g in grads),
-        scatter_grad(grad_output, "tp", "fsdp"),
-        scatter_grad(grad_gate, "fsdp", "tp"),
-        scatter_grad(grad_up, "fsdp", "tp"),
-        scatter_grad(grad_down, "tp", "fsdp"),
-    )
+    grads = (*grads, grad_output, grad_gate, grad_up, grad_down)
+    if by_kernels:
+        grads = scatter_grads(
+            [blocks_in(g) if rows_first else blocks_out(g) for g, rows_first in zip(grads, inner)]
+        )
+    else:
+        grads = [
+            scatter_grad(g, "fsdp", "tp") if rows_first else scatter_grad(g, "tp", "fsdp")
+            for g, rows_first in zip(grads, inner)
+        ]
+    return (result, d_tokens, *grads)
 
 
 def solution(mesh):
     rows = P(AXES, None)
     inner, outer = P("fsdp", "tp"), P("tp", "fsdp")
+    by_kernels = mesh.shape["fsdp"] == 8 and mesh.shape["tp"] == 4
     return jax.shard_map(
-        body,
+        functools.partial(body, by_kernels),
         mesh=mesh,
         in_specs=(
             rows,

time: 1020 us -> 636 us (0.62)
  waiting for transfers between devices: 608 us -> 0.04 us
  Pallas kernels: 0 us -> 287 us
  blocking collectives: 146 us -> 13.5 us
  local copies, waits for them, and re-layouts: 44.8 us -> 153 us
  matrix products: 148 us -> 124 us
    reduce_scatter x12 -> x0, waiting for transfers between devices: 389 us -> none  [the longest x6 277 us: scatter_grad(): lax.psum_scatter(part, 'fsdp', scatter_dimension=0 if row_axis == 'fsdp'...]
    pallas_call x0 -> x2, Pallas kernels: none -> 287 us  [the longest x1 146 us: scatter_grads(): pl.pallas_call(functools.partial(scatter_kernel, count), name='scatter_gr...]
    all_gather x8 -> x0, blocking collectives: 135 us -> none  [gather_full(): lax.all_gather(shard, 'tp', axis=0 if row_axis == 'tp' else 1, tiled=True)]
    all_gather x8 -> x0, waiting for transfers between devices: 122 us -> none  [gather_full(): lax.all_gather(part, 'fsdp', axis=0 if row_axis == 'fsdp' else 1, tiled=T...]
    reshape x0 -> x20, local copies, waits for them, and re-layouts: none -> 106 us  [the longest x10 54.7 us: blocks_in(): grad.astype(jnp.bfloat16).reshape(8, depth, 4, width).transpose(0, 2, 1, 3)]
    unnamed x30 -> x2, waiting for transfers between devices: 90.9 us -> 0.03 us
    dot_general x8, matrix products: 43 us -> 27.3 us  [mm(): return jnp.dot(left, right, preferred_element_type=jnp.float32)]
    transpose x0 -> x2, local copies, waits for them, and re-layouts: none -> 13.9 us  [blocks_in(): grad.astype(jnp.bfloat16).reshape(8, depth, 4, width).transpose(0, 2, 1, 3)]
  transfers between devices with their start and end apart: 26 -> 2, of which waited for: 21 -> 0; matrix products, arithmetic and copies ran while one was open for 18% -> 19% of each run, Pallas kernels for 0% -> 0%
where the time goes in v2:
time: 636 us; the launch traced here: 627 us
  Pallas kernels  287 us (45%)
  local copies, waits for them, and re-layouts  153 us (24%)
  matrix products  124 us (19%)
  other arithmetic  33.4 us (5%)
  between operations  15.9 us (2%)
  blocking collectives  13.5 us (2%)
    pallas_call x1, Pallas kernels, scatter_grads(): pl.pallas_call(functools.partial(scatter_kernel, count), name='scatter_gr...  146 us
    pallas_call x1, Pallas kernels, gather_weights(): pl.pallas_call(functools.partial(gather_kernel, count), name='gather_weig...  141 us
    reshape x10, local copies, waits for them, and re-layouts, blocks_in(): grad.astype(jnp.bfloat16).reshape(8, depth, 4, width).transpose(0, 2, 1, 3)  54.7 us
    dot_general x8, matrix products, mm_trans(): lax.dot_general(left, right, (((1,), (1,)), ((), ())), preferred_element_...  36.3 us
    reshape x6, local copies, waits for them, and re-layouts, whole_in(): blocks.reshape(8, 4, depth, width).transpose(0, 2, 1, 3)  34.4 us
    dot_general x12, matrix products, heads_dot(): return jnp.einsum(spec, left, right, preferred_element_type=jnp.float32)  31.4 us
    unnamed x151, local copies, waits for them, and re-layouts  29.9 us
    dot_general x8, matrix products, mm_inner(): lax.dot_general(left, right, (((0,), (0,)), ((), ())), preferred_element_...  29 us
  transfers between devices with their start and end apart: 2, of which 0 were waited for; matrix products, arithmetic and copies ran while one was open for 19% of the time, Pallas kernels for 0%

profile of v2, /device:TPU:0, one launch (start us, length us, event | category | flops | bytes accessed | tf_op | source)
XLA Modules:
  0.0 626.8 jit_solution(7303272521048554069)
XLA Ops:
  10.1 13.5 %all-reduce = f32[8]{0:T(128)S(1)} all-reduce(f32[8]{0:T(128)S(1)} %dynamic-update-slice), channel_id=1, replica_groups=mesh['fsdp'=8,'tp'=4] {'tp'}, use_global_device_ids=true, to_apply=%add | all-reduce | flops 8 | bytes 64
  31.4 140.7 %gather_weights.1 = (bf16[2,2,2,4,128,256]{5,4,3,2,1,0:T(8,128)(2,1)}, bf16[2,2,2,4,128,256]{5,4,3,2,1,0:T(8,128)(2,1)}, bf16[2,2,2,4,128,256]{5,4,3,2,1,0:T(8,1...) custom-call(bf16[128,256]{1,0:T(8,128)(2,1)} %refs_0_.1, ...), custom_call_target="tpu_custom_call" | custom-call | tf_op jit(solution)/shard_map/gather_weights/pallas_call | solution.py:224
  172.1 4.3 copy.166
  179.7 4.6 fusion.83
  186.9 4.3 copy.170
  208.5 4.3 copy.180
  218.0 9.1 %copy.182 = bf16[8,4,128,704]{2,0,3,1:T(8,128)(2,1)} copy(bf16[8,4,128,704]{3,2,1,0:T(8,128)(2,1)} %bitcast.299) | data formatting | bytes 11534336 | tf_op jit(solution)/shard_map/reshape | solution.py:417
  227.1 9.1 %copy.183 = bf16[8,4,128,704]{2,0,3,1:T(8,128)(2,1)} copy(bf16[8,4,128,704]{3,2,1,0:T(8,128)(2,1)} %bitcast.298) | data formatting | bytes 11534336 | tf_op jit(solution)/shard_map/reshape | solution.py:417
  236.2 8.8 %copy.184 = bf16[8,4,704,128]{3,0,2,1:T(8,128)(2,1)} copy(bf16[8,4,704,128]{3,2,1,0:T(8,128)(2,1)} %bitcast.300) | data formatting | bytes 11534336 | tf_op jit(solution)/shard_map/reshape | solution.py:422
  247.8 4.2 multiply_convert_fusion.1
  264.8 5.0 fusion.10
  269.8 5.0 fusion.6
  274.9 9.1 %multiply_convert_fusion.3 = (bf16[512,2816]{1,0:T(8,128)(2,1)}, bf16[512,2816]{1,0:T(8,128)(2,1)}, bf16[512,2816]{1,0:T(8,128)(2,1)}) fusion(f32[512,2816]{1,0:T(8,128)} %fusion.6, f32[512,2816]{1,0:T(8,128)} %fusion.10, bf16[352,8,8,128]{3,2,1,0:T(8,128)(2,1)S(1)} %bitcast.284, bf16[512,1024]{1,0:T(8,128)(2,1)} %param.23, f32[512]{0:T(512)S(1)} %get-tuple-element.112), kind=kOutput, calls=%fused_computation.17 | convolution fusion | flops 2963013632 | bytes 27002880 | tf_op jit(solution)/shard_map/dot_general | solution.py:57
  284.0 6.8 %fusion.4 = f32[512,1024]{1,0:T(8,128)S(1)} fusion(bf16[512,2816]{1,0:T(8,128)(2,1)} %get-tuple-element.88, bf16[352,8,8,128]{3,2,1,0:T(8,128)(2,1)} %bitcast.305), kind=kOutput, calls=%fused_computation.7 | convolution fusion | flops 2952790016 | bytes 10747904 | tf_op jit(solution)/shard_map/dot_general | solution.py:57
  290.8 6.1 multiply_reduce_fusion
  316.2 4.4 multiply_convert_fusion
  320.6 5.1 convolution_convert_fusion.1
  325.6 5.1 convolution_convert_fusion
  332.8 5.1 fusion.128
  337.9 5.2 convert_bitcast_fusion
  344.9 4.7 reshape.732
  358.8 3.9 copy.212
  362.7 14.0 %reshape.751 = bf16[8,128,4,704]{3,2,1,0:T(4,128)(2,1)} reshape(bf16[1024,2816]{1,0:T(8,128)(2,1)} %convolution_convert_fusion.1) | data formatting | bytes 11534336 | tf_op jit(solution)/shard_map/reshape | solution.py:427
  376.7 6.8 %copy.231 = bf16[8,128,4,704]{3,1,2,0:T(8,128)(2,1)} copy(bf16[8,128,4,704]{3,2,1,0:T(4,128)(2,1)} %reshape.751) | data formatting | bytes 11534336 | tf_op jit(solution)/shard_map/transpose | solution.py:427
  383.5 14.1 %reshape.752 = bf16[8,128,4,704]{3,2,1,0:T(4,128)(2,1)} reshape(bf16[1024,2816]{1,0:T(8,128)(2,1)} %convolution_convert_fusion) | data formatting | bytes 11534336 | tf_op jit(solution)/shard_map/reshape | solution.py:427
  397.6 7.2 %copy.233 = bf16[8,128,4,704]{3,1,2,0:T(8,128)(2,1)} copy(bf16[8,128,4,704]{3,2,1,0:T(4,128)(2,1)} %reshape.752) | data formatting | bytes 11534336 | tf_op jit(solution)/shard_map/transpose | solution.py:427
  408.1 4.1 add_convert_fusion
  416.5 4.3 fusion.34
  434.6 4.6 reshape.730
  450.7 3.6 reshape.726
  461.1 146.3 %scatter_grads.1 = (f32[128,256]{1,0:T(8,128)}, f32[128,256]{1,0:T(8,128)}, f32[128,256]{1,0:T(8,128)}, f32[128,256]{1,0:T(8,128)}, f32[256,128]{1,0:T(8,128)}, ...) custom-call(bf16[2,2,2,4,128,256]{5,4,3,2,1,0:T(8,128)(2,1)} %bitcast.293, ...), custom_call_target="tpu_custom_call" | custom-call | tf_op jit(solution)/shard_map/scatter_grads/pallas_call | solution.py:389
  611.4 4.1 fusion.24
  (237 shorter events, 133.8 us)
Async XLA Ops:
  7.2 244.8 %all-gather.5.cloned.1.call-start = ((), (), s32[]{:S(2)}) async-start(), calls=%async_computation | async-start | bytes 1310720 | tf_op jit(solution)/shard_map/all_gather | solution.py:544
  179.6 4.6 copy-start.19
  208.5 203.7 %all-gather.7.cloned.1.call-start = ((), (), s32[]{:S(2)}) async-start(), calls=%async_computation.1 | async-start | bytes 1310720 | tf_op jit(solution)/shard_map/all_gather | solution.py:583
  215.3 38.4 %copy-start.8 = (bf16[512,8,128]{2,0,1:T(8,128)(2,1)}, bf16[512,8,128]{2,0,1:T(8,128)(2,1)S(1)}, u32[]{:S(2)}) copy-start(bf16[512,8,128]{2,0,1:T(8,128)(2,1)S(1)} %pad_maximum_fusion) | copy-start | bytes 3145732
  262.0 7.8 %slice-start.6 = ((s8[5767168]{0:T(1024)(128)(4,1)}), s8[4194304]{0:T(1024)(128)(4,1)S(1)}, s32[]{:S(2)}) async-start(s8[5767168]{0:T(1024)(128)(4,1)} %bitcast.306), calls=%async_computation.8 | async-start | bytes 8388608
  262.2 7.6 %copy-start.46 = (bf16[512,1024]{1,0:T(8,128)(2,1)}, bf16[512,1024]{1,0:T(8,128)(2,1)S(1)}, u32[]{:S(2)}) copy-start(bf16[512,1024]{1,0:T(8,128)(2,1)S(1)} %multiply_convert_fusion.7) | copy-start | bytes 3145732
  264.8 5.0 slice-start.7
  269.8 5.1 slice-start
  269.8 5.0 slice-start.1
  283.9 6.8 %copy-start.22 = (f32[512,1024]{1,0:T(8,128)S(1)}, f32[512,1024]{1,0:T(8,128)}, u32[]{:S(2)}) copy-start(f32[512,1024]{1,0:T(8,128)} %copy-done.21) | copy-start | bytes 6291460
  284.0 6.8 %copy-start.33 = (bf16[512,2816]{1,0:T(8,128)(2,1)S(1)}, bf16[512,2816]{1,0:T(8,128)(2,1)}, u32[]{:S(2)}) copy-start(bf16[512,2816]{1,0:T(8,128)(2,1)} %get-tuple-element.86) | copy-start | bytes 8650756
  290.8 6.1 copy-start.28
  297.5 9.7 %copy-start.18 = (f32[512,1024]{1,0:T(8,128)}, f32[512,1024]{1,0:T(8,128)S(1)}, u32[]{:S(2)}) copy-start(f32[512,1024]{1,0:T(8,128)S(1)} %multiply_add_fusion.2) | copy-start | bytes 6291460
  313.4 17.3 %copy-start.10 = (bf16[512,8,128]{2,0,1:T(8,128)(2,1)}, bf16[512,8,128]{2,0,1:T(8,128)(2,1)S(1)}, u32[]{:S(2)}) copy-start(bf16[512,8,128]{2,0,1:T(8,128)(2,1)S(1)} %fusion.52) | copy-start | bytes 3145732
  316.2 4.4 copy-start.47
  320.6 5.1 copy-start.32
  325.6 5.1 copy-start.9
  332.8 5.1 copy-start.29
  332.8 5.1 copy-start.30
  337.9 5.2 copy-start.11
  349.6 7.7 %slice-start.8 = ((s8[5767168]{0:T(1024)(128)(4,1)}), s8[4194304]{0:T(1024)(128)(4,1)S(1)}, s32[]{:S(2)}) async-start(s8[5767168]{0:T(1024)(128)(4,1)} %bitcast.309), calls=%async_computation.10 | async-start | bytes 8388608
  383.5 23.8 %slice-start.2 = ((s8[5767168]{0:T(1024)(128)(4,1)}), s8[1572864]{0:T(1024)(128)(4,1)S(1)}, s32[]{:S(2)}) async-start(s8[5767168]{0:T(1024)(128)(4,1)} %bitcast.285), calls=%async_computation.4 | async-start | bytes 3145728
  397.6 7.2 %copy-start.3 = (bf16[8,512,512]{2,1,0:T(8,128)(2,1)S(1)}, bf16[8,512,512]{2,1,0:T(8,128)(2,1)}, u32[]{:S(2)}) copy-start(bf16[8,512,512]{2,1,0:T(8,128)(2,1)} %multiply_convert_fusion) | copy-start | bytes 12582916
  397.6 7.2 %copy-start.24 = (f32[8,128,512]{1,2,0:T(8,128)S(1)}, f32[8,128,512]{1,2,0:T(8,128)}, u32[]{:S(2)}) copy-start(f32[8,128,512]{1,2,0:T(8,128)} %fusion.130) | copy-start | bytes 6291460
  397.6 9.7 %slice-start.3 = ((s8[5767168]{0:T(1024)(128)(4,1)}), s8[4194304]{0:T(1024)(128)(4,1)S(1)}, s32[]{:S(2)}) async-start(s8[5767168]{0:T(1024)(128)(4,1)} %bitcast.285), calls=%async_computation.5 | async-start | bytes 8388608
  416.5 4.3 copy-start.6
  443.6 4.2 copy-start.42
  611.3 4.8 copy-start.52
  611.3 5.5 copy-start.51
  611.3 6.1 copy-start.50
  611.3 6.8 %copy-start.49 = (f32[256,128]{1,0:T(8,128)S(1)}, f32[256,128]{1,0:T(8,128)}, u32[]{:S(2)}) copy-start(f32[256,128]{1,0:T(8,128)} %get-tuple-element.160) | copy-start | bytes 393220
  611.3 7.4 %copy-start.48 = (f32[704,128]{1,0:T(8,128)S(1)}, f32[704,128]{1,0:T(8,128)}, u32[]{:S(2)}) copy-start(f32[704,128]{1,0:T(8,128)} %get-tuple-element.163) | copy-start | bytes 1081348
  (37 other events, 98.4 us)
Sparse Core Ops, SparseCore 0:
  208.6 29.4 all-gather.4
  332.9 29.5 all-gather.6

commit v3 on v2

--- a/solution.py
+++ b/solution.py
@@ -107,21 +107,93 @@
     return core, along_x, along_y, along_z
 
 
-def gather_kernel(count, *refs):
-    ins, outs = refs[:count], refs[count : 2 * count]
-    own_sem, z_send, z_recv, n_send, n_recv, c_send, c_recv = refs[2 * count :]
+FAR = 1e7
+
+
+def swish_of(values):
+    return values * jax.nn.sigmoid(values)
+
+
+def segment_at(where, ends):
+    return sum((where >= end).astype(jnp.int32) for end in ends)
+
+
+def row_tables(lengths_ref, t, rows):
+    ends, total = [], jnp.int32(0)
+    for j in range(SLOTS):
+        total = total + lengths_ref[0, j]
+        ends.append(total)
+    first = t * rows
+    offsets = lax.broadcasted_iota(jnp.int32, (rows, HEAD_DIM), 0)
+    return ends, first, offsets, segment_at(first + offsets, ends)
+
+
+def scalar_segment(where, ends):
+    return sum(jnp.where(where >= end, 1, 0) for end in ends)
+
+
+def fill_span(span_ref, ends, first):
+    rows = span_ref.shape[0]
+    row = first + lax.broadcasted_iota(jnp.int32, (rows, rows), 0)
+    column = first + lax.broadcasted_iota(jnp.int32, (rows, rows), 1)
+    allowed = (segment_at(row, ends) == segment_at(column, ends)) & (row >= column)
+    span_ref[...] = jnp.where(allowed, (row - column).astype(jnp.float32), FAR)
+
+
+def turn(values, cos, sin):
+    return values * cos + pltpu.roll(values, HEAD_DIM // 2, 1) * sin
+
+
+def dot(left, right):
+    return jnp.dot(left, right, preferred_element_type=jnp.float32)
+
+
+def dot_nt(left, right):
+    return lax.dot_general(left, right, (((1,), (1,)), ((), ())), preferred_element_type=jnp.float32)
+
+
+def dot_tn(left, right):
+    return lax.dot_general(left, right, (((0,), (0,)), ((), ())), preferred_element_type=jnp.float32)
+
+
+ORDER = (1, 2, 0, 3, 4, 5, 6, 7)
+N_W = 8
+FWD_IN = ("tokens", "cos", "sin", "lengths", "rates")
+FWD_OUT = (
+    "result", "qp", "kp", "up", "q", "k", "v", "o", "w", "y1", "n2", "a", "g", "e", "states", "rates8",
+)
+
+
+def forward_kernel(*refs):
+    shards, refs = refs[:N_W], refs[N_W:]
+    inp = dict(zip(FWD_IN, refs))
+    refs = refs[len(FWD_IN) :]
+    kept, refs = refs[:N_W], refs[N_W:]
+    out = dict(zip(FWD_OUT, refs))
+    refs = refs[len(FWD_OUT) :]
+    full, refs = refs[:N_W], refs[N_W:]
+    buf = dict(zip(FWD_OUT, refs))
+    refs = refs[len(FWD_OUT) :]
+    n1, span, states, rate_tiles, own_sem, z_send, z_recv, n_send, n_recv, c_send, c_recv = refs[:11]
+    s_send, s_recv, r_send, r_recv, keep_sem, out_sem = refs[11:]
+    rows = inp["tokens"].shape[0]
     y, x, c, f, t = place()
     core, along_x, along_y, along_z = peers_of(f, t)
+    rate_tiles[t] = jnp.concatenate(
+        [jnp.full((1, rows), inp["rates"][i % 2], jnp.float32) for i in range(8)], axis=0
+    )
     meet([core, along_x, along_y, *along_z])
-    pieces = [(w, h) for w in range(count) for h in range(2)]
+    pieces = [(w, h) for w in ORDER for h in range(2)]
+    total = len(pieces)
+    all_ = slice(None)
 
     def rows_of(piece):
         w, h = piece
-        half = ins[w].shape[0] // 2
+        half = shards[w].shape[0] // 2
         return pl.ds(h * half, half)
 
     def slot(piece, *index):
-        return outs[piece[0]].at[(*index, rows_of(piece))]
+        return full[piece[0]].at[(*index, rows_of(piece))]
 
     def remote(src, dst, send, recv, peer):
         return pltpu.make_async_remote_copy(
@@ -131,13 +203,13 @@
     def own_copy(p):
         piece = pieces[p]
         return pltpu.make_async_copy(
-            ins[piece[0]].at[rows_of(piece)], slot(piece, y, x, c, t), own_sem.at[p]
+            shards[piece[0]].at[rows_of(piece)], slot(piece, y, x, c, t), own_sem.at[p]
         )
 
     def z_copy(p, d, source):
         piece = pieces[p]
         return remote(
-            ins[piece[0]].at[rows_of(piece)],
+            shards[piece[0]].at[rows_of(piece)],
             slot(piece, y, x, c, source),
             z_send.at[p, d],
             z_recv.at[p, d],
@@ -152,12 +224,11 @@
             if arriving:
                 index = (y, 1 - x, c) if over_x else (1 - y, x, c)
         else:
-            all_ = slice(None)
             if over_x:
                 index = (all_, (1 - x) if arriving else x, c)
             else:
                 index = ((1 - y) if arriving else y, all_, c)
-        ref = slot(piece, *index, slice(None))
+        ref = slot(piece, *index, all_)
         return remote(
             ref, ref, n_send.at[p, stage], n_recv.at[p, stage], along_x if over_x else along_y
         )
@@ -166,26 +237,237 @@
         piece = pieces[p]
         side = (1 - c) if arriving else c
         first_x = piece[1] == 0
-        all_ = slice(None)
         index = (
             (y, x, side),
             (y, 1 - x, side) if first_x else (1 - y, x, side),
             (1 - y, all_, side) if first_x else (all_, 1 - x, side),
         )[part]
-        ref = slot(piece, *index, slice(None))
+        ref = slot(piece, *index, all_)
         return remote(ref, ref, c_send.at[p, part], c_recv.at[p, part], core)
-
-    total = len(pieces)
 
     def start_z(p):
         own_copy(p).start()
         for d in range(3):
             z_copy(p, d, t).start()
 
-    lead = 4
+    def arrived(w):
+        for h in range(2):
+            for part in range(3):
+                core_copy(pieces.index((w, h)), part, True).wait_recv()
+        keep(w).start()
+
+    def keep(w):
+        return pltpu.make_async_copy(full[w], kept[w], keep_sem.at[w])
+
+    def save(name):
+        return pltpu.make_async_copy(buf[name], out[name], out_sem.at[FWD_OUT.index(name)])
+
+    def rate_copy(d, source):
+        ref = rate_tiles.at[source]
+        return remote(ref, ref, r_send.at[d], r_recv.at[d], along_z[d])
+
+    def state_copy(d, source):
+        ref = states.at[source]
+        return remote(ref, ref, s_send.at[d], s_recv.at[d], along_z[d])
+
+    ends, first, offsets, segments = row_tables(inp["lengths"], t, rows)
+    steps_f = offsets.astype(jnp.float32)
+
+    def rate_of(h):
+        return buf["rates8"][pl.ds(h, 1), :]
+
+    def begin():
+        for d in range(3):
+            rate_copy(d, t).start()
+        values = inp["tokens"][...].astype(jnp.float32)
+        n1[...] = (values * rms_scale(values)).astype(jnp.bfloat16)
+        fill_span(span, ends, first)
+
+    def rates_here():
+        for d in range(3):
+            rate_copy(d, (t + 3 - d) % 4).wait_recv()
+        for j in range(4):
+            buf["rates8"][2 * j : 2 * j + 2] = rate_tiles[j, 0:2]
+        save("rates8").start()
+
+    def project(w, finish):
+        def run():
+            arrived(w)
+
+            def block(i, carry):
+                columns = full[w][:, :, :, i].reshape(n1.shape[1], full[w].shape[5])
+                values = dot(n1[...], columns)
+                for j in range(2):
+                    finish(2 * i + j, values[:, j * HEAD_DIM : (j + 1) * HEAD_DIM])
+                return carry
+
+            lax.fori_loop(0, 4, block, 0)
+
+        return run
+
+    def finish_key(h, values):
+        buf["kp"][h] = values.astype(jnp.bfloat16)
+        buf["k"][h] = turn(swish_of(values), inp["cos"][...], inp["sin"][...]).astype(jnp.bfloat16)
+
+    def finish_query(h, values):
+        buf["qp"][h] = values.astype(jnp.bfloat16)
+        buf["q"][h] = turn(swish_of(values), inp["cos"][...], inp["sin"][...]).astype(jnp.bfloat16)
+
+    def finish_value(h, values):
+        buf["v"][h] = values.astype(jnp.bfloat16)
+
+    def finish_update(h, values):
+        buf["up"][h] = values.astype(jnp.bfloat16)
+        columns = pl.ds(pl.multiple_of(h * HEAD_DIM, HEAD_DIM), HEAD_DIM)
+        buf["y1"][:, columns] = swish_of(values)
+
+    def make_states():
+        last = scalar_segment(first + rows - 1, ends)
+
+        def head(h, carry):
+            rate = rate_of(h)[:, :HEAD_DIM]
+            to_end = jnp.where(segments == last, jnp.exp(-(rows - 1.0 - steps_f) * rate), 0.0)
+            scaled = (buf["k"][h].astype(jnp.float32) * to_end).astype(jnp.bfloat16)
+            states[t, h] = dot_tn(scaled, buf["v"][h]).astype(jnp.bfloat16)
+            return carry
+
+        lax.fori_loop(0, 8, head, 0)
+        for name in ("k", "v", "kp"):
+            save(name).start()
+
+    def send_states():
+        for d in range(3):
+            state_copy(d, t).start()
+
+    def sum_states():
+        for d in range(3):
+            state_copy(d, (t + 3 - d) % 4).wait_recv()
+        before = scalar_segment(first - 1, ends)
+
+        def head(h, carry):
+            rate = rate_of(h)[:, :HEAD_DIM]
+            result = jnp.zeros((HEAD_DIM, HEAD_DIM), jnp.float32)
+            for j in range(3):
+                reach = jnp.where(
+                    (j < t) & (scalar_segment(j * rows + rows - 1, ends) == before), 1.0, 0.0
+                )
+                distance = jnp.maximum(t - j - 1, 0).astype(jnp.float32) * rows
+                weight = reach * jnp.exp(-rate * distance)
+                result = result + weight * states[j, h].astype(jnp.float32)
+            buf["states"][h] = result.astype(jnp.bfloat16)
+            return carry
+
+        lax.fori_loop(0, 8, head, 0)
+        save("states").start()
+        for name in ("q", "qp", "up"):
+            save(name).start()
+
+    def attend(lo, hi):
+        before = scalar_segment(first - 1, ends)
+
+        def head(h, carry):
+            rate = rate_of(h)
+            columns = pl.ds(pl.multiple_of(h * HEAD_DIM, HEAD_DIM), HEAD_DIM)
+            half = rows // 2
+            for b in range(2):
+                mine = slice(b * half, (b + 1) * half)
+                keys = (b + 1) * half
+                query = buf["q"][h, mine]
+                scores = dot_nt(query, buf["k"][h, :keys])
+                decay = jnp.exp(-span[mine, :keys] * rate[:, :keys])
+                weights = (scores * decay).astype(jnp.bfloat16)
+                into = jnp.where(
+                    segments[mine] == before, jnp.exp(-(steps_f[mine] + 1.0) * rate[:, :HEAD_DIM]), 0.0
+                )
+                attn = dot(weights, buf["v"][h, :keys]) + into * dot(query, buf["states"][h])
+                buf["o"][h, mine] = attn
+                normed = attn * rms_scale(attn, head_floor)
+                buf["w"][mine, columns] = (normed * buf["y1"][mine, columns]).astype(jnp.bfloat16)
+            return carry
+
+        return lambda: (lax.fori_loop(lo, hi, head, 0), None)[1]
+
+    def mix():
+        save("o").start()
+        save("w").start()
+        arrived(4)
+
+        def block(i, carry):
+            sides = [full[4][i // 2, i % 2, s].reshape(n1.shape[1], HEAD_DIM) for s in range(2)]
+            columns = pl.ds(pl.multiple_of(i * 2 * HEAD_DIM, 2 * HEAD_DIM), 2 * HEAD_DIM)
+            buf["y1"][:, columns] = inp["tokens"][:, columns].astype(jnp.float32) + dot(
+                buf["w"][...], jnp.concatenate(sides, axis=1)
+            )
+            return carry
+
+        lax.fori_loop(0, 4, block, 0)
+        values = buf["y1"][...]
+        buf["n2"][...] = (values * rms_scale(values)).astype(jnp.bfloat16)
+        save("y1").start()
+        save("n2").start()
+
+    def gate_up(i):
+        def go():
+            if i == 0:
+                arrived(6)
+            shape = (n1.shape[1], full[5].shape[5])
+            for b in range(2):
+                mine = slice(b * rows // 2, (b + 1) * rows // 2)
+                gate = dot(buf["n2"][mine], full[5][:, :, :, i].reshape(shape))
+                lift = dot(buf["n2"][mine], full[6][:, :, :, i].reshape(shape))
+                buf["a"][i, mine] = (gate * lift).astype(jnp.bfloat16)
+                buf["g"][i, mine] = gate.astype(jnp.bfloat16)
+                buf["e"][i, mine] = lift.astype(jnp.bfloat16)
+            if i == 3:
+                for name in ("a", "g", "e"):
+                    save(name).start()
+
+        return go
+
+    def close():
+        arrived(7)
+
+        def block(i, carry):
+            columns = pl.ds(pl.multiple_of(i * 2 * HEAD_DIM, 2 * HEAD_DIM), 2 * HEAD_DIM)
+            values = buf["y1"][:, columns]
+            for j in range(4):
+                sides = [full[7][i // 2, i % 2, s, j] for s in range(2)]
+                values = values + dot(buf["a"][j], jnp.concatenate(sides, axis=1))
+            buf["result"][:, columns] = values.astype(jnp.bfloat16)
+            return carry
+
+        lax.fori_loop(0, 4, block, 0)
+        save("result").start()
+
+    lead, lag = 4, 2
+
+    def ready(w):
+        return 2 * ORDER.index(w) + 1 + 2 * lag + 1
+
+    work = [
+        (0, begin),
+        (4, rates_here),
+        (ready(1), project(1, finish_key)),
+        (ready(2), project(2, finish_value)),
+        (ready(2), make_states),
+        (ready(0), send_states),
+        (ready(0), project(0, finish_query)),
+        (ready(3), project(3, finish_update)),
+        (ready(3), sum_states),
+        *[(ready(3), attend(h, h + 2)) for h in range(0, 8, 2)],
+        (ready(4), mix),
+        (ready(5), lambda: arrived(5)),
+        *[(ready(6), gate_up(i)) for i in range(4)],
+        (ready(7), close),
+    ]
+
+    def some_work(step):
+        if work and work[0][0] <= step:
+            work.pop(0)[1]()
+
     for p in range(min(lead, total)):
         start_z(p)
-    lag = 2
+    some_work(0)
     for step in range(total + 2 * lag):
         if lead <= step + lead < total:
             start_z(step + lead)
@@ -196,18 +478,23 @@
                 z_copy(p, d, (t + 3 - d) % 4).wait_recv()
             near_copy(p, 0, False).start()
             core_copy(p, 0, False).start()
+            some_work(step)
         p = step - lag
         if 0 <= p < total:
             near_copy(p, 0, True).wait_recv()
             near_copy(p, 1, False).start()
             core_copy(p, 1, False).start()
+            some_work(step)
         p = step - 2 * lag
         if 0 <= p < total:
             near_copy(p, 1, True).wait_recv()
             core_copy(p, 2, False).start()
-    for p in range(total):
-        for part in range(3):
-            core_copy(p, part, True).wait_recv()
+            some_work(step)
+    while work:
+        work.pop(0)[1]()
+    for d in range(3):
+        rate_copy(d, t).wait_send()
+        state_copy(d, t).wait_send()
     for p in range(total):
         for d in range(3):
             z_copy(p, d, t).wait_send()
@@ -215,19 +502,55 @@
             near_copy(p, stage, False).wait_send()
         for part in range(3):
             core_copy(p, part, False).wait_send()
-
-
-def gather_weights(shards):
-    count = len(shards)
-    pieces = 2 * count
+    for w in range(N_W):
+        keep(w).wait()
+    for name in FWD_OUT:
+        save(name).wait()
+
+
+def forward(shards, tokens, cos, sin, lengths, rates):
+    rows, width = tokens.shape
+    units = shards[5].shape[1]
+    heads = width // HEAD_DIM
+    low, wide = jnp.bfloat16, jnp.float32
+    by_head = (heads, rows, HEAD_DIM)
+    by_unit = (4, rows, units)
+    shapes = {
+        "result": ((rows, width), low),
+        "qp": (by_head, low),
+        "kp": (by_head, low),
+        "up": (by_head, low),
+        "q": (by_head, low),
+        "k": (by_head, low),
+        "v": (by_head, low),
+        "o": (by_head, wide),
+        "w": ((rows, width), low),
+        "y1": ((rows, width), wide),
+        "n2": ((rows, width), low),
+        "a": (by_unit, low),
+        "g": (by_unit, low),
+        "e": (by_unit, low),
+        "states": ((heads, HEAD_DIM, HEAD_DIM), low),
+        "rates8": ((8, rows), wide),
+    }
+    blocks = [(2, 2, 2, 4, *s.shape) for s in shards]
+    pieces = 2 * N_W
     dma = pltpu.SemaphoreType.DMA
-    return pl.pallas_call(
-        functools.partial(gather_kernel, count),
-        name="gather_weights",
-        out_shape=[jax.ShapeDtypeStruct((2, 2, 2, 4, *s.shape), s.dtype) for s in shards],
-        in_specs=[pl.BlockSpec(memory_space=pltpu.VMEM)] * count,
-        out_specs=[pl.BlockSpec(memory_space=pl.ANY)] * count,
+    in_vmem, in_smem = (pl.BlockSpec(memory_space=m) for m in (pltpu.VMEM, pltpu.SMEM))
+    outs = pl.pallas_call(
+        forward_kernel,
+        name="gather_and_forward",
+        out_shape=[jax.ShapeDtypeStruct(b, low) for b in blocks]
+        + [jax.ShapeDtypeStruct(*shapes[name]) for name in FWD_OUT],
+        in_specs=[in_vmem] * (N_W + 3) + [in_smem] * 2,
+        out_specs=[pl.BlockSpec(memory_space=pl.ANY)] * (N_W + len(FWD_OUT)),
         scratch_shapes=[
+            *[pltpu.VMEM(b, low) for b in blocks],
+            *[pltpu.VMEM(*shapes[name]) for name in FWD_OUT],
+            pltpu.VMEM((rows, width), low),
+            pltpu.VMEM((rows, rows), wide),
+            pltpu.VMEM((4, heads, HEAD_DIM, HEAD_DIM), low),
+            pltpu.VMEM((4, 8, rows), wide),
             dma((pieces,)),
             dma((pieces, 3)),
             dma((pieces, 3)),
@@ -235,9 +558,18 @@
             dma((pieces, 2)),
             dma((pieces, 3)),
             dma((pieces, 3)),
+            dma((3,)),
+            dma((3,)),
+            dma((3,)),
+            dma((3,)),
+            dma((N_W,)),
+            dma((len(FWD_OUT),)),
         ],
-        compiler_params=pltpu.CompilerParams(collective_id=0, has_side_effects=True),
-    )(*shards)
+        compiler_params=pltpu.CompilerParams(
+            collective_id=0, has_side_effects=True, vmem_limit_bytes=VMEM_BYTES
+        ),
+    )(*shards, tokens, cos, sin, lengths, rates)
+    return outs[:N_W], dict(zip(FWD_OUT, outs[N_W:]))
 
 
 def scatter_kernel(count, *refs):
@@ -453,8 +785,6 @@
     tp_index = lax.axis_index("tp")
     rows, width = tokens.shape
     head_width = HEAD_DIM
-    all_rates = lax.all_gather(rates, "tp", axis=0, tiled=True)
-    heads = all_rates.shape[0]
     ends = jnp.cumsum(lengths[0], dtype=jnp.int32)
     first = tp_index * rows
     places = first + jnp.arange(rows, dtype=jnp.int32)
@@ -469,55 +799,24 @@
     turned = positions[:, None] * frequency[None, :]
     cos_table, sin_table = jnp.cos(turned)[:, None, :], jnp.sin(turned)[:, None, :]
 
-    gaps = places[:, None] - places[None, :]
-    allowed = (segments[:, None] == segments[None, :]) & (gaps >= 0)
-    spans = jnp.maximum(gaps, 0).astype(jnp.float32)
-    decay = jnp.where(
-        allowed[None], jnp.exp(-all_rates[:, None, None] * spans[None]), 0.0
-    )
-    blocks = jnp.arange(tp_count, dtype=jnp.int32)
-    seg_before = segment_of(first - 1, ends)
-    seg_after = segment_of(first + rows, ends)
-    seg_last = segment_of(blocks * rows + rows - 1, ends)
-    seg_first = segment_of(blocks * rows, ends)
-    offsets = jnp.arange(rows, dtype=jnp.float32)
-
-    def row_decay(distance, mask):
-        return jnp.where(mask[:, None], jnp.exp(-distance[:, None] * all_rates[None]), 0.0)[
-            :, :, None
-        ]
-
-    to_end = row_decay(rows - 1 - offsets, segments == segments[rows - 1])
-    from_start = row_decay(offsets, segments == segments[0])
-    into = row_decay(offsets + 1.0, segments == seg_before)
-    out_of = row_decay(rows - offsets, segments == seg_after)
-
-    def block_weights(mask, distance):
-        distance = jnp.maximum(distance, 0).astype(jnp.float32)
-        return jnp.where(mask[:, None], jnp.exp(-distance[:, None] * all_rates[None]), 0.0)
-
-    before_weights = block_weights(
-        (blocks < tp_index) & (seg_last == seg_before), (tp_index - blocks - 1) * rows
-    )
-    after_weights = block_weights(
-        (blocks > tp_index) & (seg_first == seg_after), (blocks - tp_index - 1) * rows
-    )
-
     tokens_f = tokens.astype(jnp.float32)
     scale1 = rms_scale(tokens_f)
     normed1 = (tokens_f * scale1).astype(jnp.bfloat16)
     shards = (w_query, w_key, w_value, w_update, w_output, w_gate, w_up, w_down)
     inner = (True, True, True, True, False, True, True, False)
     if by_kernels:
-        full = [
-            whole_in(w) if rows_first else whole_out(w)
-            for w, rows_first in zip(gather_weights(shards), inner)
-        ]
+        cos2 = jnp.concatenate([cos_table, cos_table], axis=2).reshape(rows, head_width)
+        sin2 = jnp.concatenate([-sin_table, sin_table], axis=2).reshape(rows, head_width)
+        kept, saved = forward(shards, tokens, cos2, sin2, lengths, rates)
+        full = [whole_in(w) if rows_first else whole_out(w) for w, rows_first in zip(kept, inner)]
+        all_rates = saved["rates8"][:, 0]
     else:
         full = [
             gather_full(w, "fsdp", "tp") if rows_first else gather_full(w, "tp", "fsdp")
             for w, rows_first in zip(shards, inner)
         ]
+        all_rates = lax.all_gather(rates, "tp", axis=0, tiled=True)
+    heads = all_rates.shape[0]
     (
         query_full,
         key_full,
@@ -528,37 +827,87 @@
         up_full,
         down_full,
     ) = full
+    gaps = places[:, None] - places[None, :]
+    allowed = (segments[:, None] == segments[None, :]) & (gaps >= 0)
+    spans = jnp.maximum(gaps, 0).astype(jnp.float32)
+    decay = jnp.where(
+        allowed[None], jnp.exp(-all_rates[:, None, None] * spans[None]), 0.0
+    )
+    blocks = jnp.arange(tp_count, dtype=jnp.int32)
+    seg_before = segment_of(first - 1, ends)
+    seg_after = segment_of(first + rows, ends)
+    seg_last = segment_of(blocks * rows + rows - 1, ends)
+    seg_first = segment_of(blocks * rows, ends)
+    offsets = jnp.arange(rows, dtype=jnp.float32)
+
+    def row_decay(distance, mask):
+        return jnp.where(mask[:, None], jnp.exp(-distance[:, None] * all_rates[None]), 0.0)[
+            :, :, None
+        ]
+
+    to_end = row_decay(rows - 1 - offsets, segments == segments[rows - 1])
+    from_start = row_decay(offsets, segments == segments[0])
+    into = row_decay(offsets + 1.0, segments == seg_before)
+    out_of = row_decay(rows - offsets, segments == seg_after)
+
+    def block_weights(mask, distance):
+        distance = jnp.maximum(distance, 0).astype(jnp.float32)
+        return jnp.where(mask[:, None], jnp.exp(-distance[:, None] * all_rates[None]), 0.0)
+
+    before_weights = block_weights(
+        (blocks < tp_index) & (seg_last == seg_before), (tp_index - blocks - 1) * rows
+    )
+    after_weights = block_weights(
+        (blocks > tp_index) & (seg_first == seg_after), (blocks - tp_index - 1) * rows
+    )
+
     shape_heads = (rows, heads, head_width)
-    query_pre = mm(normed1, query_full)
-    key_pre = mm(normed1, key_full)
-    value_rows = mm(normed1, value_full).astype(jnp.bfloat16).reshape(shape_heads)
-    update_pre = mm(normed1, update_full)
-    query = rotate(swish(query_pre).reshape(shape_heads), cos_table, sin_table).astype(jnp.bfloat16)
-    key_rows = rotate(swish(key_pre).reshape(shape_heads), cos_table, sin_table).astype(
-        jnp.bfloat16
-    )
-    update = swish(update_pre)
-    key_state = heads_dot(
-        "shc,shd->hcd", (key_rows * to_end).astype(jnp.bfloat16), value_rows
-    ).astype(jnp.bfloat16)
-    key_states = lax.all_gather(key_state, "tp", axis=0, tiled=False)
-    state_in = jnp.sum(
-        key_states.astype(jnp.float32) * before_weights[:, :, None, None], axis=0
-    ).astype(jnp.bfloat16)
-    weights = (heads_dot("thc,shc->hts", query, key_rows) * decay).astype(jnp.bfloat16)
-    attn = heads_dot("hts,shd->thd", weights, value_rows) + into * heads_dot(
-        "thc,hcd->thd", query, state_in
-    )
-    scale_attn = rms_scale(attn, head_floor)
-    normed_attn = (attn * scale_attn).reshape(rows, width)
-    mixed = (normed_attn * update).astype(jnp.bfloat16)
-    middle = tokens_f + mm(mixed, output_full)
-    scale2 = rms_scale(middle)
-    normed2 = (middle * scale2).astype(jnp.bfloat16)
-    gate_rows = mm(normed2, gate_full)
-    up_rows = mm(normed2, up_full)
-    hidden = (gate_rows * up_rows).astype(jnp.bfloat16)
-    result = (middle + mm(hidden, down_full)).astype(jnp.bfloat16)
+    if by_kernels:
+        by_row = lambda name: saved[name].transpose(1, 0, 2)
+        query_pre, key_pre, update_pre = (
+            by_row(n).reshape(rows, width).astype(jnp.float32) for n in ("qp", "kp", "up")
+        )
+        query, key_rows, value_rows = (by_row(n) for n in ("q", "k", "v"))
+        update = swish(update_pre)
+        state_in = saved["states"]
+        attn = by_row("o")
+        weights = (heads_dot("thc,shc->hts", query, key_rows) * decay).astype(jnp.bfloat16)
+        scale_attn = rms_scale(attn, head_floor)
+        normed_attn = (attn * scale_attn).reshape(rows, width)
+        mixed, middle, normed2, result = (saved[n] for n in ("w", "y1", "n2", "result"))
+        scale2 = rms_scale(middle)
+        hidden, gate_rows, up_rows = (by_row(n).reshape(rows, -1) for n in ("a", "g", "e"))
+    else:
+        query_pre = mm(normed1, query_full)
+        key_pre = mm(normed1, key_full)
+        value_rows = mm(normed1, value_full).astype(jnp.bfloat16).reshape(shape_heads)
+        update_pre = mm(normed1, update_full)
+        query = rotate(swish(query_pre).reshape(shape_heads), cos_table, sin_table).astype(jnp.bfloat16)
+        key_rows = rotate(swish(key_pre).reshape(shape_heads), cos_table, sin_table).astype(
+            jnp.bfloat16
+        )
+        update = swish(update_pre)
+        key_state = heads_dot(
+            "shc,shd->hcd", (key_rows * to_end).astype(jnp.bfloat16), value_rows
+        ).astype(jnp.bfloat16)
+        key_states = lax.all_gather(key_state, "tp", axis=0, tiled=False)
+        state_in = jnp.sum(
+            key_states.astype(jnp.float32) * before_weights[:, :, None, None], axis=0
+        ).astype(jnp.bfloat16)
+        weights = (heads_dot("thc,shc->hts", query, key_rows) * decay).astype(jnp.bfloat16)
+        attn = heads_dot("hts,shd->thd", weights, value_rows) + into * heads_dot(
+            "thc,hcd->thd", query, state_in
+        )
+        scale_attn = rms_scale(attn, head_floor)
+        normed_attn = (attn * scale_attn).reshape(rows, width)
+        mixed = (normed_attn * update).astype(jnp.bfloat16)
+        middle = tokens_f + mm(mixed, output_full)
+        scale2 = rms_scale(middle)
+        normed2 = (middle * scale2).astype(jnp.bfloat16)
+        gate_rows = mm(normed2, gate_full)
+        up_rows = mm(normed2, up_full)
+        hidden = (gate_rows * up_rows).astype(jnp.bfloat16)
+        result = (middle + mm(hidden, down_full)).astype(jnp.bfloat16)
 
     cotangent = out_grad.astype(jnp.float32) * live[:, None]
     cot_rows = cotangent.astype(jnp.bfloat16)

time: 636 us -> 696 us (1.094)
  local copies, waits for them, and re-layouts: 153 us -> 203 us
  Pallas kernels: 287 us -> 324 us
  matrix products: 124 us -> 96.9 us
  blocking collectives: 13.5 us -> 0 us
  other arithmetic: 33.4 us -> 44.2 us
    convert_element_type x0 -> x12, local copies, waits for them, and re-layouts: none -> 42 us  [the longest x6 13.5 us: body(): by_row(n).reshape(rows, width).astype(jnp.float32)]
    pallas_call x1, Pallas kernels: 141 us -> 174 us  [forward(): pl.pallas_call(forward_kernel, name='gather_and_forward', out_shape=[jax....]
    dot_general x8 -> x0, matrix products: 27.3 us -> none  [mm(): return jnp.dot(left, right, preferred_element_type=jnp.float32)]
    convert_element_type x1 -> x6, other arithmetic: 0.18 us -> 14.6 us  [the longest x1 5.04 us: body(): d_gate = (d_hidden * up_rows).astype(jnp.bfloat16)]
    unnamed x1 -> x0, blocking collectives: 13.5 us -> none
    reshape x0 -> x4, local copies, waits for them, and re-layouts: none -> 8.72 us  [the longest x1 3.07 us: body(): (d_mixed * update).reshape(shape_heads)]
    dot_general x8, matrix products: 29 us -> 37 us  [mm_inner(): lax.dot_general(left, right, (((0,), (0,)), ((), ())), preferred_element_...]
    unnamed x151 -> x135, local copies, waits for them, and re-layouts: 29.9 us -> 24.7 us
  transfers between devices with their start and end apart: 2 -> 1, of which waited for: 0 -> 0; matrix products, arithmetic and copies ran while one was open for 19% -> 22% of each run, Pallas kernels for 0% -> 0%
where the time goes in v3:
time: 696 us; the launch traced here: 684 us
  Pallas kernels  324 us (47%)
  local copies, waits for them, and re-layouts  203 us (29%)
  matrix products  96.9 us (14%)
  other arithmetic  44.2 us (6%)
  between operations  15.3 us (2%)
    pallas_call x1, Pallas kernels, forward(): pl.pallas_call(forward_kernel, name='gather_and_forward', out_shape=[jax....  174 us
    pallas_call x1, Pallas kernels, scatter_grads(): pl.pallas_call(functools.partial(scatter_kernel, count), name='scatter_gr...  150 us
    reshape x10, local copies, waits for them, and re-layouts, blocks_in(): grad.astype(jnp.bfloat16).reshape(8, depth, 4, width).transpose(0, 2, 1, 3)  48.5 us
    dot_general x8, matrix products, mm_inner(): lax.dot_general(left, right, (((0,), (0,)), ((), ())), preferred_element_...  37 us
    dot_general x8, matrix products, mm_trans(): lax.dot_general(left, right, (((1,), (1,)), ((), ())), preferred_element_...  33.5 us
    reshape x6, local copies, waits for them, and re-layouts, whole_in(): blocks.reshape(8, 4, depth, width).transpose(0, 2, 1, 3)  33 us
    dot_general x8, matrix products, heads_dot(): return jnp.einsum(spec, left, right, preferred_element_type=jnp.float32)  26.4 us
    unnamed x135, local copies, waits for them, and re-layouts  24.7 us
  transfers between devices with their start and end apart: 1, of which 0 were waited for; matrix products, arithmetic and copies ran while one was open for 22% of the time, Pallas kernels for 0%

profile of v3, /device:TPU:0, one launch (start us, length us, event | category | flops | bytes accessed | tf_op | source)
XLA Modules:
  0.0 684.1 jit_solution(15991640903348593229)
XLA Ops:
  15.6 174.3 %gather_and_forward.1 = (bf16[2,2,2,4,128,256]{5,4,3,2,1,0:T(8,128)(2,1)}, bf16[2,2,2,4,128,256]{5,4,3,2,1,0:T(8,128)(2,1)}, bf16[2,2,2,4,128,256]{5,4,3,2,1,0:T...) custom-call(bf16[128,256]{1,0:T(8,128)(2,1)} %refs_0_.1, ...), custom_call_target="tpu_custom_call" | custom-call | tf_op jit(solution)/shard_map/gather_and_forward/pallas_call | solution.py:540
  189.9 5.0 convert_bitcast_fusion.1
  194.9 6.3 copy.168
  201.3 6.5 copy.169
  210.9 6.3 copy.171
  217.2 6.3 copy.172
  223.5 8.8 %copy.167 = bf16[8,4,704,128]{3,0,2,1:T(8,128)(2,1)} copy(bf16[8,4,704,128]{3,2,1,0:T(8,128)(2,1)} %bitcast.251) | data formatting | bytes 11534336 | tf_op jit(solution)/shard_map/reshape | solution.py:754
  232.3 9.2 %copy.173 = bf16[8,4,128,704]{2,0,3,1:T(8,128)(2,1)} copy(bf16[8,4,128,704]{3,2,1,0:T(8,128)(2,1)} %bitcast.250) | data formatting | bytes 11534336 | tf_op jit(solution)/shard_map/reshape | solution.py:749
  241.7 9.6 %copy.170 = bf16[8,4,128,704]{2,0,3,1:T(8,128)(2,1)} copy(bf16[8,4,128,704]{3,2,1,0:T(8,128)(2,1)} %bitcast.249) | data formatting | bytes 11534336 | tf_op jit(solution)/shard_map/reshape | solution.py:749
  253.2 9.2 %multiply_convert_fusion.3 = (bf16[512,2816]{1,0:T(8,128)(2,1)S(1)}, bf16[512,2816]{1,0:T(8,128)(2,1)S(1)}) fusion(f32[512,2816]{1,0:T(8,128)} %copy.169, f32[512,2816]{1,0:T(8,128)} %copy.172, bf16[352,8,8,128]{3,2,1,0:T(8,128)(2,1)} %bitcast.234, bf16[512,1024]{1,0:T(8,128)(2,1)S(1)} %copy-done.24, f32[512]{0:T(512)S(1)} %get-tuple-element.138), kind=kOutput, calls=%fused_computation.16 | convolution fusion | flops 2960130048 | bytes 24119296 | tf_op jit(solution)/shard_map/dot_general | solution.py:57
  262.5 7.9 %fusion = f32[512,1024]{1,0:T(8,128)S(1)} fusion(bf16[512,2816]{1,0:T(8,128)(2,1)S(1)} %get-tuple-element.123, bf16[352,8,8,128]{3,2,1,0:T(8,128)(2,1)} %bitcast.252), kind=kOutput, calls=%fused_computation.5 | convolution fusion | flops 2952790016 | bytes 10747904 | tf_op jit(solution)/shard_map/dot_general | solution.py:57
  270.4 4.5 multiply_reduce_fusion.1
  278.9 3.7 copy.174
  305.7 6.7 convolution_convert_fusion.1
  312.5 5.1 convolution_convert_fusion
  332.0 4.7 copy.221
  336.7 6.9 %convert_bitcast_fusion.2 = bf16[352,8,8,128]{3,1,2,0:T(8,128)(2,1)} fusion(bf16[512,2816]{0,1:T(8,128)(2,1)} %bitcast.256, bf16[512,1024]{1,0:T(8,128)(2,1)S(1)} %copy-done.25, f32[512]{0:T(512)S(1)} %get-tuple-element.138), kind=kOutput, calls=%fused_computation.14 | convolution fusion | flops 2957246464 | bytes 9701376 | tf_op jit(solution)/shard_map/dot_general | solution.py:63
  343.6 4.6 copy.201
  356.8 4.2 multiply_convert_fusion.1
  373.2 14.0 %reshape.734 = bf16[8,128,4,704]{3,2,1,0:T(4,128)(2,1)} reshape(bf16[1024,2816]{1,0:T(8,128)(2,1)} %convolution_convert_fusion.1) | data formatting | bytes 11534336 | tf_op jit(solution)/shard_map/reshape | solution.py:759
  387.2 6.7 copy.237
  393.8 14.4 %reshape.735 = bf16[8,128,4,704]{3,2,1,0:T(4,128)(2,1)} reshape(bf16[1024,2816]{1,0:T(8,128)(2,1)} %convolution_convert_fusion) | data formatting | bytes 11534336 | tf_op jit(solution)/shard_map/reshape | solution.py:759
  408.2 6.6 copy.239
  419.9 4.1 copy.249
  424.1 3.8 copy.222
  430.5 4.4 copy.197
  437.5 5.4 fusion.55
  444.6 6.7 fusion.9
  465.1 5.1 convolution_convert_fusion.4
  476.5 4.0 multiply_convert_fusion.10
  484.4 5.1 convolution_convert_fusion.5
  505.7 150.0 %scatter_grads.1 = (f32[128,256]{1,0:T(8,128)}, f32[128,256]{1,0:T(8,128)}, f32[128,256]{1,0:T(8,128)}, f32[128,256]{1,0:T(8,128)}, f32[256,128]{1,0:T(8,128)}, ...) custom-call(bf16[2,2,2,4,128,256]{5,4,3,2,1,0:T(8,128)(2,1)} %bitcast.238, ...), custom_call_target="tpu_custom_call" | custom-call | tf_op jit(solution)/shard_map/scatter_grads/pallas_call | solution.py:721
  (223 shorter events, 148.8 us)
Async XLA Ops:
  7.2 444.1 %all-gather.3.cloned.1.call-start = ((), (), s32[]{:S(2)}) async-start(), calls=%async_computation | async-start | bytes 1310720 | tf_op jit(solution)/shard_map/all_gather | solution.py:932
  201.3 6.5 copy-start.30
  232.3 9.2 %copy-start.16 = (f32[512,1024]{1,0:T(8,128)S(1)}, f32[512,1024]{1,0:T(8,128)}, u32[]{:S(2)}) copy-start(f32[512,1024]{1,0:T(8,128)} %get-tuple-element.43) | copy-start | bytes 6291460
  241.7 11.5 %copy-start.24 = (bf16[512,1024]{1,0:T(8,128)(2,1)S(1)}, bf16[512,1024]{1,0:T(8,128)(2,1)}, u32[]{:S(2)}) copy-start(bf16[512,1024]{1,0:T(8,128)(2,1)} %param.23) | copy-start | bytes 3145732
  262.5 7.9 %copy-start.31 = (bf16[512,2816]{1,0:T(8,128)(2,1)}, bf16[512,2816]{1,0:T(8,128)(2,1)S(1)}, u32[]{:S(2)}) copy-start(bf16[512,2816]{1,0:T(8,128)(2,1)S(1)} %get-tuple-element.123) | copy-start | bytes 8650756
  262.5 7.9 %copy-start.33 = (bf16[512,2816]{1,0:T(8,128)(2,1)}, bf16[512,2816]{1,0:T(8,128)(2,1)S(1)}, u32[]{:S(2)}) copy-start(bf16[512,2816]{1,0:T(8,128)(2,1)S(1)} %get-tuple-element.122) | copy-start | bytes 8650756
  262.5 7.9 %copy-start.19 = (bf16[8,4,128,704]{2,0,3,1:T(8,128)(2,1)S(1)}, bf16[8,4,128,704]{2,0,3,1:T(8,128)(2,1)}, u32[]{:S(2)}) copy-start(bf16[8,4,128,704]{2,0,3,1:T(8,128)(2,1)} %copy.170) | copy-start | bytes 17301508
  270.4 4.5 copy-start.46
  278.9 4.4 copy-start.4
  278.9 3.8 copy-start.17
  278.9 3.8 copy-start.42
  283.2 3.4 copy-start.7
  289.5 3.1 copy-start.6
  300.0 5.4 copy-start.1
  302.1 3.6 copy-start.34
  305.7 6.8 copy-start.32
  305.7 6.7 copy-start.60
  319.4 4.0 copy-start.27
  332.0 4.7 copy-start.25
  343.6 4.6 copy-start.5
  356.8 4.2 copy-start.11
  362.8 3.1 copy-start.10
  424.1 3.8 copy-start.36
  430.5 4.4 copy-start.35
  437.5 5.5 copy-start.3
  437.5 5.5 copy-start.18
  437.5 5.5 copy-start.20
  455.4 3.2 copy-start.28
  655.6 5.5 copy-start.29
  659.5 3.1 copy-start.50
  671.8 3.6 copy-start.54
  671.8 4.3 copy-start.53
  (30 other events, 66.5 us)
Sparse Core Ops, SparseCore 0:
  302.2 32.5 all-gather.2

commit v4 on v3

v4 whole, which is shorter than its diff:
```python
import jax
import jax.numpy as jnp
from jax import lax
from jax.experimental import pallas as pl
from jax.experimental.pallas import tpu as pltpu
from jax.sharding import PartitionSpec as P

HEAD_DIM = 128
SLOTS = 4

epsilon = 1e-06
head_floor = 1.0
AXES = ("fsdp", "tp")


def swish(values):
    return values * jax.nn.sigmoid(values)


def swish_slope(values):
    sigma = jax.nn.sigmoid(values)
    return sigma * (1.0 + values * (1.0 - sigma))


def rms_scale(values, offset=epsilon):
    return lax.rsqrt(jnp.mean(values * values, axis=-1, keepdims=True) + offset)


def norm_back(values, scale, grads):
    normed = values * scale
    return scale * (grads - normed * jnp.mean(grads * normed, axis=-1, keepdims=True))


def segment_of(places, ends):
    return jnp.sum((places[..., None] >= ends).astype(jnp.int32), axis=-1, dtype=jnp.int32)


def rotate(values, cos_table, sin_table):
    half = values.shape[-1] // 2
    front, back = values[..., :half], values[..., half:]
    return jnp.concatenate(
        [front * cos_table - back * sin_table, front * sin_table + back * cos_table], axis=-1
    )


def rotate_back(values, cos_table, sin_table):
    return rotate(values, cos_table, -sin_table)


def mm(left, right):
    return jnp.dot(left, right, preferred_element_type=jnp.float32)


def mm_trans(left, right):
    return lax.dot_general(
        left, right, (((1,), (1,)), ((), ())), preferred_element_type=jnp.float32
    )


def mm_inner(left, right):
    return lax.dot_general(
        left, right, (((0,), (0,)), ((), ())), preferred_element_type=jnp.float32
    )


def heads_dot(spec, left, right):
    return jnp.einsum(spec, left, right, preferred_element_type=jnp.float32)


def gather_full(shard, row_axis, column_axis):
    part = lax.all_gather(shard, "tp", axis=0 if row_axis == "tp" else 1, tiled=True)
    return lax.all_gather(part, "fsdp", axis=0 if row_axis == "fsdp" else 1, tiled=True)


def scatter_grad(grad, row_axis, column_axis):
    part = grad.astype(jnp.bfloat16)
    part = lax.psum_scatter(
        part, "fsdp", scatter_dimension=0 if row_axis == "fsdp" else 1, tiled=True
    )
    part = lax.psum_scatter(part, "tp", scatter_dimension=0 if row_axis == "tp" else 1, tiled=True)
    return part.astype(jnp.float32)


MESH = pl.DeviceIdType.MESH
VMEM_BYTES = 66_000_000


def place():
    f, t = lax.axis_index("fsdp"), lax.axis_index("tp")
    return f // 4, (f // 2) % 2, f % 2, f, t


def meet(peers):
    barrier = pltpu.get_barrier_semaphore()
    for peer in peers:
        pl.semaphore_signal(barrier, inc=1, device_id=peer, device_id_type=MESH)
    pl.semaphore_wait(barrier, len(peers))


def peers_of(f, t):
    core = (f // 2 * 2 + (1 - f % 2), t)
    along_x = (f // 4 * 4 + (f + 2) % 4, t)
    along_y = ((f + 4) % 8, t)
    along_z = [(f, (t + d) % 4) for d in (1, 2, 3)]
    return core, along_x, along_y, along_z


FAR = 1e7


def swish_of(values):
    return values * jax.nn.sigmoid(values)


def segment_at(where, ends):
    return sum((where >= end).astype(jnp.int32) for end in ends)


def row_tables(lengths_ref, t, rows):
    ends, total = [], jnp.int32(0)
    for j in range(SLOTS):
        total = total + lengths_ref[0, j]
        ends.append(total)
    first = t * rows
    offsets = lax.broadcasted_iota(jnp.int32, (rows, HEAD_DIM), 0)
    return ends, first, offsets, segment_at(first + offsets, ends)


def scalar_segment(where, ends):
    return sum(jnp.where(where >= end, 1, 0) for end in ends)


def fill_span(span_ref, ends, first):
    rows = span_ref.shape[0]
    band = 32

    def step(i, carry):
        row = first + i * band + lax.broadcasted_iota(jnp.int32, (band, rows), 0)
        column = first + lax.broadcasted_iota(jnp.int32, (band, rows), 1)
        allowed = (segment_at(row, ends) == segment_at(column, ends)) & (row >= column)
        span_ref[pl.ds(pl.multiple_of(i * band, band), band), :] = jnp.where(
            allowed, (row - column).astype(jnp.float32), FAR
        )
        return carry

    lax.fori_loop(0, rows // band, step, 0)


def turn(values, cos, sin):
    return values * cos + pltpu.roll(values, HEAD_DIM // 2, 1) * sin


def dot(left, right):
    return jnp.dot(left, right, preferred_element_type=jnp.float32)


def dot_nt(left, right):
    return lax.dot_general(left, right, (((1,), (1,)), ((), ())), preferred_element_type=jnp.float32)


def dot_tn(left, right):
    return lax.dot_general(left, right, (((0,), (0,)), ((), ())), preferred_element_type=jnp.float32)


ORDER = (1, 2, 0, 3, 4, 5, 6, 7)
N_W = 8
FWD_IN = ("tokens", "cos", "sin", "lengths", "rates")
FWD_OUT = (
    "result",
    "qp",
    "kp",
    "up",
    "q",
    "k",
    "v",
    "o",
    "w_turned",
    "y1",
    "n1_turned",
    "n2_turned",
    "g",
    "e",
    "states",
    "rates8",
)


def forward_kernel(*refs):
    shards, refs = refs[:N_W], refs[N_W:]
    inp = dict(zip(FWD_IN, refs))
    refs = refs[len(FWD_IN) :]
    kept, refs = refs[:N_W], refs[N_W:]
    a_out, refs = refs[0], refs[1:]
    out = dict(zip(FWD_OUT, refs))
    refs = refs[len(FWD_OUT) :]
    full, refs = refs[:N_W], refs[N_W:]
    buf = dict(zip(FWD_OUT, refs))
    refs = refs[len(FWD_OUT) :]
    n1, n2, mixed, hidden, hidden_turned, span, states, rate_tiles = refs[:8]
    own_sem, z_send, z_recv, n_send, n_recv, c_send, c_recv = refs[8:15]
    s_send, s_recv, r_send, r_recv, keep_sem, out_sem, turn_sem = refs[15:]
    rows = inp["tokens"].shape[0]
    y, x, c, f, t = place()
    core, along_x, along_y, along_z = peers_of(f, t)
    rate_tiles[t] = jnp.concatenate(
        [jnp.full((1, rows), inp["rates"][i % 2], jnp.float32) for i in range(8)], axis=0
    )
    meet([core, along_x, along_y, *along_z])
    pieces = [(w, h) for w in ORDER for h in range(2)]
    total = len(pieces)
    all_ = slice(None)

    def rows_of(piece):
        w, h = piece
        half = shards[w].shape[0] // 2
        return pl.ds(h * half, half)

    def slot(piece, *index):
        return full[piece[0]].at[(*index, rows_of(piece))]

    def remote(src, dst, send, recv, peer):
        return pltpu.make_async_remote_copy(
            src_ref=src, dst_ref=dst, send_sem=send, recv_sem=recv, device_id=peer, device_id_type=MESH
        )

    def own_copy(p):
        piece = pieces[p]
        return pltpu.make_async_copy(
            shards[piece[0]].at[rows_of(piece)], slot(piece, y, x, c, t), own_sem.at[p]
        )

    def z_copy(p, d, source):
        piece = pieces[p]
        return remote(
            shards[piece[0]].at[rows_of(piece)],
            slot(piece, y, x, c, source),
            z_send.at[p, d],
            z_recv.at[p, d],
            along_z[d],
        )

    def near_copy(p, stage, arriving):
        piece = pieces[p]
        over_x = (piece[1] == 0) == (stage == 0)
        if stage == 0:
            index = (y, x, c)
            if arriving:
                index = (y, 1 - x, c) if over_x else (1 - y, x, c)
        else:
            if over_x:
                index = (all_, (1 - x) if arriving else x, c)
            else:
                index = ((1 - y) if arriving else y, all_, c)
        ref = slot(piece, *index, all_)
        return remote(
            ref, ref, n_send.at[p, stage], n_recv.at[p, stage], along_x if over_x else along_y
        )

    def core_copy(p, part, arriving):
        piece = pieces[p]
        side = (1 - c) if arriving else c
        first_x = piece[1] == 0
        index = (
            (y, x, side),
            (y, 1 - x, side) if first_x else (1 - y, x, side),
            (1 - y, all_, side) if first_x else (all_, 1 - x, side),
        )[part]
        ref = slot(piece, *index, all_)
        return remote(ref, ref, c_send.at[p, part], c_recv.at[p, part], core)

    def start_z(p):
        own_copy(p).start()
        for d in range(3):
            z_copy(p, d, t).start()

    def arrived(w):
        for h in range(2):
            for part in range(3):
                core_copy(pieces.index((w, h)), part, True).wait_recv()
        keep(w).start()

    def keep(w):
        return pltpu.make_async_copy(full[w], kept[w], keep_sem.at[w])

    def save(name):
        return pltpu.make_async_copy(buf[name], out[name], out_sem.at[FWD_OUT.index(name)])

    def rate_copy(d, source):
        ref = rate_tiles.at[source]
        return remote(ref, ref, r_send.at[d], r_recv.at[d], along_z[d])

    def state_copy(d, source):
        ref = states.at[source]
        return remote(ref, ref, s_send.at[d], s_recv.at[d], along_z[d])

    ends, first, offsets, segments = row_tables(inp["lengths"], t, rows)
    steps_f = offsets.astype(jnp.float32)

    def head_columns(i, j):
        return pl.ds(pl.multiple_of(i * 2 * HEAD_DIM + j * HEAD_DIM, HEAD_DIM), HEAD_DIM)

    def rate_of(h):
        return buf["rates8"][pl.ds(h, 1), :]

    def turn_rows(source, target):
        for j in range(8):
            part = source[:, j * HEAD_DIM : (j + 1) * HEAD_DIM]
            target[j % 2, j // 2 * HEAD_DIM : (j // 2 + 1) * HEAD_DIM] = part.T

    def begin():
        for d in range(3):
            rate_copy(d, t).start()
        values = inp["tokens"][...].astype(jnp.float32)
        n1[...] = (values * rms_scale(values)).astype(jnp.bfloat16)
        turn_rows(n1, buf["n1_turned"])
        save("n1_turned").start()
        fill_span(span, ends, first)

    def rates_here():
        for d in range(3):
            rate_copy(d, (t + 3 - d) % 4).wait_recv()
        for j in range(4):
            buf["rates8"][2 * j : 2 * j + 2] = rate_tiles[j, 0:2]
        save("rates8").start()

    def project(w, finish):
        def run():
            arrived(w)

            def block(i, carry):
                columns = full[w][:, :, :, i].reshape(n1.shape[1], full[w].shape[5])
                values = dot(n1[...], columns)
                for j in range(2):
                    finish(i, j, values[:, j * HEAD_DIM : (j + 1) * HEAD_DIM])
                return carry

            lax.fori_loop(0, 4, block, 0)

        return run

    def finish_key(i, j, values):
        lanes = slice(j * HEAD_DIM, (j + 1) * HEAD_DIM)
        buf["kp"][i, :, lanes] = values.astype(jnp.bfloat16)
        buf["k"][i, :, lanes] = turn(swish_of(values), inp["cos"][...], inp["sin"][...]).astype(jnp.bfloat16)

    def finish_query(i, j, values):
        lanes = slice(j * HEAD_DIM, (j + 1) * HEAD_DIM)
        buf["qp"][i, :, lanes] = values.astype(jnp.bfloat16)
        buf["q"][i, :, lanes] = turn(swish_of(values), inp["cos"][...], inp["sin"][...]).astype(jnp.bfloat16)

    def finish_value(i, j, values):
        lanes = slice(j * HEAD_DIM, (j + 1) * HEAD_DIM)
        buf["v"][i, :, lanes] = values.astype(jnp.bfloat16)

    def finish_update(i, j, values):
        lanes = slice(j * HEAD_DIM, (j + 1) * HEAD_DIM)
        buf["up"][i, :, lanes] = values.astype(jnp.bfloat16)
        buf["y1"][:, head_columns(i, j)] = swish_of(values)

    def make_states():
        last = scalar_segment(first + rows - 1, ends)

        def pair(i, carry):
            for j in range(2):
                h, lanes = 2 * i + j, slice(j * HEAD_DIM, (j + 1) * HEAD_DIM)
                rate = rate_of(h)[:, :HEAD_DIM]
                to_end = jnp.where(segments == last, jnp.exp(-(rows - 1.0 - steps_f) * rate), 0.0)
                scaled = (buf["k"][i, :, lanes].astype(jnp.float32) * to_end).astype(jnp.bfloat16)
                states[t, h] = dot_tn(scaled, buf["v"][i, :, lanes]).astype(jnp.bfloat16)
            return carry

        lax.fori_loop(0, 4, pair, 0)
        for name in ("k", "v", "kp"):
            save(name).start()

    def send_states():
        for d in range(3):
            state_copy(d, t).start()

    def sum_states():
        for d in range(3):
            state_copy(d, (t + 3 - d) % 4).wait_recv()
        before = scalar_segment(first - 1, ends)

        def head(h, carry):
            rate = rate_of(h)[:, :HEAD_DIM]
            result = jnp.zeros((HEAD_DIM, HEAD_DIM), jnp.float32)
            for j in range(3):
                reach = jnp.where(
                    (j < t) & (scalar_segment(j * rows + rows - 1, ends) == before), 1.0, 0.0
                )
                distance = jnp.maximum(t - j - 1, 0).astype(jnp.float32) * rows
                weight = reach * jnp.exp(-rate * distance)
                result = result + weight * states[j, h].astype(jnp.float32)
            buf["states"][h] = result.astype(jnp.bfloat16)
            return carry

        lax.fori_loop(0, 8, head, 0)
        save("states").start()
        for name in ("q", "qp", "up"):
            save(name).start()

    def attend(i):
        before = scalar_segment(first - 1, ends)
        half = rows // 2

        def go():
            for j in range(2):
                h, lanes = 2 * i + j, slice(j * HEAD_DIM, (j + 1) * HEAD_DIM)
                rate = rate_of(h)
                for b in range(2):
                    mine = slice(b * half, (b + 1) * half)
                    keys = (b + 1) * half
                    query = buf["q"][i, mine, lanes]
                    scores = dot_nt(query, buf["k"][i, :keys, lanes])
                    decay = jnp.exp(-span[mine, :keys] * rate[:, :keys])
                    weights = (scores * decay).astype(jnp.bfloat16)
                    into = jnp.where(
                        segments[mine] == before,
                        jnp.exp(-(steps_f[mine] + 1.0) * rate[:, :HEAD_DIM]),
                        0.0,
                    )
                    attn = dot(weights, buf["v"][i, :keys, lanes]) + into * dot(
                        query, buf["states"][h]
                    )
                    columns = head_columns(i, j)
                    buf["o"][mine, columns] = attn
                    normed = attn * rms_scale(attn, head_floor)
                    mixed[mine, columns] = (normed * buf["y1"][mine, columns]).astype(jnp.bfloat16)

        return go

    def attend_pairs(lo, hi):
        def step(i, carry):
            attend(i)()
            return carry

        return lambda: (lax.fori_loop(lo, hi, step, 0), None)[1]

    def mix():
        save("o").start()
        for i in range(4):
            columns = slice(i * 2 * HEAD_DIM, (i + 1) * 2 * HEAD_DIM)
            buf["w_turned"][i] = mixed[:, columns].T
        save("w_turned").start()
        arrived(4)

        def block(i, carry):
            sides = [full[4][i // 2, i % 2, s].reshape(n1.shape[1], HEAD_DIM) for s in range(2)]
            columns = pl.ds(pl.multiple_of(i * 2 * HEAD_DIM, 2 * HEAD_DIM), 2 * HEAD_DIM)
            buf["y1"][:, columns] = inp["tokens"][:, columns].astype(jnp.float32) + dot(
                mixed[...], jnp.concatenate(sides, axis=1)
            )
            return carry

        lax.fori_loop(0, 4, block, 0)
        values = buf["y1"][...]
        n2[...] = (values * rms_scale(values)).astype(jnp.bfloat16)
        turn_rows(n2, buf["n2_turned"])
        save("y1").start()
        save("n2_turned").start()

    def turned_out(i):
        return pltpu.make_async_copy(hidden_turned.at[i % 2], a_out.at[i], turn_sem.at[i])

    def gate_up(i):
        def go():
            if i == 0:
                arrived(6)
            shape = (n1.shape[1], full[5].shape[5])
            for b in range(2):
                mine = slice(b * rows // 2, (b + 1) * rows // 2)
                gate = dot(n2[mine], full[5][:, :, :, i].reshape(shape))
                lift = dot(n2[mine], full[6][:, :, :, i].reshape(shape))
                hidden[i, mine] = (gate * lift).astype(jnp.bfloat16)
                buf["g"][i, mine] = gate.astype(jnp.bfloat16)
                buf["e"][i, mine] = lift.astype(jnp.bfloat16)
            if i >= 2:
                turned_out(i - 2).wait()
            hidden_turned[i % 2] = hidden[i].T
            turned_out(i).start()
            if i == 3:
                for name in ("g", "e"):
                    save(name).start()

        return go

    def close():
        arrived(7)

        def block(i, carry):
            columns = pl.ds(pl.multiple_of(i * 2 * HEAD_DIM, 2 * HEAD_DIM), 2 * HEAD_DIM)
            values = buf["y1"][:, columns]
            for j in range(4):
                sides = [full[7][i // 2, i % 2, s, j] for s in range(2)]
                values = values + dot(hidden[j], jnp.concatenate(sides, axis=1))
            buf["result"][:, columns] = values.astype(jnp.bfloat16)
            return carry

        lax.fori_loop(0, 4, block, 0)
        save("result").start()

    lead, lag = 4, 2

    def ready(w):
        return 2 * ORDER.index(w) + 1 + 2 * lag + 1

    work = [
        (0, begin),
        (4, rates_here),
        (ready(1), project(1, finish_key)),
        (ready(2), project(2, finish_value)),
        (ready(2), make_states),
        (ready(0), send_states),
        (ready(0), project(0, finish_query)),
        (ready(3), project(3, finish_update)),
        (ready(3), sum_states),
        *[(ready(3), attend_pairs(i, i + 1)) for i in range(4)],
        (ready(4), mix),
        (ready(5), lambda: arrived(5)),
        *[(ready(6), gate_up(i)) for i in range(4)],
        (ready(7), close),
    ]

    def some_work(step):
        if work and work[0][0] <= step:
            work.pop(0)[1]()

    for p in range(min(lead, total)):
        start_z(p)
    some_work(0)
    for step in range(total + 2 * lag):
        if lead <= step + lead < total:
            start_z(step + lead)
        p = step
        if p < total:
            own_copy(p).wait()
            for d in range(3):
                z_copy(p, d, (t + 3 - d) % 4).wait_recv()
            near_copy(p, 0, False).start()
            core_copy(p, 0, False).start()
            some_work(step)
        p = step - lag
        if 0 <= p < total:
            near_copy(p, 0, True).wait_recv()
            near_copy(p, 1, False).start()
            core_copy(p, 1, False).start()
            some_work(step)
        p = step - 2 * lag
        if 0 <= p < total:
            near_copy(p, 1, True).wait_recv()
            core_copy(p, 2, False).start()
            some_work(step)
    while work:
        work.pop(0)[1]()
    for d in range(3):
        rate_copy(d, t).wait_send()
        state_copy(d, t).wait_send()
    for p in range(total):
        for d in range(3):
            z_copy(p, d, t).wait_send()
        for stage in range(2):
            near_copy(p, stage, False).wait_send()
        for part in range(3):
            core_copy(p, part, False).wait_send()
    for w in range(N_W):
        keep(w).wait()
    for name in FWD_OUT:
        save(name).wait()
    for i in range(2, 4):
        turned_out(i).wait()


def forward(shards, tokens, cos, sin, lengths, rates):
    rows, width = tokens.shape
    units = shards[5].shape[1]
    heads = width // HEAD_DIM
    low, wide = jnp.bfloat16, jnp.float32
    by_pair = (4, rows, heads // 4 * HEAD_DIM)
    turned = (2, width // 2, rows)
    by_unit = (4, rows, units)
    shapes = {
        "result": ((rows, width), low),
        "qp": (by_pair, low),
        "kp": (by_pair, low),
        "up": (by_pair, low),
        "q": (by_pair, low),
        "k": (by_pair, low),
        "v": (by_pair, low),
        "o": ((rows, width), wide),
        "w_turned": ((4, width // 4, rows), low),
        "y1": ((rows, width), wide),
        "n1_turned": (turned, low),
        "n2_turned": (turned, low),
        "g": (by_unit, low),
        "e": (by_unit, low),
        "states": ((heads, HEAD_DIM, HEAD_DIM), low),
        "rates8": ((8, rows), wide),
    }
    blocks = [(2, 2, 2, 4, *s.shape) for s in shards]
    pieces = 2 * N_W
    dma = pltpu.SemaphoreType.DMA
    in_vmem, in_smem = (pl.BlockSpec(memory_space=m) for m in (pltpu.VMEM, pltpu.SMEM))
    outs = pl.pallas_call(
        forward_kernel,
        name="gather_and_forward",
        out_shape=[jax.ShapeDtypeStruct(b, low) for b in blocks]
        + [jax.ShapeDtypeStruct((4, units, rows), low)]
        + [jax.ShapeDtypeStruct(*shapes[name]) for name in FWD_OUT],
        in_specs=[in_vmem] * (N_W + 3) + [in_smem] * 2,
        out_specs=[pl.BlockSpec(memory_space=pl.ANY)] * (N_W + 1 + len(FWD_OUT)),
        scratch_shapes=[
            *[pltpu.VMEM(b, low) for b in blocks],
            *[pltpu.VMEM(*shapes[name]) for name in FWD_OUT],
            pltpu.VMEM((rows, width), low),
            pltpu.VMEM((rows, width), low),
            pltpu.VMEM((rows, width), low),
            pltpu.VMEM(by_unit, low),
            pltpu.VMEM((2, units, rows), low),
            pltpu.VMEM((rows, rows), wide),
            pltpu.VMEM((4, heads, HEAD_DIM, HEAD_DIM), low),
            pltpu.VMEM((4, 8, rows), wide),
            dma((pieces,)),
            dma((pieces, 3)),
            dma((pieces, 3)),
            dma((pieces, 2)),
            dma((pieces, 2)),
            dma((pieces, 3)),
            dma((pieces, 3)),
            dma((3,)),
            dma((3,)),
            dma((3,)),
            dma((3,)),
            dma((N_W,)),
            dma((len(FWD_OUT),)),
            dma((4,)),
        ],
        compiler_params=pltpu.CompilerParams(
            collective_id=0, has_side_effects=True, vmem_limit_bytes=VMEM_BYTES
        ),
    )(*shards, tokens, cos, sin, lengths, rates)
    return outs[:N_W], outs[N_W], dict(zip(FWD_OUT, outs[N_W + 1 :]))


BWD_ANY = ("q", "k", "v", "up", "qp", "kp", "o", "w_turned", "y1", "n1_turned", "n2_turned", "g", "e")
BWD_VMEM = ("states", "rates8", "cos", "sin")
BAND = 32
LINK = 42_000.0


def slope_of(values):
    sigma = jax.nn.sigmoid(values)
    return sigma * (1.0 + values * (1.0 - sigma))


def turn_back(values, cos, sin):
    return values * cos - pltpu.roll(values, HEAD_DIM // 2, 1) * sin


def backward_kernel(*refs):
    kept, refs = refs[:N_W], refs[N_W:]
    a_in, refs = refs[0], refs[1:]
    inp = dict(zip(BWD_ANY + BWD_VMEM, refs))
    refs = refs[len(BWD_ANY + BWD_VMEM) :]
    tokens, out_grad, lengths = refs[:3]
    grads, d_tokens = refs[3 : 3 + N_W], refs[3 + N_W]
    refs = refs[4 + N_W :]
    mine, from_near, from_far, from_z = (refs[i * N_W : (i + 1) * N_W] for i in range(4))
    refs = refs[4 * N_W :]
    tall, wide, turned_a, gq, ev, d_side, n_turned, rows_a, rows_b, tall_w, wide_w = refs[:11]
    q_pre, w_turned, span, states, back = refs[11:16]
    load_sem, tall_sem, wide_sem, c_send, c_recv, n_send, n_recv, z_send, z_recv = refs[16:25]
    s_send, s_recv = refs[25:]
    rows, width = rows_a.shape
    half = rows // 2
    y, x, c, f, t = place()
    core, along_x, along_y, along_z = peers_of(f, t)
    all_ = slice(None)
    side = {"theirs": 1 - c, "mine": c}

    keys = {}

    def load(key, source, target):
        index = keys.setdefault(key, len(keys))
        return pltpu.make_async_copy(source, target, load_sem.at[index])

    def pair_columns(i):
        return slice(i * 2 * HEAD_DIM, (i + 1) * 2 * HEAD_DIM)

    def by_pairs(key, source, place_):
        return [load((key, i), source.at[:, pair_columns(i)], q_pre.at[place_, i]) for i in range(4)]

    lane_pair = [slice(0, 2 * HEAD_DIM), slice(2 * HEAD_DIM, 4 * HEAD_DIM)]
    loads = {
        "cot": by_pairs("cot", out_grad, 0),
        "tokens": by_pairs("tokens", tokens, 0),
        "a": [load("a", a_in, turned_a)],
        "g": [load("g", inp["g"], gq)],
        "e": [load("e", inp["e"], ev)],
        "n2": [load("n2", inp["n2_turned"], n_turned)],
        "n1": [load("n1", inp["n1_turned"], n_turned)],
        "y1": [load("y1", inp["y1"], rows_a)],
        "o": [load("o", inp["o"], rows_a)],
        "w": [load("w", inp["w_turned"], w_turned)],
        "qp": [load("qp", inp["qp"], q_pre.at[0])],
        "kp": [load("kp", inp["kp"], q_pre.at[1])],
        "q": [load("q", inp["q"], gq.at[:, :, lane_pair[0]])],
        "k": [load("k", inp["k"], gq.at[:, :, lane_pair[1]])],
        "v": [load("v", inp["v"], ev.at[:, :, lane_pair[0]])],
        "up": [load("up", inp["up"], turned_a.at[:, :rows, lane_pair[1]])],
        "out": [load("out", rows_b, d_tokens)],
    }

    def start(*names):
        for name in names:
            for copy in loads[name]:
                copy.start()

    def wait(*names):
        for name in names:
            for copy in loads[name]:
                copy.wait()

    def tile(w, i, slot):
        if w in (4, 7):
            depth = kept[w].shape[4]
            return pltpu.make_async_copy(
                kept[w].at[:, :, :, i], tall_w.at[slot, :, :, :, :depth], tall_sem.at[slot]
            )
        lanes = kept[w].shape[5]
        return pltpu.make_async_copy(
            kept[w].at[:, :, :, i], wide_w.at[slot, :, :, :, :, :lanes], wide_sem.at[slot]
        )

    def over_tiles(w, use):
        tile(w, 0, 0).start()

        def step(i, carry):
            slot = lax.rem(i, 2)

            @pl.when(i < 3)
            def _():
                tile(w, i + 1, 1 - slot).start()

            tile(w, i, slot).wait()
            use(i, slot)
            return carry

        lax.fori_loop(0, 4, step, 0)

    pieces = [(w, h) for w in range(N_W) for h in range(2)]

    def remote(src, dst, send, recv, peer):
        return pltpu.make_async_remote_copy(
            src_ref=src, dst_ref=dst, send_sem=send, recv_sem=recv, device_id=peer, device_id_type=MESH
        )

    def rows_of(p):
        w, h = pieces[p]
        part = grads[w].shape[0] // 2
        return pl.ds(h * part, part)

    def ring_of(w):
        return (tall, 0) if w in (4, 7) else (wide, 1)

    def core_copy(w, i):
        ring, kind = ring_of(w)
        depth, lanes = grads[w].shape
        return remote(
            ring.at[lax.rem(i, 2), :, :, :depth, :lanes],
            mine[w].at[:, :, i],
            c_send.at[kind, lax.rem(i, 2)],
            c_recv.at[w, i],
            core,
        )

    def near_copy(p):
        (w, h), part = pieces[p], rows_of(p)
        src = mine[w].at[1 - y, :, :, part] if h == 0 else mine[w].at[:, 1 - x, :, part]
        return remote(
            src,
            from_near[w].at[:, :, part],
            n_send.at[p, 0],
            n_recv.at[p, 0],
            along_y if h == 0 else along_x,
        )

    def far_copy(p):
        (w, h), part = pieces[p], rows_of(p)
        src = mine[w].at[y, 1 - x, :, part] if h == 0 else mine[w].at[1 - y, x, :, part]
        return remote(
            src,
            from_far[w].at[:, part],
            n_send.at[p, 1],
            n_recv.at[p, 1],
            along_x if h == 0 else along_y,
        )

    def z_copy(p, d):
        w, part = pieces[p][0], rows_of(p)
        return remote(
            mine[w].at[y, x, (t + d + 1) % 4, part],
            from_z[w].at[d, part],
            z_send.at[p, d],
            z_recv.at[p, d],
            along_z[d],
        )

    def add(steps, target, other):
        def step(i, carry):
            into, term = target(i), other(i)
            into[...] = (into[...].astype(jnp.float32) + term[...].astype(jnp.float32)).astype(
                jnp.bfloat16
            )
            return carry

        lax.fori_loop(0, steps, step, 0)

    def after_near(p):
        (w, h), part = pieces[p], rows_of(p)
        near_copy(p).wait_recv()
        if h == 0:
            into = lambda i: mine[w].at[y, i // 4, i % 4, part]
        else:
            into = lambda i: mine[w].at[i // 4, x, i % 4, part]
        add(8, into, lambda i: from_near[w].at[i // 4, i % 4, part])
        far_copy(p).start()

    def after_far(p):
        w, part = pieces[p][0], rows_of(p)
        far_copy(p).wait_recv()
        add(4, lambda i: mine[w].at[y, x, i, part], lambda i: from_far[w].at[i, part])
        for d in range(3):
            z_copy(p, d).start()

    def after_z(p):
        w, part = pieces[p][0], rows_of(p)
        for d in range(3):
            z_copy(p, d).wait_recv()
        result = mine[w][y, x, t, part].astype(jnp.float32)
        for d in range(3):
            result = result + from_z[w][d, part].astype(jnp.float32)
        grads[w][part] = result

    used = {0: None, 1: None}

    def gradient(w, whose, value):
        ring, kind = ring_of(w)
        depth, lanes = grads[w].shape

        def blocks(result):
            if kind == 1:
                return [(j // 2, j % 2, result[j * depth : (j + 1) * depth]) for j in range(4)]
            return [(j // 2, j % 2, result[:, j * lanes : (j + 1) * lanes]) for j in range(4)]

        def run():
            if whose == "theirs":
                before = used[kind]
                used[kind] = w

                def step(i, carry):
                    if before is not None:

                        @pl.when(i < 2)
                        def _():
                            core_copy(before, i + 2).wait_send()

                    @pl.when(i >= 2)
                    def _():
                        core_copy(w, i - 2).wait_send()

                    slot = lax.rem(i, 2)
                    result = value(i, side[whose]).astype(jnp.bfloat16)
                    for a, b, part in blocks(result):
                        ring[slot, a, b, :depth, :lanes] = part
                    core_copy(w, i).start()
                    return carry

                lax.fori_loop(0, 4, step, 0)
            else:

                def step(i, carry):
                    core_copy(w, i).wait_recv()
                    result = value(i, side[whose])
                    for a, b, part in blocks(result):
                        mine[w][a, b, i] = (mine[w][a, b, i].astype(jnp.float32) + part).astype(
                            jnp.bfloat16
                        )
                    return carry

                lax.fori_loop(0, 4, step, 0)
                for h in range(2):
                    near_copy(2 * w + h).start()

        return run

    ends, first, offsets, segments = row_tables(lengths, t, rows)
    steps_f = offsets.astype(jnp.float32)
    seg_before = scalar_segment(first - 1, ends)
    seg_after = scalar_segment(first + rows, ends)
    seg_first = scalar_segment(first, ends)

    def lanes_of(j, base=0):
        return slice(base + j * HEAD_DIM, base + (j + 1) * HEAD_DIM)

    def rate_of(h):
        return inp["rates8"][pl.ds(h, 1), :]

    def over_rows(use):
        def step(i, carry):
            use(pl.ds(pl.multiple_of(i * BAND, BAND), BAND))
            return carry

        lax.fori_loop(0, rows // BAND, step, 0)

    def begin():
        start("cot", "a", "e", "g", "n2", "y1", "w")
        fill_span(span, ends, first)
        live = jnp.where(segments < SLOTS - 1, 1.0, 0.0)
        wait("cot")
        for i in range(4):
            for s in range(2):
                part = q_pre[0, i, :, lanes_of(s)].astype(jnp.float32) * live
                d_side[s, :, lanes_of(i)] = part.astype(jnp.bfloat16)
        start("qp", "kp")
        wait("a")

    def expand():
        wait("e", "g")

        def use(i, slot):
            for b in range(2):
                part = slice(b * half, (b + 1) * half)
                d_hidden = sum(
                    dot_nt(
                        d_side[s, part],
                        jnp.concatenate([tall_w[slot, j // 2, j % 2, s] for j in range(4)], axis=1),
                    )
                    for s in range(2)
                )
                lift, gate = ev[i, part].astype(jnp.float32), gq[i, part].astype(jnp.float32)
                ev[i, part] = (d_hidden * lift).astype(jnp.bfloat16)
                gq[i, part] = (d_hidden * gate).astype(jnp.bfloat16)

        over_tiles(7, use)
        wait("n2")

    def through(w, source, target, clear):
        def run():
            if clear:
                target[...] = jnp.zeros_like(target)
            lanes = kept[w].shape[5]

            def use(i, slot):
                for j in range(4):
                    part = wide_w[slot, j // 2, j % 2, :, :, :lanes].reshape(2 * HEAD_DIM, lanes)
                    target[:, pair_columns(j)] += dot_nt(source(i), part)

            over_tiles(w, use)

        return run

    def middle_back():
        start("v", "q", "k")
        wait("y1")

        def use(part):
            values = rows_a[part, :]
            cot = jnp.concatenate(
                [d_side[j % 2, part, lanes_of(j // 2)].astype(jnp.float32) for j in range(8)], axis=1
            )
            result = cot + norm_back(values, rms_scale(values), rows_b[part, :])
            rows_b[part, :] = result
            for j in range(8):
                d_side[j % 2, part, lanes_of(j // 2)] = result[:, lanes_of(j)].astype(jnp.bfloat16)

        over_rows(use)
        start("o")
        wait("w")

    def mixed_back():
        wait("o", "up")

        def use(i, slot):
            d_mixed = sum(
                dot_nt(
                    d_side[s],
                    jnp.concatenate(
                        [tall_w[slot, j // 2, j % 2, s, : 2 * HEAD_DIM] for j in range(4)], axis=1
                    ),
                )
                for s in range(2)
            )
            for j in range(2):
                columns = pl.ds(pl.multiple_of((2 * i + j) * HEAD_DIM, HEAD_DIM), HEAD_DIM)
                attn = rows_a[:, columns]
                scale = rms_scale(attn, head_floor)
                normed = attn * scale
                pre = turned_a[i, :rows, lanes_of(j, 2 * HEAD_DIM)].astype(jnp.float32)
                part = d_mixed[:, lanes_of(j)]
                turned_a[i, :rows, lanes_of(j)] = (part * normed * slope_of(pre)).astype(jnp.bfloat16)
                d_attn = norm_back(attn, scale, part * swish_of(pre))
                ev[i, :, lanes_of(j, 2 * HEAD_DIM)] = d_attn.astype(jnp.bfloat16)

        over_tiles(4, use)
        wait("n1", "q")

    def make_states():
        def pair(i, carry):
            for j in range(2):
                rate = rate_of(2 * i + j)[:, :HEAD_DIM]
                from_start = jnp.where(segments == seg_first, jnp.exp(-steps_f * rate), 0.0)
                scaled = (gq[i, :, lanes_of(j)].astype(jnp.float32) * from_start).astype(jnp.bfloat16)
                states[t, 2 * i + j] = dot_tn(scaled, ev[i, :, lanes_of(j, 2 * HEAD_DIM)]).astype(
                    jnp.bfloat16
                )
            return carry

        lax.fori_loop(0, 4, pair, 0)

    def state_copy(d, source):
        ref = states.at[source]
        return remote(ref, ref, s_send.at[d], s_recv.at[d], along_z[d])

    def send_states():
        for d in range(3):
            state_copy(d, t).start()

    def sum_states():
        wait("v", "k", "qp", "kp")
        for d in range(3):
            state_copy(d, (t + 3 - d) % 4).wait_recv()

        def head(h, carry):
            rate = rate_of(h)[:, :HEAD_DIM]
            result = jnp.zeros((HEAD_DIM, HEAD_DIM), jnp.float32)
            for j in range(1, 4):
                reach = jnp.where((j > t) & (scalar_segment(j * rows, ends) == seg_after), 1.0, 0.0)
                distance = jnp.maximum(j - t - 1, 0).astype(jnp.float32) * rows
                weight = reach * jnp.exp(-rate * distance)
                result = result + weight * states[j, h].astype(jnp.float32)
            back[h] = result.astype(jnp.bfloat16)
            return carry

        lax.fori_loop(0, 8, head, 0)

    def attend_back(h, carry):
        cos, sin = inp["cos"][...], inp["sin"][...]
        i, j = h // 2, lax.rem(h, 2)
        low_lanes = pl.ds(pl.multiple_of(j * HEAD_DIM, HEAD_DIM), HEAD_DIM)
        high_lanes = pl.ds(pl.multiple_of((2 + j) * HEAD_DIM, HEAD_DIM), HEAD_DIM)
        rate = rate_of(h)
        short = rate[:, :HEAD_DIM]
        key, value = gq[i, :, high_lanes], ev[i, :, low_lanes]
        state_in, state_back = inp["states"][h], back[h]
        out_of = jnp.where(segments == seg_after, jnp.exp(-(rows - steps_f) * short), 0.0)
        d_value = out_of * dot(key, state_back)
        d_key = out_of * dot_nt(value, state_back)
        d_query = []
        for b in range(2):
            part = slice(b * half, (b + 1) * half)
            keys = (b + 1) * half
            query = gq[i, part, low_lanes]
            grad = ev[i, part, high_lanes]
            decay = jnp.exp(-span[part, :keys] * rate[:, :keys])
            weights = (dot_nt(query, key[:keys]) * decay).astype(jnp.bfloat16)
            d_raw = (dot_nt(grad, value[:keys]) * decay).astype(jnp.bfloat16)
            into = jnp.where(
                segments[part] == seg_before, jnp.exp(-(steps_f[part] + 1.0) * short), 0.0
            )
            d_query.append(dot(d_raw, key[:keys]) + into * dot_nt(grad, state_in))
            add_value, add_key = dot_tn(weights, grad), dot_tn(d_raw, query)
            if b == 0:
                d_value = jnp.concatenate([d_value[:half] + add_value, d_value[half:]], axis=0)
                d_key = jnp.concatenate([d_key[:half] + add_key, d_key[half:]], axis=0)
            else:
                d_value, d_key = d_value + add_value, d_key + add_key
        d_query = jnp.concatenate(d_query, axis=0)
        pre_query = q_pre[0, i, :, low_lanes].astype(jnp.float32)
        pre_key = q_pre[1, i, :, low_lanes].astype(jnp.float32)
        gq[i, :, low_lanes] = (slope_of(pre_query) * turn_back(d_query, cos, sin)).astype(
            jnp.bfloat16
        )
        gq[i, :, high_lanes] = (
            slope_of(pre_key) * turn_back(d_key, cos, sin)
        ).astype(jnp.bfloat16)
        ev[i, :, low_lanes] = d_value.astype(jnp.bfloat16)
        return carry

    def close():
        wait("tokens")

        def use(part):
            values = jnp.concatenate([q_pre[0, i, part, :] for i in range(4)], axis=1)
            values = values.astype(jnp.float32)
            rows_b[part, :] += norm_back(values, rms_scale(values), rows_a[part, :])

        over_rows(use)
        start("out")

    low_pair, high_pair = slice(0, 2 * HEAD_DIM), slice(2 * HEAD_DIM, 4 * HEAD_DIM)
    sources = {
        0: lambda i: gq[i, :, low_pair],
        1: lambda i: gq[i, :, high_pair],
        2: lambda i: ev[i, :, low_pair],
        3: lambda i: turned_a[i, :rows, low_pair],
        5: lambda i: ev[i],
        6: lambda i: gq[i],
    }

    def grad(w, whose):
        if w == 7:
            value = lambda i, s: dot(turned_a[i], d_side[s])
        elif w == 4:
            value = lambda i, s: dot(w_turned[i], d_side[s])
        else:
            value = lambda i, s: dot(n_turned[s], sources[w](i))
        return gradient(w, whose, value)

    def attend_pairs(lo, hi):
        return lambda: (lax.fori_loop(2 * lo, 2 * hi, attend_back, 0), None)[1]

    work = [
        (3.0, begin, None),
        (2.5, grad(7, "theirs"), None),
        (6.0, expand, None),
        (2.5, grad(5, "theirs"), None),
        (3.0, grad(7, "mine"), 7),
        (0.1, lambda: start("up"), None),
        (2.5, grad(6, "theirs"), None),
        (3.0, grad(5, "mine"), 5),
        (3.0, grad(6, "mine"), 6),
        (0.1, lambda: start("n1"), None),
        (5.0, through(5, sources[5], rows_b, True), None),
        (5.0, through(6, sources[6], rows_b, False), None),
        (3.0, middle_back, None),
        (1.0, grad(4, "theirs"), None),
        (6.0, mixed_back, None),
        (1.0, grad(3, "theirs"), None),
        (1.2, grad(4, "mine"), 4),
        (2.0, make_states, None),
        (1.2, grad(3, "mine"), 3),
        (0.1, send_states, None),
        (2.0, through(3, sources[3], rows_a, True), None),
        (1.0, sum_states, None),
        (4.0, attend_pairs(0, 1), None),
        (4.0, attend_pairs(1, 2), None),
        (4.0, attend_pairs(2, 3), None),
        (4.0, attend_pairs(3, 4), None),
        (1.0, grad(2, "theirs"), None),
        (1.0, grad(0, "theirs"), None),
        (1.0, grad(1, "theirs"), None),
        (1.2, grad(2, "mine"), 2),
        (1.2, grad(0, "mine"), 0),
        (1.2, grad(1, "mine"), 1),
        (0.1, lambda: start("tokens"), None),
        (2.0, through(2, sources[2], rows_a, False), None),
        (2.0, through(0, sources[0], rows_a, False), None),
        (2.0, through(1, sources[1], rows_a, False), None),
        (2.0, close, None),
    ]
    meet([core, along_x, along_y, *along_z])
    clock, free, events = 0.0, {"x": 0.0, "y": 0.0, "z": 0.0}, []

    def expect(link, blocks, p, step):
        size = blocks * grads[pieces[p][0]].size // 2 * 2
        free[link] = max(free[link], clock) + size / LINK
        events.append((free[link] + 2.0, step, p))

    while work or events:
        events.sort(key=lambda event: event[0])
        if events and (not work or events[0][0] <= clock):
            due, step, p = events.pop(0)
            clock = max(clock, due) + 0.3
            h = pieces[p][1]
            if step == "near":
                after_near(p)
                expect("x" if h == 0 else "y", 4, p, "far")
            elif step == "far":
                after_far(p)
                expect("z", 4, p, "z")
            else:
                after_z(p)
        else:
            time_, run, done = work.pop(0)
            run()
            clock += time_
            if done is not None:
                for h in range(2):
                    expect("y" if h == 0 else "x", 8, 2 * done + h, "near")
    for kind in range(2):
        for i in range(2, 4):
            core_copy(used[kind], i).wait_send()
    for p in range(len(pieces)):
        near_copy(p).wait_send()
        far_copy(p).wait_send()
        for d in range(3):
            z_copy(p, d).wait_send()
    for d in range(3):
        state_copy(d, t).wait_send()
    wait("out")


def backward(kept, a_turned, saved, cos, sin, tokens, out_grad, lengths):
    rows, width = tokens.shape
    low, wide = jnp.bfloat16, jnp.float32
    units = a_turned.shape[1]
    pair = width // 4
    shards = [w.shape[4:] for w in kept]
    dma = pltpu.SemaphoreType.DMA
    anywhere, in_vmem, in_smem = (
        pl.BlockSpec(memory_space=m) for m in (pl.ANY, pltpu.VMEM, pltpu.SMEM)
    )
    pieces = 2 * N_W

    def buffers(*lead):
        return [pltpu.VMEM((*lead, *s), low) for s in shards]

    outs = pl.pallas_call(
        backward_kernel,
        name="backward_and_scatter",
        out_shape=[jax.ShapeDtypeStruct(s, wide) for s in shards]
        + [jax.ShapeDtypeStruct((rows, width), wide)],
        in_specs=[anywhere] * (N_W + 1 + len(BWD_ANY))
        + [in_vmem] * len(BWD_VMEM)
        + [anywhere, anywhere, in_smem],
        out_specs=[in_vmem] * N_W + [anywhere],
        scratch_shapes=[
            *buffers(2, 2, 4),
            *buffers(2, 4),
            *buffers(4),
            *buffers(3),
            pltpu.VMEM((2, 2, 2, units, HEAD_DIM), low),
            pltpu.VMEM((2, 2, 2, HEAD_DIM, units), low),
            pltpu.VMEM((4, units, rows), low),
            pltpu.VMEM((4, rows, units), low),
            pltpu.VMEM((4, rows, units), low),
            pltpu.VMEM((2, rows, width // 2), low),
            pltpu.VMEM((2, width // 2, rows), low),
            pltpu.VMEM((rows, width), wide),
            pltpu.VMEM((rows, width), wide),
            pltpu.VMEM((2, 2, 2, 2, units, HEAD_DIM), low),
            pltpu.VMEM((2, 2, 2, 2, HEAD_DIM, units), low),
            pltpu.VMEM((2, 4, rows, pair), low),
            pltpu.VMEM((4, pair, rows), low),
            pltpu.VMEM((rows, rows), wide),
            pltpu.VMEM((4, width // HEAD_DIM, HEAD_DIM, HEAD_DIM), low),
            pltpu.VMEM((width // HEAD_DIM, HEAD_DIM, HEAD_DIM), low),
            dma((24,)),
            dma((2,)),
            dma((2,)),
            dma((2, 2)),
            dma((N_W, 4)),
            dma((pieces, 2)),
            dma((pieces, 2)),
            dma((pieces, 3)),
            dma((pieces, 3)),
            dma((3,)),
            dma((3,)),
        ],
        compiler_params=pltpu.CompilerParams(
            collective_id=1, has_side_effects=True, vmem_limit_bytes=VMEM_BYTES
        ),
    )(
        *kept,
        a_turned,
        *[saved[name] for name in BWD_ANY],
        saved["states"],
        saved["rates8"],
        cos,
        sin,
        tokens,
        out_grad,
        lengths,
    )
    return outs[:N_W], outs[N_W]


def body_by_kernels(
    tokens,
    lengths,
    rates,
    w_query,
    w_key,
    w_value,
    w_update,
    w_output,
    w_gate,
    w_up,
    w_down,
    out_grad,
):
    rows = tokens.shape[0]
    ends = jnp.cumsum(lengths[0], dtype=jnp.int32)
    places = lax.axis_index("tp") * rows + jnp.arange(rows, dtype=jnp.int32)
    segments = segment_of(places, ends)
    slots = jnp.arange(SLOTS, dtype=jnp.int32)
    starts = jnp.sum(jnp.where(segments[:, None] == slots, ends - lengths[0], 0), axis=1)
    positions = (places - starts).astype(jnp.float32)
    frequency = 10000.0 ** (-2.0 * jnp.arange(HEAD_DIM // 2, dtype=jnp.float32) / HEAD_DIM)
    turned = positions[:, None] * frequency[None, :]
    cos_half, sin_half = jnp.cos(turned), jnp.sin(turned)
    cos = jnp.concatenate([cos_half, cos_half], axis=1)
    sin = jnp.concatenate([-sin_half, sin_half], axis=1)
    shards = (w_query, w_key, w_value, w_update, w_output, w_gate, w_up, w_down)
    kept, a_turned, saved = forward(shards, tokens, cos, sin, lengths, rates)
    grads, d_tokens = backward(kept, a_turned, saved, cos, sin, tokens, out_grad, lengths)
    return (saved["result"], d_tokens, *grads)


def body(
    tokens,
    lengths,
    rates,
    w_query,
    w_key,
    w_value,
    w_update,
    w_output,
    w_gate,
    w_up,
    w_down,
    out_grad,
):
    tp_count = lax.axis_size("tp")
    tp_index = lax.axis_index("tp")
    rows, width = tokens.shape
    head_width = HEAD_DIM
    all_rates = lax.all_gather(rates, "tp", axis=0, tiled=True)
    heads = all_rates.shape[0]
    ends = jnp.cumsum(lengths[0], dtype=jnp.int32)
    first = tp_index * rows
    places = first + jnp.arange(rows, dtype=jnp.int32)
    segments = segment_of(places, ends)
    starts = ends - lengths[0]
    slots = jnp.arange(SLOTS, dtype=jnp.int32)
    positions = (
        places - jnp.sum(jnp.where(segments[:, None] == slots, starts, 0), axis=1)
    ).astype(jnp.float32)
    live = (segments < SLOTS - 1).astype(jnp.float32)
    frequency = 10000.0 ** (-2.0 * jnp.arange(head_width // 2, dtype=jnp.float32) / head_width)
    turned = positions[:, None] * frequency[None, :]
    cos_table, sin_table = jnp.cos(turned)[:, None, :], jnp.sin(turned)[:, None, :]

    gaps = places[:, None] - places[None, :]
    allowed = (segments[:, None] == segments[None, :]) & (gaps >= 0)
    spans = jnp.maximum(gaps, 0).astype(jnp.float32)
    decay = jnp.where(
        allowed[None], jnp.exp(-all_rates[:, None, None] * spans[None]), 0.0
    )
    blocks = jnp.arange(tp_count, dtype=jnp.int32)
    seg_before = segment_of(first - 1, ends)
    seg_after = segment_of(first + rows, ends)
    seg_last = segment_of(blocks * rows + rows - 1, ends)
    seg_first = segment_of(blocks * rows, ends)
    offsets = jnp.arange(rows, dtype=jnp.float32)

    def row_decay(distance, mask):
        return jnp.where(mask[:, None], jnp.exp(-distance[:, None] * all_rates[None]), 0.0)[
            :, :, None
        ]

    to_end = row_decay(rows - 1 - offsets, segments == segments[rows - 1])
    from_start = row_decay(offsets, segments == segments[0])
    into = row_decay(offsets + 1.0, segments == seg_before)
    out_of = row_decay(rows - offsets, segments == seg_after)

    def block_weights(mask, distance):
        distance = jnp.maximum(distance, 0).astype(jnp.float32)
        return jnp.where(mask[:, None], jnp.exp(-distance[:, None] * all_rates[None]), 0.0)

    before_weights = block_weights(
        (blocks < tp_index) & (seg_last == seg_before), (tp_index - blocks - 1) * rows
    )
    after_weights = block_weights(
        (blocks > tp_index) & (seg_first == seg_after), (blocks - tp_index - 1) * rows
    )

    tokens_f = tokens.astype(jnp.float32)
    scale1 = rms_scale(tokens_f)
    normed1 = (tokens_f * scale1).astype(jnp.bfloat16)
    shards = (w_query, w_key, w_value, w_update, w_output, w_gate, w_up, w_down)
    inner = (True, True, True, True, False, True, True, False)
    full = [
        gather_full(w, "fsdp", "tp") if rows_first else gather_full(w, "tp", "fsdp")
        for w, rows_first in zip(shards, inner)
    ]
    (
        query_full,
        key_full,
        value_full,
        update_full,
        output_full,
        gate_full,
        up_full,
        down_full,
    ) = full
    shape_heads = (rows, heads, head_width)
    query_pre = mm(normed1, query_full)
    key_pre = mm(normed1, key_full)
    value_rows = mm(normed1, value_full).astype(jnp.bfloat16).reshape(shape_heads)
    update_pre = mm(normed1, update_full)
    query = rotate(swish(query_pre).reshape(shape_heads), cos_table, sin_table).astype(jnp.bfloat16)
    key_rows = rotate(swish(key_pre).reshape(shape_heads), cos_table, sin_table).astype(
        jnp.bfloat16
    )
    update = swish(update_pre)
    key_state = heads_dot(
        "shc,shd->hcd", (key_rows * to_end).astype(jnp.bfloat16), value_rows
    ).astype(jnp.bfloat16)
    key_states = lax.all_gather(key_state, "tp", axis=0, tiled=False)
    state_in = jnp.sum(
        key_states.astype(jnp.float32) * before_weights[:, :, None, None], axis=0
    ).astype(jnp.bfloat16)
    weights = (heads_dot("thc,shc->hts", query, key_rows) * decay).astype(jnp.bfloat16)
    attn = heads_dot("hts,shd->thd", weights, value_rows) + into * heads_dot(
        "thc,hcd->thd", query, state_in
    )
    scale_attn = rms_scale(attn, head_floor)
    normed_attn = (attn * scale_attn).reshape(rows, width)
    mixed = (normed_attn * update).astype(jnp.bfloat16)
    middle = tokens_f + mm(mixed, output_full)
    scale2 = rms_scale(middle)
    normed2 = (middle * scale2).astype(jnp.bfloat16)
    gate_rows = mm(normed2, gate_full)
    up_rows = mm(normed2, up_full)
    hidden = (gate_rows * up_rows).astype(jnp.bfloat16)
    result = (middle + mm(hidden, down_full)).astype(jnp.bfloat16)

    cotangent = out_grad.astype(jnp.float32) * live[:, None]
    cot_rows = cotangent.astype(jnp.bfloat16)
    grad_down = mm_inner(hidden, cot_rows)
    d_hidden = mm_trans(cot_rows, down_full)
    d_gate = (d_hidden * up_rows).astype(jnp.bfloat16)
    d_up = (d_hidden * gate_rows).astype(jnp.bfloat16)
    grad_gate = mm_inner(normed2, d_gate)
    grad_up = mm_inner(normed2, d_up)
    d_normed2 = mm_trans(d_gate, gate_full) + mm_trans(d_up, up_full)
    d_middle = cotangent + norm_back(middle, scale2, d_normed2)
    mid_rows = d_middle.astype(jnp.bfloat16)
    d_mixed = mm_trans(mid_rows, output_full)
    grad_output = mm_inner(mixed, mid_rows)
    d_update_pre = (d_mixed * normed_attn * swish_slope(update_pre)).astype(jnp.bfloat16)
    d_attn = norm_back(attn, scale_attn, (d_mixed * update).reshape(shape_heads)).astype(
        jnp.bfloat16
    )
    query_state = heads_dot(
        "thc,thd->hcd", (query * from_start).astype(jnp.bfloat16), d_attn
    ).astype(jnp.bfloat16)
    query_states = lax.all_gather(query_state, "tp", axis=0, tiled=False)
    state_back = jnp.sum(
        query_states.astype(jnp.float32) * after_weights[:, :, None, None], axis=0
    ).astype(jnp.bfloat16)
    d_raw = (heads_dot("thd,shd->hts", d_attn, value_rows) * decay).astype(jnp.bfloat16)
    d_value = heads_dot("hts,thd->shd", weights, d_attn) + out_of * heads_dot(
        "shc,hcd->shd", key_rows, state_back
    )
    d_query = heads_dot("hts,shc->thc", d_raw, key_rows) + into * heads_dot(
        "thd,hcd->thc", d_attn, state_in
    )
    d_key = heads_dot("hts,thc->shc", d_raw, query) + out_of * heads_dot(
        "shd,hcd->shc", value_rows, state_back
    )
    d_query_pre = (
        swish_slope(query_pre) * rotate_back(d_query, cos_table, sin_table).reshape(rows, width)
    ).astype(jnp.bfloat16)
    d_key_pre = (
        swish_slope(key_pre) * rotate_back(d_key, cos_table, sin_table).reshape(rows, width)
    ).astype(jnp.bfloat16)
    d_value_pre = d_value.reshape(rows, width).astype(jnp.bfloat16)
    grads = [mm_inner(normed1, d) for d in (d_query_pre, d_key_pre, d_value_pre, d_update_pre)]
    d_normed1 = (
        mm_trans(d_query_pre, query_full)
        + mm_trans(d_key_pre, key_full)
        + mm_trans(d_value_pre, value_full)
        + mm_trans(d_update_pre, update_full)
    )
    d_tokens = d_middle + norm_back(tokens_f, scale1, d_normed1)
    grads = (*grads, grad_output, grad_gate, grad_up, grad_down)
    grads = [
        scatter_grad(g, "fsdp", "tp") if rows_first else scatter_grad(g, "tp", "fsdp")
        for g, rows_first in zip(grads, inner)
    ]
    return (result, d_tokens, *grads)


def solution(mesh):
    rows = P(AXES, None)
    inner, outer = P("fsdp", "tp"), P("tp", "fsdp")
    by_kernels = mesh.shape["fsdp"] == 8 and mesh.shape["tp"] == 4
    return jax.shard_map(
        body_by_kernels if by_kernels else body,
        mesh=mesh,
        in_specs=(
            rows,
            P("fsdp", None),
            P("tp"),
            inner,
            inner,
            inner,
            inner,
            outer,
            inner,
            inner,
            outer,
            rows,
        ),
        out_specs=(rows, rows, inner, inner, inner, inner, outer, inner, inner, outer),
        check_vma=False,
    )
```

time: 696 us -> 384 us (0.55); the launches traced: 684 us -> 383 us
  local copies, waits for them, and re-layouts: 203 us -> 15 us
  matrix products: 96.9 us -> 0 us
  other arithmetic: 44.2 us -> 3.67 us
  Pallas kernels: 324 us -> 364 us
  between operations: 15.3 us -> 0.73 us
    reshape x24 -> x0, local copies, waits for them, and re-layouts: 108 us -> none  [the longest x10 48.5 us: blocks_in(): grad.astype(jnp.bfloat16).reshape(8, depth, 4, width).transpose(0, 2, 1, 3)]
    dot_general x24 -> x0, matrix products: 96.9 us -> none  [the longest x8 37 us: mm_inner(): lax.dot_general(left, right, (((0,), (0,)), ((), ())), preferred_element_...]
    convert_element_type x13 -> x0, local copies, waits for them, and re-layouts: 42.5 us -> none  [the longest x6 13.5 us: body(): by_row(n).reshape(rows, width).astype(jnp.float32)]
    pallas_call x1, Pallas kernels: 150 us -> 191 us  [backward(): pl.pallas_call(backward_kernel, name='backward_and_scatter', out_shape=[j...]
    convert_element_type x11 -> x1, other arithmetic: 23.7 us -> 0.01 us  [body_by_kernels(): positions = (places - starts).astype(jnp.float32)]
    transpose x3 -> x0, local copies, waits for them, and re-layouts: 18 us -> none  [the longest x2 13.3 us: blocks_in(): grad.astype(jnp.bfloat16).reshape(8, depth, 4, width).transpose(0, 2, 1, 3)]
    unnamed x135 -> x26, local copies, waits for them, and re-layouts: 24.7 us -> 15 us
  transfers between devices with their start and end apart: 1 -> 0, of which waited for: 0 -> 0; matrix products, arithmetic and copies ran while one was open for 22% -> 0% of each run, Pallas kernels for 0% -> 0%
where the time goes in v4:
time: 384 us; the launch traced here: 383 us
  Pallas kernels  364 us (95%)
  local copies, waits for them, and re-layouts  15 us (4%)
    pallas_call x1, Pallas kernels, backward(): pl.pallas_call(backward_kernel, name='backward_and_scatter', out_shape=[j...  191 us
    pallas_call x1, Pallas kernels, forward(): pl.pallas_call(forward_kernel, name='gather_and_forward', out_shape=[jax....  173 us
    unnamed x26, local copies, waits for them, and re-layouts  15 us

profile of v4, /device:TPU:0, one launch (start us, length us, event | category | flops | bytes accessed | tf_op | source)
XLA Modules:
  0.0 383.5 jit_solution(6492259240449919885)
XLA Ops:
  0.6 0.8 reduce-window.8
  1.5 0.7 bitcast_subtract_fusion
  2.2 0.1 convert_reduce_fusion
  2.2 0.1 select_reduce_fusion
  2.3 1.7 copy.26.refs_5_
  4.1 1.7 copy.27.refs_6_
  5.8 1.0 fusion
  6.8 1.0 pad_maximum_fusion
  7.8 173.5 %gather_and_forward.1 = (bf16[2,2,2,4,128,256]{5,4,3,2,1,0:T(8,128)(2,1)}, bf16[2,2,2,4,128,256]{5,4,3,2,1,0:T(8,128)(2,1)}, bf16[2,2,2,4,128,256]{5,4,3,2,1,0:T...) custom-call(bf16[128,256]{1,0:T(8,128)(2,1)} %refs_0_.1, ...), custom_call_target="tpu_custom_call" | custom-call | tf_op jit(solution)/shard_map/gather_and_forward/pallas_call | solution.py:604
  181.3 190.5 %backward_and_scatter.1 = (f32[128,256]{1,0:T(8,128)}, f32[128,256]{1,0:T(8,128)}, f32[128,256]{1,0:T(8,128)}, f32[128,256]{1,0:T(8,128)}, f32[256,128]{1,0:T(8,...) custom-call(bf16[2,2,2,4,128,256]{5,4,3,2,1,0:T(8,128)(2,1)} %get-tuple-element.45.ref, ...), custom_call_target="tpu_custom_call" | custom-call | tf_op jit(solution)/shard_map/backward_and_scatter/pallas_call | solution.py:1219
  371.9 0.0 copy-start
  371.9 2.0 copy.28
  373.9 1.9 copy.29
  375.8 2.3 copy.38
  378.1 0.0 copy-done
  378.1 0.0 copy-start.6
  378.1 0.0 copy-start.3
  378.1 0.0 copy-start.2
  378.1 0.0 copy-start.1
  378.1 1.3 copy.39
  379.4 0.0 copy-done.6
  379.4 0.7 copy.40
  380.1 0.0 copy-done.5
  380.1 0.7 copy.41
  380.8 0.0 copy-done.4
  380.8 0.7 copy.42
  381.4 0.0 copy-done.3
  381.4 0.7 copy.43
  382.1 0.0 copy-done.2
  382.1 0.7 copy.44
  382.7 0.0 copy-done.1
  382.7 0.7 copy.45
  (5 shorter events, 0.0 us)
Async XLA Ops:
  371.9 6.2 %copy-start = (f32[512,1024]{1,0:T(8,128)S(1)}, f32[512,1024]{1,0:T(8,128)}, u32[]{:S(2)}) copy-start(f32[512,1024]{1,0:T(8,128)} %get-tuple-element.114) | copy-start | bytes 6291460
  378.1 1.4 copy-start.6
  378.1 2.0 copy-start.5
  378.1 2.7 copy-start.4
  378.1 3.3 copy-start.3
  378.1 4.0 %copy-start.2 = (f32[256,128]{1,0:T(8,128)S(1)}, f32[256,128]{1,0:T(8,128)}, u32[]{:S(2)}) copy-start(f32[256,128]{1,0:T(8,128)} %get-tuple-element.119) | copy-start | bytes 393220
  378.1 4.6 %copy-start.1 = (f32[704,128]{1,0:T(8,128)S(1)}, f32[704,128]{1,0:T(8,128)}, u32[]{:S(2)}) copy-start(f32[704,128]{1,0:T(8,128)} %get-tuple-element.122) | copy-start | bytes 1081348

commit v5 on v4

--- a/solution.py
+++ b/solution.py
@@ -1,3 +1,5 @@
+import functools
+
 import jax
 import jax.numpy as jnp
 from jax import lax
@@ -163,10 +165,55 @@
 
 
 ORDER = (1, 2, 0, 3, 4, 5, 6, 7)
+ROUTES = ("ab", "ab", "ab", "ab", "ab", "cdab", "abab", "abab")
+SLACK = 10.0
+RATE = 42_000.0
+
+
+def arrange(work, first, after):
+    clock, free, waiting, events, count = 0.0, {}, {}, [], 0
+    known, work = set(), list(work)
+
+    def offer(name):
+        known.add(name)
+        for item in after(name):
+            waiting.setdefault(item[0], []).append(item)
+
+    def pump():
+        nonlocal count
+        for link, items in waiting.items():
+            while items and free.get(link, 0.0) <= clock + SLACK:
+                _, size, send, receive, name = items.pop(0)
+                send()
+                free[link] = max(free.get(link, 0.0), clock) + size / RATE + 0.2
+                events.append((free[link] + 2.0, count, receive, name))
+                count += 1
+        events.sort(key=lambda event: event[:2])
+
+    for name in first:
+        offer(name)
+    pump()
+    while work or events:
+        if events and events[0][0] <= clock:
+            _, _, receive, name = events.pop(0)
+            receive()
+            offer(name)
+        elif work and work[0][2] <= known:
+            took, step, _, done = work.pop(0)
+            step()
+            clock += took
+            if done is not None:
+                offer(done)
+        else:
+            times = [free[link] - SLACK for link, items in waiting.items() if items]
+            clock = max(clock, min(times + [event[0] for event in events]))
+        pump()
+
+
 N_W = 8
 FWD_IN = ("tokens", "cos", "sin", "lengths", "rates")
 FWD_OUT = (
-    "result",
+    "res",
     "qp",
     "kp",
     "up",
@@ -174,14 +221,14 @@
     "k",
     "v",
     "o",
-    "w_turned",
+    "wt",
     "y1",
-    "n1_turned",
-    "n2_turned",
+    "n1t",
+    "n2t",
     "g",
     "e",
-    "states",
-    "rates8",
+    "st",
+    "r8",
 )
 
 
@@ -196,9 +243,12 @@
     full, refs = refs[:N_W], refs[N_W:]
     buf = dict(zip(FWD_OUT, refs))
     refs = refs[len(FWD_OUT) :]
-    n1, n2, mixed, hidden, hidden_turned, span, states, rate_tiles = refs[:8]
+    n1, hidden, hidden_turned, span, states, rate_tiles, gate_shard, up_shard = refs[:8]
     own_sem, z_send, z_recv, n_send, n_recv, c_send, c_recv = refs[8:15]
     s_send, s_recv, r_send, r_recv, keep_sem, out_sem, turn_sem = refs[15:]
+    gate_shard[...], up_shard[...] = shards[5][...].T, shards[6][...].T
+    shards = (*shards[:5], gate_shard, up_shard, shards[7])
+    n2, mixed = n1, buf["res"]
     rows = inp["tokens"].shape[0]
     y, x, c, f, t = place()
     core, along_x, along_y, along_z = peers_of(f, t)
@@ -206,17 +256,21 @@
         [jnp.full((1, rows), inp["rates"][i % 2], jnp.float32) for i in range(8)], axis=0
     )
     meet([core, along_x, along_y, *along_z])
-    pieces = [(w, h) for w in ORDER for h in range(2)]
+    pieces = [(w, h) for w in ORDER for h in range(len(ROUTES[w]))]
     total = len(pieces)
     all_ = slice(None)
 
-    def rows_of(piece):
-        w, h = piece
-        half = shards[w].shape[0] // 2
-        return pl.ds(h * half, half)
-
-    def slot(piece, *index):
-        return full[piece[0]].at[(*index, rows_of(piece))]
+    def rows_of(p):
+        w, h = pieces[p]
+        part = shards[w].shape[0] // len(ROUTES[w])
+        return pl.ds(h * part, part)
+
+    def route_of(p):
+        w, h = pieces[p]
+        return ROUTES[w][h]
+
+    def slot(p, *index):
+        return full[pieces[p][0]].at[(*index, rows_of(p))]
 
     def remote(src, dst, send, recv, peer):
         return pltpu.make_async_remote_copy(
@@ -224,24 +278,19 @@
         )
 
     def own_copy(p):
-        piece = pieces[p]
         return pltpu.make_async_copy(
-            shards[piece[0]].at[rows_of(piece)], slot(piece, y, x, c, t), own_sem.at[p]
+            shards[pieces[p][0]].at[rows_of(p)], slot(p, y, x, c, t), own_sem.at[p]
         )
 
     def z_copy(p, d, source):
-        piece = pieces[p]
-        return remote(
-            shards[piece[0]].at[rows_of(piece)],
-            slot(piece, y, x, c, source),
-            z_send.at[p, d],
-            z_recv.at[p, d],
-            along_z[d],
-        )
+        if route_of(p) in "ab":
+            src, dst = shards[pieces[p][0]].at[rows_of(p)], slot(p, y, x, c, source)
+        else:
+            src, dst = slot(p, all_, all_, c, t), slot(p, all_, all_, c, source)
+        return remote(src, dst, z_send.at[p, d], z_recv.at[p, d], along_z[d])
 
     def near_copy(p, stage, arriving):
-        piece = pieces[p]
-        over_x = (piece[1] == 0) == (stage == 0)
+        over_x = (route_of(p) in "ac") == (stage == 0)
         if stage == 0:
             index = (y, x, c)
             if arriving:
@@ -251,32 +300,36 @@
                 index = (all_, (1 - x) if arriving else x, c)
             else:
                 index = ((1 - y) if arriving else y, all_, c)
-        ref = slot(piece, *index, all_)
+        ref = slot(p, *index, all_ if route_of(p) in "ab" else t)
+        src = ref
+        if stage == 0 and route_of(p) in "cd":
+            src = shards[pieces[p][0]].at[rows_of(p)]
         return remote(
-            ref, ref, n_send.at[p, stage], n_recv.at[p, stage], along_x if over_x else along_y
+            src, ref, n_send.at[p, stage], n_recv.at[p, stage], along_x if over_x else along_y
         )
 
+    def core_parts(p):
+        return range(3 if route_of(p) in "ab" else 4)
+
     def core_copy(p, part, arriving):
-        piece = pieces[p]
         side = (1 - c) if arriving else c
-        first_x = piece[1] == 0
-        index = (
-            (y, x, side),
-            (y, 1 - x, side) if first_x else (1 - y, x, side),
-            (1 - y, all_, side) if first_x else (all_, 1 - x, side),
-        )[part]
-        ref = slot(piece, *index, all_)
+        if route_of(p) in "ab":
+            first_x = route_of(p) == "a"
+            index = (
+                (y, x, side, all_),
+                (y, 1 - x, side, all_) if first_x else (1 - y, x, side, all_),
+                (1 - y, all_, side, all_) if first_x else (all_, 1 - x, side, all_),
+            )[part]
+        else:
+            index = (all_, all_, side, (t + part) % 4)
+        ref = slot(p, *index)
         return remote(ref, ref, c_send.at[p, part], c_recv.at[p, part], core)
 
-    def start_z(p):
-        own_copy(p).start()
-        for d in range(3):
-            z_copy(p, d, t).start()
-
     def arrived(w):
-        for h in range(2):
-            for part in range(3):
-                core_copy(pieces.index((w, h)), part, True).wait_recv()
+        for p in range(total):
+            if pieces[p][0] == w:
+                for part in core_parts(p):
+                    core_copy(p, part, True).wait_recv()
         keep(w).start()
 
     def keep(w):
@@ -300,7 +353,7 @@
         return pl.ds(pl.multiple_of(i * 2 * HEAD_DIM + j * HEAD_DIM, HEAD_DIM), HEAD_DIM)
 
     def rate_of(h):
-        return buf["rates8"][pl.ds(h, 1), :]
+        return buf["r8"][pl.ds(h, 1), :]
 
     def turn_rows(source, target):
         for j in range(8):
@@ -312,16 +365,16 @@
             rate_copy(d, t).start()
         values = inp["tokens"][...].astype(jnp.float32)
         n1[...] = (values * rms_scale(values)).astype(jnp.bfloat16)
-        turn_rows(n1, buf["n1_turned"])
-        save("n1_turned").start()
+        turn_rows(n1, buf["n1t"])
+        save("n1t").start()
         fill_span(span, ends, first)
 
     def rates_here():
         for d in range(3):
             rate_copy(d, (t + 3 - d) % 4).wait_recv()
         for j in range(4):
-            buf["rates8"][2 * j : 2 * j + 2] = rate_tiles[j, 0:2]
-        save("rates8").start()
+            buf["r8"][2 * j : 2 * j + 2] = rate_tiles[j, 0:2]
+        save("r8").start()
 
     def project(w, finish):
         def run():
@@ -392,57 +445,48 @@
                 distance = jnp.maximum(t - j - 1, 0).astype(jnp.float32) * rows
                 weight = reach * jnp.exp(-rate * distance)
                 result = result + weight * states[j, h].astype(jnp.float32)
-            buf["states"][h] = result.astype(jnp.bfloat16)
+            buf["st"][h] = result.astype(jnp.bfloat16)
             return carry
 
         lax.fori_loop(0, 8, head, 0)
-        save("states").start()
+        save("st").start()
         for name in ("q", "qp", "up"):
             save(name).start()
 
-    def attend(i):
+    def attend(h, carry):
         before = scalar_segment(first - 1, ends)
         half = rows // 2
-
-        def go():
-            for j in range(2):
-                h, lanes = 2 * i + j, slice(j * HEAD_DIM, (j + 1) * HEAD_DIM)
-                rate = rate_of(h)
-                for b in range(2):
-                    mine = slice(b * half, (b + 1) * half)
-                    keys = (b + 1) * half
-                    query = buf["q"][i, mine, lanes]
-                    scores = dot_nt(query, buf["k"][i, :keys, lanes])
-                    decay = jnp.exp(-span[mine, :keys] * rate[:, :keys])
-                    weights = (scores * decay).astype(jnp.bfloat16)
-                    into = jnp.where(
-                        segments[mine] == before,
-                        jnp.exp(-(steps_f[mine] + 1.0) * rate[:, :HEAD_DIM]),
-                        0.0,
-                    )
-                    attn = dot(weights, buf["v"][i, :keys, lanes]) + into * dot(
-                        query, buf["states"][h]
-                    )
-                    columns = head_columns(i, j)
-                    buf["o"][mine, columns] = attn
-                    normed = attn * rms_scale(attn, head_floor)
-                    mixed[mine, columns] = (normed * buf["y1"][mine, columns]).astype(jnp.bfloat16)
-
-        return go
+        i = h // 2
+        lanes = pl.ds(pl.multiple_of(lax.rem(h, 2) * HEAD_DIM, HEAD_DIM), HEAD_DIM)
+        columns = pl.ds(pl.multiple_of(h * HEAD_DIM, HEAD_DIM), HEAD_DIM)
+        rate = rate_of(h)
+        for b in range(2):
+            mine = slice(b * half, (b + 1) * half)
+            keys = (b + 1) * half
+            query = buf["q"][i, mine, lanes]
+            scores = dot_nt(query, buf["k"][i, :keys, lanes])
+            decay = jnp.exp(-span[mine, :keys] * rate[:, :keys])
+            weights = (scores * decay).astype(jnp.bfloat16)
+            into = jnp.where(
+                segments[mine] == before,
+                jnp.exp(-(steps_f[mine] + 1.0) * rate[:, :HEAD_DIM]),
+                0.0,
+            )
+            attn = dot(weights, buf["v"][i, :keys, lanes]) + into * dot(query, buf["st"][h])
+            buf["o"][mine, columns] = attn
+            normed = attn * rms_scale(attn, head_floor)
+            mixed[mine, columns] = (normed * buf["y1"][mine, columns]).astype(jnp.bfloat16)
+        return carry
 
     def attend_pairs(lo, hi):
-        def step(i, carry):
-            attend(i)()
-            return carry
-
-        return lambda: (lax.fori_loop(lo, hi, step, 0), None)[1]
+        return lambda: (lax.fori_loop(2 * lo, 2 * hi, attend, 0), None)[1]
 
     def mix():
         save("o").start()
         for i in range(4):
             columns = slice(i * 2 * HEAD_DIM, (i + 1) * 2 * HEAD_DIM)
-            buf["w_turned"][i] = mixed[:, columns].T
-        save("w_turned").start()
+            buf["wt"][i] = mixed[:, columns].T
+        save("wt").start()
         arrived(4)
 
         def block(i, carry):
@@ -456,9 +500,9 @@
         lax.fori_loop(0, 4, block, 0)
         values = buf["y1"][...]
         n2[...] = (values * rms_scale(values)).astype(jnp.bfloat16)
-        turn_rows(n2, buf["n2_turned"])
+        turn_rows(n2, buf["n2t"])
         save("y1").start()
-        save("n2_turned").start()
+        save("n2t").start()
 
     def turned_out(i):
         return pltpu.make_async_copy(hidden_turned.at[i % 2], a_out.at[i], turn_sem.at[i])
@@ -468,13 +512,17 @@
             if i == 0:
                 arrived(6)
             shape = (n1.shape[1], full[5].shape[5])
-            for b in range(2):
-                mine = slice(b * rows // 2, (b + 1) * rows // 2)
+
+            def band(b, carry):
+                mine = pl.ds(pl.multiple_of(b * rows // 2, rows // 2), rows // 2)
                 gate = dot(n2[mine], full[5][:, :, :, i].reshape(shape))
                 lift = dot(n2[mine], full[6][:, :, :, i].reshape(shape))
                 hidden[i, mine] = (gate * lift).astype(jnp.bfloat16)
                 buf["g"][i, mine] = gate.astype(jnp.bfloat16)
                 buf["e"][i, mine] = lift.astype(jnp.bfloat16)
+                return carry
+
+            lax.fori_loop(0, 2, band, 0)
             if i >= 2:
                 turned_out(i - 2).wait()
             hidden_turned[i % 2] = hidden[i].T
@@ -494,65 +542,86 @@
             for j in range(4):
                 sides = [full[7][i // 2, i % 2, s, j] for s in range(2)]
                 values = values + dot(hidden[j], jnp.concatenate(sides, axis=1))
-            buf["result"][:, columns] = values.astype(jnp.bfloat16)
+            buf["res"][:, columns] = values.astype(jnp.bfloat16)
             return carry
 
         lax.fori_loop(0, 4, block, 0)
-        save("result").start()
-
-    lead, lag = 4, 2
-
-    def ready(w):
-        return 2 * ORDER.index(w) + 1 + 2 * lag + 1
-
-    work = [
-        (0, begin),
-        (4, rates_here),
-        (ready(1), project(1, finish_key)),
-        (ready(2), project(2, finish_value)),
-        (ready(2), make_states),
-        (ready(0), send_states),
-        (ready(0), project(0, finish_query)),
-        (ready(3), project(3, finish_update)),
-        (ready(3), sum_states),
-        *[(ready(3), attend_pairs(i, i + 1)) for i in range(4)],
-        (ready(4), mix),
-        (ready(5), lambda: arrived(5)),
-        *[(ready(6), gate_up(i)) for i in range(4)],
-        (ready(7), close),
-    ]
-
-    def some_work(step):
-        if work and work[0][0] <= step:
-            work.pop(0)[1]()
-
-    for p in range(min(lead, total)):
-        start_z(p)
-    some_work(0)
-    for step in range(total + 2 * lag):
-        if lead <= step + lead < total:
-            start_z(step + lead)
-        p = step
-        if p < total:
-            own_copy(p).wait()
-            for d in range(3):
-                z_copy(p, d, (t + 3 - d) % 4).wait_recv()
-            near_copy(p, 0, False).start()
-            core_copy(p, 0, False).start()
-            some_work(step)
-        p = step - lag
-        if 0 <= p < total:
-            near_copy(p, 0, True).wait_recv()
-            near_copy(p, 1, False).start()
-            core_copy(p, 1, False).start()
-            some_work(step)
-        p = step - 2 * lag
-        if 0 <= p < total:
-            near_copy(p, 1, True).wait_recv()
-            core_copy(p, 2, False).start()
-            some_work(step)
-    while work:
-        work.pop(0)[1]()
+        save("res").start()
+
+    def after(name):
+        stage, p, part = name
+        size = shards[pieces[p][0]].size * 2 // len(ROUTES[pieces[p][0]])
+        early = route_of(p) in "ab"
+
+        def over_z():
+            def send():
+                for d in range(3):
+                    z_copy(p, d, t).start()
+
+            def receive():
+                for d in range(3):
+                    z_copy(p, d, (t + 3 - d) % 4).wait_recv()
+                if early:
+                    own_copy(p).wait()
+
+            return ("z", (4 if early else 16) * size, send, receive, ("z", p, 0))
+
+        def over_near(k):
+            blocks = (4, 8)[k] if early else (1, 2)[k]
+            link = "x" if (route_of(p) in "ac") == (k == 0) else "y"
+
+            def receive():
+                near_copy(p, k, True).wait_recv()
+                if k == 0 and not early:
+                    own_copy(p).wait()
+
+            return (link, blocks * size, near_copy(p, k, False).start, receive, ("n", p, k))
+
+        def over_core(k, blocks):
+            def send():
+                core_copy(p, k, False).start()
+
+            return ("c", blocks * size // 4, send, lambda: None, ("c", p, k))
+
+        if stage == "go":
+            own_copy(p).start()
+            return [over_z() if early else over_near(0)]
+        if stage == "z":
+            if early:
+                return [over_near(0), over_core(0, 4)]
+            return [over_core(k, 4) for k in (1, 2, 3)]
+        if stage == "n":
+            if part == 0:
+                return [over_near(1)] + ([over_core(1, 4)] if early else [])
+            return [over_core(2, 8)] if early else [over_z(), over_core(0, 4)]
+        return []
+
+    needs = set()
+    steps = []
+
+    def then(took, step, *weights):
+        for p in range(total):
+            if pieces[p][0] in weights:
+                needs.update(("c", p, k) for k in core_parts(p))
+        steps.append((took, step, set(needs), None))
+
+    then(2.0, begin)
+    then(0.2, rates_here)
+    then(2.2, project(1, finish_key), 1)
+    then(2.2, project(2, finish_value), 2)
+    then(1.5, make_states)
+    then(2.2, project(0, finish_query), 0)
+    then(0.2, send_states)
+    then(2.2, project(3, finish_update), 3)
+    then(0.5, sum_states)
+    for i in range(4):
+        then(1.8, attend_pairs(i, i + 1))
+    then(3.0, mix, 4)
+    then(0.1, lambda: arrived(5), 5)
+    for i in range(4):
+        then(3.0, gate_up(i), 6)
+    then(4.0, close, 7)
+    arrange(steps, [("go", p, 0) for p in range(total)], after)
     for d in range(3):
         rate_copy(d, t).wait_send()
         state_copy(d, t).wait_send()
@@ -561,7 +630,7 @@
             z_copy(p, d, t).wait_send()
         for stage in range(2):
             near_copy(p, stage, False).wait_send()
-        for part in range(3):
+        for part in core_parts(p):
             core_copy(p, part, False).wait_send()
     for w in range(N_W):
         keep(w).wait()
@@ -573,14 +642,14 @@
 
 def forward(shards, tokens, cos, sin, lengths, rates):
     rows, width = tokens.shape
-    units = shards[5].shape[1]
+    units, depth = shards[5].shape
     heads = width // HEAD_DIM
     low, wide = jnp.bfloat16, jnp.float32
     by_pair = (4, rows, heads // 4 * HEAD_DIM)
     turned = (2, width // 2, rows)
     by_unit = (4, rows, units)
     shapes = {
-        "result": ((rows, width), low),
+        "res": ((rows, width), low),
         "qp": (by_pair, low),
         "kp": (by_pair, low),
         "up": (by_pair, low),
@@ -588,17 +657,17 @@
         "k": (by_pair, low),
         "v": (by_pair, low),
         "o": ((rows, width), wide),
-        "w_turned": ((4, width // 4, rows), low),
+        "wt": ((4, width // 4, rows), low),
         "y1": ((rows, width), wide),
-        "n1_turned": (turned, low),
-        "n2_turned": (turned, low),
+        "n1t": (turned, low),
+        "n2t": (turned, low),
         "g": (by_unit, low),
         "e": (by_unit, low),
-        "states": ((heads, HEAD_DIM, HEAD_DIM), low),
-        "rates8": ((8, rows), wide),
+        "st": ((heads, HEAD_DIM, HEAD_DIM), low),
+        "r8": ((8, rows), wide),
     }
-    blocks = [(2, 2, 2, 4, *s.shape) for s in shards]
-    pieces = 2 * N_W
+    blocks = [(2, 2, 2, 4, *(s.shape[::-1] if i in (5, 6) else s.shape)) for i, s in enumerate(shards)]
+    pieces = sum(len(route) for route in ROUTES)
     dma = pltpu.SemaphoreType.DMA
     in_vmem, in_smem = (pl.BlockSpec(memory_space=m) for m in (pltpu.VMEM, pltpu.SMEM))
     outs = pl.pallas_call(
@@ -613,20 +682,20 @@
             *[pltpu.VMEM(b, low) for b in blocks],
             *[pltpu.VMEM(*shapes[name]) for name in FWD_OUT],
             pltpu.VMEM((rows, width), low),
-            pltpu.VMEM((rows, width), low),
-            pltpu.VMEM((rows, width), low),
             pltpu.VMEM(by_unit, low),
             pltpu.VMEM((2, units, rows), low),
             pltpu.VMEM((rows, rows), wide),
             pltpu.VMEM((4, heads, HEAD_DIM, HEAD_DIM), low),
             pltpu.VMEM((4, 8, rows), wide),
+            pltpu.VMEM((depth, units), low),
+            pltpu.VMEM((depth, units), low),
             dma((pieces,)),
             dma((pieces, 3)),
             dma((pieces, 3)),
             dma((pieces, 2)),
             dma((pieces, 2)),
-            dma((pieces, 3)),
-            dma((pieces, 3)),
+            dma((pieces, 4)),
+            dma((pieces, 4)),
             dma((3,)),
             dma((3,)),
             dma((3,)),
@@ -642,10 +711,10 @@
     return outs[:N_W], outs[N_W], dict(zip(FWD_OUT, outs[N_W + 1 :]))
 
 
-BWD_ANY = ("q", "k", "v", "up", "qp", "kp", "o", "w_turned", "y1", "n1_turned", "n2_turned", "g", "e")
-BWD_VMEM = ("states", "rates8", "cos", "sin")
+BWD_ANY = ("q", "k", "v", "up", "qp", "kp", "o", "wt", "y1", "n1t", "n2t", "g", "e")
+BWD_VMEM = ("st", "r8", "cos", "sin")
 BAND = 32
-LINK = 42_000.0
+SUMS = ("ab", "ab", "ab", "ab", "ab", "cb", "ab", "ab")
 
 
 def slope_of(values):
@@ -670,13 +739,12 @@
     tall, wide, turned_a, gq, ev, d_side, n_turned, rows_a, rows_b, tall_w, wide_w = refs[:11]
     q_pre, w_turned, span, states, back = refs[11:16]
     load_sem, tall_sem, wide_sem, c_send, c_recv, n_send, n_recv, z_send, z_recv = refs[16:25]
-    s_send, s_recv = refs[25:]
+    s_send, s_recv, o_send, o_recv = refs[25:]
     rows, width = rows_a.shape
     half = rows // 2
     y, x, c, f, t = place()
     core, along_x, along_y, along_z = peers_of(f, t)
     all_ = slice(None)
-    side = {"theirs": 1 - c, "mine": c}
 
     keys = {}
 
@@ -697,11 +765,11 @@
         "a": [load("a", a_in, turned_a)],
         "g": [load("g", inp["g"], gq)],
         "e": [load("e", inp["e"], ev)],
-        "n2": [load("n2", inp["n2_turned"], n_turned)],
-        "n1": [load("n1", inp["n1_turned"], n_turned)],
+        "n2": [load("n2", inp["n2t"], n_turned)],
+        "n1": [load("n1", inp["n1t"], n_turned)],
         "y1": [load("y1", inp["y1"], rows_a)],
         "o": [load("o", inp["o"], rows_a)],
-        "w": [load("w", inp["w_turned"], w_turned)],
+        "w": [load("w", inp["wt"], w_turned)],
         "qp": [load("qp", inp["qp"], q_pre.at[0])],
         "kp": [load("kp", inp["kp"], q_pre.at[1])],
         "q": [load("q", inp["q"], gq.at[:, :, lane_pair[0]])],
@@ -732,13 +800,13 @@
             kept[w].at[:, :, :, i], wide_w.at[slot, :, :, :, :, :lanes], wide_sem.at[slot]
         )
 
-    def over_tiles(w, use):
-        tile(w, 0, 0).start()
+    def over_tiles(w, use, lo=0, hi=4):
+        tile(w, lo, lo % 2).start()
 
         def step(i, carry):
             slot = lax.rem(i, 2)
 
-            @pl.when(i < 3)
+            @pl.when(i < hi - 1)
             def _():
                 tile(w, i + 1, 1 - slot).start()
 
@@ -746,7 +814,7 @@
             use(i, slot)
             return carry
 
-        lax.fori_loop(0, 4, step, 0)
+        lax.fori_loop(lo, hi, step, 0)
 
     pieces = [(w, h) for w in range(N_W) for h in range(2)]
 
@@ -806,6 +874,31 @@
             along_z[d],
         )
 
+    def far_first(p, d, a, source):
+        w, part = pieces[p][0], rows_of(p)
+        dst = from_near[w].at[d, 2 * a : 2 * a + 2] if d < 2 else from_far[w].at[2 * a : 2 * a + 2]
+        return remote(
+            mine[w].at[a, :, source, part],
+            dst.at[:, part],
+            o_send.at[2 * d + a],
+            o_recv.at[2 * d + a],
+            along_z[d],
+        )
+
+    def then_near(p, k):
+        w, part = pieces[p][0], rows_of(p)
+        if k == 0:
+            src, dst = mine[w].at[1 - y, :, t, part], from_z[w].at[0:2, part]
+        else:
+            src, dst = mine[w].at[y, 1 - x, t, part], from_z[w].at[2, part]
+        return remote(src, dst, o_send.at[6 + k], o_recv.at[6 + k], (along_y, along_x)[k])
+
+    def plus(into, *terms):
+        total = into[...].astype(jnp.float32)
+        for term in terms:
+            total = total + term[...].astype(jnp.float32)
+        return total
+
     def add(steps, target, other):
         def step(i, carry):
             into, term = target(i), other(i)
@@ -824,14 +917,11 @@
         else:
             into = lambda i: mine[w].at[i // 4, x, i % 4, part]
         add(8, into, lambda i: from_near[w].at[i // 4, i % 4, part])
-        far_copy(p).start()
 
     def after_far(p):
         w, part = pieces[p][0], rows_of(p)
         far_copy(p).wait_recv()
         add(4, lambda i: mine[w].at[y, x, i, part], lambda i: from_far[w].at[i, part])
-        for d in range(3):
-            z_copy(p, d).start()
 
     def after_z(p):
         w, part = pieces[p][0], rows_of(p)
@@ -844,17 +934,21 @@
 
     used = {0: None, 1: None}
 
-    def gradient(w, whose, value):
+    def gradient(w, own, value):
         ring, kind = ring_of(w)
         depth, lanes = grads[w].shape
 
-        def blocks(result):
-            if kind == 1:
-                return [(j // 2, j % 2, result[j * depth : (j + 1) * depth]) for j in range(4)]
-            return [(j // 2, j % 2, result[:, j * lanes : (j + 1) * lanes]) for j in range(4)]
+        def blocks(i):
+            for q in range(2):
+                result = value(i, (c if own else 1 - c), slice(2 * q * HEAD_DIM, (2 * q + 2) * HEAD_DIM))
+                for b in range(2):
+                    if kind == 1:
+                        yield q, b, result[b * depth : (b + 1) * depth]
+                    else:
+                        yield q, b, result[:, b * lanes : (b + 1) * lanes]
 
         def run():
-            if whose == "theirs":
+            if not own:
                 before = used[kind]
                 used[kind] = w
 
@@ -870,9 +964,8 @@
                         core_copy(w, i - 2).wait_send()
 
                     slot = lax.rem(i, 2)
-                    result = value(i, side[whose]).astype(jnp.bfloat16)
-                    for a, b, part in blocks(result):
-                        ring[slot, a, b, :depth, :lanes] = part
+                    for a, b, part in blocks(i):
+                        ring[slot, a, b, :depth, :lanes] = part.astype(jnp.bfloat16)
                     core_copy(w, i).start()
                     return carry
 
@@ -881,16 +974,13 @@
 
                 def step(i, carry):
                     core_copy(w, i).wait_recv()
-                    result = value(i, side[whose])
-                    for a, b, part in blocks(result):
+                    for a, b, part in blocks(i):
                         mine[w][a, b, i] = (mine[w][a, b, i].astype(jnp.float32) + part).astype(
                             jnp.bfloat16
                         )
                     return carry
 
                 lax.fori_loop(0, 4, step, 0)
-                for h in range(2):
-                    near_copy(2 * w + h).start()
 
         return run
 
@@ -904,7 +994,7 @@
         return slice(base + j * HEAD_DIM, base + (j + 1) * HEAD_DIM)
 
     def rate_of(h):
-        return inp["rates8"][pl.ds(h, 1), :]
+        return inp["r8"][pl.ds(h, 1), :]
 
     def over_rows(use):
         def step(i, carry):
@@ -925,12 +1015,10 @@
         start("qp", "kp")
         wait("a")
 
-    def expand():
-        wait("e", "g")
-
+    def expand(lo, hi):
         def use(i, slot):
-            for b in range(2):
-                part = slice(b * half, (b + 1) * half)
+            def band(b, carry):
+                part = pl.ds(pl.multiple_of(b * half, half), half)
                 d_hidden = sum(
                     dot_nt(
                         d_side[s, part],
@@ -941,9 +1029,18 @@
                 lift, gate = ev[i, part].astype(jnp.float32), gq[i, part].astype(jnp.float32)
                 ev[i, part] = (d_hidden * lift).astype(jnp.bfloat16)
                 gq[i, part] = (d_hidden * gate).astype(jnp.bfloat16)
-
-        over_tiles(7, use)
-        wait("n2")
+                return carry
+
+            lax.fori_loop(0, 2, band, 0)
+
+        def run():
+            if lo == 0:
+                wait("e", "g")
+            over_tiles(7, use, lo, hi)
+            if hi == 4:
+                wait("n2")
+
+        return run
 
     def through(w, source, target, clear):
         def run():
@@ -982,25 +1079,32 @@
         wait("o", "up")
 
         def use(i, slot):
-            d_mixed = sum(
-                dot_nt(
-                    d_side[s],
-                    jnp.concatenate(
-                        [tall_w[slot, j // 2, j % 2, s, : 2 * HEAD_DIM] for j in range(4)], axis=1
-                    ),
+            def band(b, carry):
+                part = pl.ds(pl.multiple_of(b * half, half), half)
+                d_mixed = sum(
+                    dot_nt(
+                        d_side[s, part],
+                        jnp.concatenate(
+                            [tall_w[slot, j // 2, j % 2, s, : 2 * HEAD_DIM] for j in range(4)], axis=1
+                        ),
+                    )
+                    for s in range(2)
                 )
-                for s in range(2)
-            )
-            for j in range(2):
-                columns = pl.ds(pl.multiple_of((2 * i + j) * HEAD_DIM, HEAD_DIM), HEAD_DIM)
-                attn = rows_a[:, columns]
-                scale = rms_scale(attn, head_floor)
-                normed = attn * scale
-                pre = turned_a[i, :rows, lanes_of(j, 2 * HEAD_DIM)].astype(jnp.float32)
-                part = d_mixed[:, lanes_of(j)]
-                turned_a[i, :rows, lanes_of(j)] = (part * normed * slope_of(pre)).astype(jnp.bfloat16)
-                d_attn = norm_back(attn, scale, part * swish_of(pre))
-                ev[i, :, lanes_of(j, 2 * HEAD_DIM)] = d_attn.astype(jnp.bfloat16)
+                for j in range(2):
+                    columns = pl.ds(pl.multiple_of((2 * i + j) * HEAD_DIM, HEAD_DIM), HEAD_DIM)
+                    attn = rows_a[part, columns]
+                    scale = rms_scale(attn, head_floor)
+                    normed = attn * scale
+                    pre = turned_a[i, part, lanes_of(j, 2 * HEAD_DIM)].astype(jnp.float32)
+                    grad_ = d_mixed[:, lanes_of(j)]
+                    turned_a[i, part, lanes_of(j)] = (grad_ * normed * slope_of(pre)).astype(
+                        jnp.bfloat16
+                    )
+                    d_attn = norm_back(attn, scale, grad_ * swish_of(pre))
+                    ev[i, part, lanes_of(j, 2 * HEAD_DIM)] = d_attn.astype(jnp.bfloat16)
+                return carry
+
+            lax.fori_loop(0, 2, band, 0)
 
         over_tiles(4, use)
         wait("n1", "q")
@@ -1052,7 +1156,7 @@
         rate = rate_of(h)
         short = rate[:, :HEAD_DIM]
         key, value = gq[i, :, high_lanes], ev[i, :, low_lanes]
-        state_in, state_back = inp["states"][h], back[h]
+        state_in, state_back = inp["st"][h], back[h]
         out_of = jnp.where(segments == seg_after, jnp.exp(-(rows - steps_f) * short), 0.0)
         d_value = out_of * dot(key, state_back)
         d_key = out_of * dot_nt(value, state_back)
@@ -1108,38 +1212,39 @@
         6: lambda i: gq[i],
     }
 
-    def grad(w, whose):
+    def grad(w, own):
         if w == 7:
-            value = lambda i, s: dot(turned_a[i], d_side[s])
+            value = lambda i, s, half_: dot(turned_a[i], d_side[s, :, half_])
         elif w == 4:
-            value = lambda i, s: dot(w_turned[i], d_side[s])
+            value = lambda i, s, half_: dot(w_turned[i], d_side[s, :, half_])
         else:
-            value = lambda i, s: dot(n_turned[s], sources[w](i))
-        return gradient(w, whose, value)
+            value = lambda i, s, half_: dot(n_turned[s, half_], sources[w](i))
+        return gradient(w, own, value)
 
     def attend_pairs(lo, hi):
         return lambda: (lax.fori_loop(2 * lo, 2 * hi, attend_back, 0), None)[1]
 
     work = [
         (3.0, begin, None),
-        (2.5, grad(7, "theirs"), None),
-        (6.0, expand, None),
-        (2.5, grad(5, "theirs"), None),
-        (3.0, grad(7, "mine"), 7),
+        (2.5, grad(7, False), None),
+        (3.0, expand(0, 2), None),
+        (3.0, grad(7, True), 7),
+        (3.0, expand(2, 4), None),
+        (2.5, grad(5, False), None),
         (0.1, lambda: start("up"), None),
-        (2.5, grad(6, "theirs"), None),
-        (3.0, grad(5, "mine"), 5),
-        (3.0, grad(6, "mine"), 6),
+        (2.5, grad(6, False), None),
+        (3.0, grad(5, True), 5),
+        (3.0, grad(6, True), 6),
         (0.1, lambda: start("n1"), None),
         (5.0, through(5, sources[5], rows_b, True), None),
         (5.0, through(6, sources[6], rows_b, False), None),
         (3.0, middle_back, None),
-        (1.0, grad(4, "theirs"), None),
+        (1.0, grad(4, False), None),
         (6.0, mixed_back, None),
-        (1.0, grad(3, "theirs"), None),
-        (1.2, grad(4, "mine"), 4),
+        (1.0, grad(3, False), None),
+        (1.2, grad(4, True), 4),
         (2.0, make_states, None),
-        (1.2, grad(3, "mine"), 3),
+        (1.2, grad(3, True), 3),
         (0.1, send_states, None),
         (2.0, through(3, sources[3], rows_a, True), None),
         (1.0, sum_states, None),
@@ -1147,12 +1252,12 @@
         (4.0, attend_pairs(1, 2), None),
         (4.0, attend_pairs(2, 3), None),
         (4.0, attend_pairs(3, 4), None),
-        (1.0, grad(2, "theirs"), None),
-        (1.0, grad(0, "theirs"), None),
-        (1.0, grad(1, "theirs"), None),
-        (1.2, grad(2, "mine"), 2),
-        (1.2, grad(0, "mine"), 0),
-        (1.2, grad(1, "mine"), 1),
+        (1.0, grad(2, False), None),
+        (1.0, grad(0, False), None),
+        (1.0, grad(1, False), None),
+        (1.2, grad(2, True), 2),
+        (1.2, grad(0, True), 0),
+        (1.2, grad(1, True), 1),
         (0.1, lambda: start("tokens"), None),
         (2.0, through(2, sources[2], rows_a, False), None),
         (2.0, through(0, sources[0], rows_a, False), None),
@@ -1160,42 +1265,89 @@
         (2.0, close, None),
     ]
     meet([core, along_x, along_y, *along_z])
-    clock, free, events = 0.0, {"x": 0.0, "y": 0.0, "z": 0.0}, []
-
-    def expect(link, blocks, p, step):
-        size = blocks * grads[pieces[p][0]].size // 2 * 2
-        free[link] = max(free[link], clock) + size / LINK
-        events.append((free[link] + 2.0, step, p))
-
-    while work or events:
-        events.sort(key=lambda event: event[0])
-        if events and (not work or events[0][0] <= clock):
-            due, step, p = events.pop(0)
-            clock = max(clock, due) + 0.3
-            h = pieces[p][1]
-            if step == "near":
-                after_near(p)
-                expect("x" if h == 0 else "y", 4, p, "far")
-            elif step == "far":
-                after_far(p)
-                expect("z", 4, p, "z")
-            else:
-                after_z(p)
-        else:
-            time_, run, done = work.pop(0)
-            run()
-            clock += time_
-            if done is not None:
-                for h in range(2):
-                    expect("y" if h == 0 else "x", 8, 2 * done + h, "near")
+
+    def after(name):
+        stage, p = name
+        if stage == "grad":
+            return [first_send(2 * p + h) for h in range(2)]
+        (w, h), part = pieces[p], rows_of(p)
+        size = grads[w].size
+        route = SUMS[w][h]
+        if stage == "near":
+            link = "x" if route == "a" else "y"
+            return [(link, 4 * size, far_copy(p).start, lambda: after_far(p), ("far", p))]
+        if stage == "far":
+
+            def send():
+                for d in range(3):
+                    z_copy(p, d).start()
+
+            return [("z", 4 * size, send, lambda: after_z(p), ("z", p))]
+        if stage == "c0":
+
+            def receive_y():
+                then_near(p, 0).wait_recv()
+                for b in range(2):
+                    into = mine[w].at[y, b, t, part]
+                    into[...] = plus(into, from_z[w].at[b, part]).astype(jnp.bfloat16)
+
+            return [("y", 2 * size, then_near(p, 0).start, receive_y, ("c1", p))]
+        if stage == "c1":
+
+            def receive_x():
+                then_near(p, 1).wait_recv()
+                grads[w][part] = plus(mine[w].at[y, x, t, part], from_z[w].at[2, part])
+
+            return [("x", size, then_near(p, 1).start, receive_x, ("c2", p))]
+        return []
+
+    def first_send(p):
+        (w, h), part = pieces[p], rows_of(p)
+        size = grads[w].size
+        if SUMS[w][h] == "c":
+
+            def send():
+                for d in range(3):
+                    for a in range(2):
+                        far_first(p, d, a, (t + d + 1) % 4).start()
+
+            def receive():
+                for d in range(3):
+                    for a in range(2):
+                        far_first(p, d, a, (t + d + 1) % 4).wait_recv()
+                for i in range(4):
+                    into = mine[w].at[i // 2, i % 2, t, part]
+                    into[...] = plus(
+                        into,
+                        from_near[w].at[0, i, part],
+                        from_near[w].at[1, i, part],
+                        from_far[w].at[i, part],
+                    ).astype(jnp.bfloat16)
+
+            return ("z", 16 * size, send, receive, ("c0", p))
+        link = "y" if SUMS[w][h] == "a" else "x"
+        return (link, 8 * size, near_copy(p).start, lambda: after_near(p), ("near", p))
+
+    arrange(
+        [(took, run, set(), None if done is None else ("grad", done)) for took, run, done in work],
+        [],
+        after,
+    )
     for kind in range(2):
         for i in range(2, 4):
             core_copy(used[kind], i).wait_send()
     for p in range(len(pieces)):
-        near_copy(p).wait_send()
-        far_copy(p).wait_send()
-        for d in range(3):
-            z_copy(p, d).wait_send()
+        if SUMS[pieces[p][0]][pieces[p][1]] == "c":
+            for d in range(3):
+                for a in range(2):
+                    far_first(p, d, a, (t + d + 1) % 4).wait_send()
+            then_near(p, 0).wait_send()
+            then_near(p, 1).wait_send()
+        else:
+            near_copy(p).wait_send()
+            far_copy(p).wait_send()
+            for d in range(3):
+                z_copy(p, d).wait_send()
     for d in range(3):
         state_copy(d, t).wait_send()
     wait("out")
@@ -1257,6 +1409,8 @@
             dma((pieces, 3)),
             dma((3,)),
             dma((3,)),
+            dma((8,)),
+            dma((8,)),
         ],
         compiler_params=pltpu.CompilerParams(
             collective_id=1, has_side_effects=True, vmem_limit_bytes=VMEM_BYTES
@@ -1265,8 +1419,8 @@
         *kept,
         a_turned,
         *[saved[name] for name in BWD_ANY],
-        saved["states"],
-        saved["rates8"],
+        saved["st"],
+        saved["r8"],
         cos,
         sin,
         tokens,
@@ -1274,6 +1428,46 @@
         lengths,
     )
     return outs[:N_W], outs[N_W]
+
+
+def hand_out_kernel(turned, *refs):
+    count = (len(refs) - 2 - len(turned)) // 3
+    ins, outs, bufs = (refs[i * count : (i + 1) * count] for i in range(3))
+    flipped, (load_sem, store_sem) = refs[3 * count : -2], refs[-2:]
+    loads = [pltpu.make_async_copy(ins[i], bufs[i], load_sem.at[i]) for i in range(count)]
+    order = [*turned, *(i for i in range(count) if i not in turned)]
+    stores = []
+    for i in order:
+        loads[i].start()
+    for i in order:
+        loads[i].wait()
+        source = bufs[i]
+        if i in turned:
+            source = flipped[turned.index(i)]
+            source[...] = bufs[i][...].T
+        stores.append(pltpu.make_async_copy(source, outs[i], store_sem.at[i]))
+        stores[-1].start()
+    for store in stores:
+        store.wait()
+
+
+def hand_out(arrays, turned):
+    anywhere = pl.BlockSpec(memory_space=pl.ANY)
+    shapes = [a.shape[::-1] if i in turned else a.shape for i, a in enumerate(arrays)]
+    outs = pl.pallas_call(
+        functools.partial(hand_out_kernel, turned),
+        name="hand_out",
+        out_shape=[jax.ShapeDtypeStruct(s, a.dtype) for s, a in zip(shapes, arrays)],
+        in_specs=[anywhere] * len(arrays),
+        out_specs=[anywhere] * len(arrays),
+        scratch_shapes=[
+            *[pltpu.VMEM(a.shape, a.dtype) for a in arrays],
+            *[pltpu.VMEM(shapes[i], arrays[i].dtype) for i in turned],
+            pltpu.SemaphoreType.DMA((len(arrays),)),
+            pltpu.SemaphoreType.DMA((len(arrays),)),
+        ],
+    )(*arrays)
+    return [out.T if i in turned else out for i, out in enumerate(outs)]
 
 
 def body_by_kernels(
@@ -1302,10 +1496,10 @@
     cos_half, sin_half = jnp.cos(turned), jnp.sin(turned)
     cos = jnp.concatenate([cos_half, cos_half], axis=1)
     sin = jnp.concatenate([-sin_half, sin_half], axis=1)
-    shards = (w_query, w_key, w_value, w_update, w_output, w_gate, w_up, w_down)
+    shards = (w_query, w_key, w_value, w_update, w_output, w_gate.T, w_up.T, w_down)
     kept, a_turned, saved = forward(shards, tokens, cos, sin, lengths, rates)
     grads, d_tokens = backward(kept, a_turned, saved, cos, sin, tokens, out_grad, lengths)
-    return (saved["result"], d_tokens, *grads)
+    return tuple(hand_out([saved["res"], d_tokens, *grads], (7, 8)))
 
 
 def body(

time: 384 us -> 345 us (0.90)
  Pallas kernels: 364 us -> 339 us
  local copies, waits for them, and re-layouts: 15 us -> 0 us
    pallas_call x1, Pallas kernels: 173 us -> 153 us  [forward(): pl.pallas_call(forward_kernel, name='gather_and_forward', out_shape=[jax....]
    unnamed x26 -> x0, local copies, waits for them, and re-layouts: 15 us -> none
    pallas_call x1, Pallas kernels: 191 us -> 181 us  [backward(): pl.pallas_call(backward_kernel, name='backward_and_scatter', out_shape=[j...]
    pallas_call x0 -> x1, Pallas kernels: none -> 3.98 us  [hand_out(): pl.pallas_call(functools.partial(hand_out_kernel, turned), name='hand_out...]
where the time goes in v5:
time: 345 us; the launch traced here: 343 us
  Pallas kernels  339 us (98%)
  other arithmetic  3.67 us (1%)
    pallas_call x1, Pallas kernels, backward(): pl.pallas_call(backward_kernel, name='backward_and_scatter', out_shape=[j...  181 us
    pallas_call x1, Pallas kernels, forward(): pl.pallas_call(forward_kernel, name='gather_and_forward', out_shape=[jax....  153 us

profile of v5, /device:TPU:0, one launch (start us, length us, event | category | flops | bytes accessed | tf_op | source)
XLA Modules:
  0.0 343.3 jit_solution(9035758698334368756)
XLA Ops:
  0.6 0.8 reduce-window.8
  1.5 0.7 bitcast_subtract_fusion
  2.2 0.1 convert_reduce_fusion
  2.2 0.1 select_reduce_fusion
  2.3 1.0 fusion
  3.3 1.0 pad_maximum_fusion
  4.3 153.4 %gather_and_forward.1 = (bf16[2,2,2,4,128,256]{5,4,3,2,1,0:T(8,128)(2,1)}, bf16[2,2,2,4,128,256]{5,4,3,2,1,0:T(8,128)(2,1)}, bf16[2,2,2,4,128,256]{5,4,3,2,1,0:T...) custom-call(bf16[128,256]{1,0:T(8,128)(2,1)} %refs_0_.1, ...), custom_call_target="tpu_custom_call" | custom-call | tf_op jit(solution)/shard_map/gather_and_forward/pallas_call | solution.py:673
  157.7 181.4 %backward_and_scatter.1 = (f32[128,256]{1,0:T(8,128)}, f32[128,256]{1,0:T(8,128)}, f32[128,256]{1,0:T(8,128)}, f32[128,256]{1,0:T(8,128)}, f32[256,128]{1,0:T(8,...) custom-call(bf16[2,2,2,4,128,256]{5,4,3,2,1,0:T(8,128)(2,1)} %get-tuple-element.55.ref, ...), custom_call_target="tpu_custom_call" | custom-call | tf_op jit(solution)/shard_map/backward_and_scatter/pallas_call | solution.py:1371
  339.1 4.0 %hand_out.1 = (bf16[512,1024]{1,0:T(8,128)(2,1)}, f32[512,1024]{1,0:T(8,128)}, f32[128,256]{1,0:T(8,128)}, f32[128,256]{1,0:T(8,128)}, f32[128,256]{1,0:T(8,128)...) custom-call(bf16[512,1024]{1,0:T(8,128)(2,1)} %get-tuple-element.54., ...), custom_call_target="tpu_custom_call" | custom-call | tf_op jit(solution)/shard_map/hand_out/pallas_call | solution.py:1457
  (3 shorter events, 0.0 us)

commit v6 on v5

--- a/solution.py
+++ b/solution.py
@@ -166,6 +166,7 @@
 
 ORDER = (1, 2, 0, 3, 4, 5, 6, 7)
 ROUTES = ("ab", "ab", "ab", "ab", "ab", "cdab", "abab", "abab")
+STATE_BYTES = 8 * HEAD_DIM * HEAD_DIM * 2
 SLACK = 10.0
 RATE = 42_000.0
 
@@ -177,7 +178,8 @@
     def offer(name):
         known.add(name)
         for item in after(name):
-            waiting.setdefault(item[0], []).append(item)
+            items = waiting.setdefault(item[0], [])
+            items.insert(0 if name[0] == "st" else len(items), item)
 
     def pump():
         nonlocal count
@@ -430,9 +432,11 @@
         for d in range(3):
             state_copy(d, t).start()
 
-    def sum_states():
+    def receive_states():
         for d in range(3):
             state_copy(d, (t + 3 - d) % 4).wait_recv()
+
+    def sum_states():
         before = scalar_segment(first - 1, ends)
 
         def head(h, carry):
@@ -583,6 +587,8 @@
 
             return ("c", blocks * size // 4, send, lambda: None, ("c", p, k))
 
+        if stage == "st":
+            return [("z", 4 * STATE_BYTES, send_states, receive_states, ("sr", 0, 0))]
         if stage == "go":
             own_copy(p).start()
             return [over_z() if early else over_near(0)]
@@ -599,20 +605,20 @@
     needs = set()
     steps = []
 
-    def then(took, step, *weights):
+    def then(took, step, *weights, done=None):
         for p in range(total):
             if pieces[p][0] in weights:
                 needs.update(("c", p, k) for k in core_parts(p))
-        steps.append((took, step, set(needs), None))
+        steps.append((took, step, set(needs), done))
 
     then(2.0, begin)
     then(0.2, rates_here)
     then(2.2, project(1, finish_key), 1)
     then(2.2, project(2, finish_value), 2)
-    then(1.5, make_states)
+    then(1.5, make_states, done=("st", 0, 0))
     then(2.2, project(0, finish_query), 0)
-    then(0.2, send_states)
     then(2.2, project(3, finish_update), 3)
+    needs.add(("sr", 0, 0))
     then(0.5, sum_states)
     for i in range(4):
         then(1.8, attend_pairs(i, i + 1))
@@ -1130,10 +1136,12 @@
         for d in range(3):
             state_copy(d, t).start()
 
+    def receive_states():
+        for d in range(3):
+            state_copy(d, (t + 3 - d) % 4).wait_recv()
+
     def sum_states():
         wait("v", "k", "qp", "kp")
-        for d in range(3):
-            state_copy(d, (t + 3 - d) % 4).wait_recv()
 
         def head(h, carry):
             rate = rate_of(h)[:, :HEAD_DIM]
@@ -1241,11 +1249,10 @@
         (3.0, middle_back, None),
         (1.0, grad(4, False), None),
         (6.0, mixed_back, None),
+        (2.0, make_states, -1),
         (1.0, grad(3, False), None),
         (1.2, grad(4, True), 4),
-        (2.0, make_states, None),
         (1.2, grad(3, True), 3),
-        (0.1, send_states, None),
         (2.0, through(3, sources[3], rows_a, True), None),
         (1.0, sum_states, None),
         (4.0, attend_pairs(0, 1), None),
@@ -1268,6 +1275,10 @@
 
     def after(name):
         stage, p = name
+        if stage == "st":
+            return [("z", 4 * STATE_BYTES, send_states, receive_states, ("sr", 0))]
+        if stage == "sr":
+            return []
         if stage == "grad":
             return [first_send(2 * p + h) for h in range(2)]
         (w, h), part = pieces[p], rows_of(p)
@@ -1329,7 +1340,15 @@
         return (link, 8 * size, near_copy(p).start, lambda: after_near(p), ("near", p))
 
     arrange(
-        [(took, run, set(), None if done is None else ("grad", done)) for took, run, done in work],
+        [
+            (
+                took,
+                run,
+                {("sr", 0)} if run is sum_states else set(),
+                ("st", 0) if done == -1 else None if done is None else ("grad", done),
+            )
+            for took, run, done in work
+        ],
         [],
         after,
     )

time: 345 us -> 334 us (0.968)
  Pallas kernels: 339 us -> 329 us
    pallas_call x1, Pallas kernels: 181 us -> 173 us  [backward(): pl.pallas_call(backward_kernel, name='backward_and_scatter', out_shape=[j...]
where the time goes in v6:
time: 334 us
  Pallas kernels  329 us (99%)
  other arithmetic  3.67 us (1%)
    pallas_call x1, Pallas kernels, backward(): pl.pallas_call(backward_kernel, name='backward_and_scatter', out_shape=[j...  173 us
    pallas_call x1, Pallas kernels, forward(): pl.pallas_call(forward_kernel, name='gather_and_forward', out_shape=[jax....  152 us

profile of v6, /device:TPU:0, one launch (start us, length us, event | category | flops | bytes accessed | tf_op | source)
XLA Modules:
  0.0 333.6 jit_solution(13489369494346919889)
XLA Ops:
  0.6 0.8 reduce-window.8
  1.5 0.7 bitcast_subtract_fusion
  2.2 0.1 convert_reduce_fusion
  2.2 0.1 select_reduce_fusion
  2.3 1.0 fusion
  3.3 1.0 pad_maximum_fusion
  4.3 152.4 %gather_and_forward.1 = (bf16[2,2,2,4,128,256]{5,4,3,2,1,0:T(8,128)(2,1)}, bf16[2,2,2,4,128,256]{5,4,3,2,1,0:T(8,128)(2,1)}, bf16[2,2,2,4,128,256]{5,4,3,2,1,0:T...) custom-call(bf16[128,256]{1,0:T(8,128)(2,1)} %refs_0_.1, ...), custom_call_target="tpu_custom_call" | custom-call | tf_op jit(solution)/shard_map/gather_and_forward/pallas_call | solution.py:679
  156.8 172.6 %backward_and_scatter.1 = (f32[128,256]{1,0:T(8,128)}, f32[128,256]{1,0:T(8,128)}, f32[128,256]{1,0:T(8,128)}, f32[128,256]{1,0:T(8,128)}, f32[256,128]{1,0:T(8,...) custom-call(bf16[2,2,2,4,128,256]{5,4,3,2,1,0:T(8,128)(2,1)} %get-tuple-element.55.ref, ...), custom_call_target="tpu_custom_call" | custom-call | tf_op jit(solution)/shard_map/backward_and_scatter/pallas_call | solution.py:1390
  329.4 4.0 %hand_out.1 = (bf16[512,1024]{1,0:T(8,128)(2,1)}, f32[512,1024]{1,0:T(8,128)}, f32[128,256]{1,0:T(8,128)}, f32[128,256]{1,0:T(8,128)}, f32[128,256]{1,0:T(8,128)...) custom-call(bf16[512,1024]{1,0:T(8,128)(2,1)} %get-tuple-element.54., ...), custom_call_target="tpu_custom_call" | custom-call | tf_op jit(solution)/shard_map/hand_out/pallas_call | solution.py:1476
  (3 shorter events, 0.0 us)
